TPU v7x, 256 devices: a whole 4x4x8 slice. The times are simulated.
256 devices in a mesh: depth: 16 (over x, z_lo), col: 16 (over z_hi, y, core).
Axes of the slice: x: 4, y: 4, z: 8 (z_hi: 2, z_lo: 4; z = z_hi * 4 + z_lo), core: 2. Of those that a mesh axis runs over, the one named last changes fastest.
Arguments:
- recorded: bfloat16 [4, 32, 2, 512, 512], P(None, 'depth', None, 'col'), may hold values from -6 to 6
- vertical: float32 [4, 512], replicated, may hold values from 0.05 to 0.8
Outputs:
- prediction: float32 [4, 2, 512, 512], P(None, None, 'col', 'depth')
All inputs are finite; a program needn't handle non-finite values.
Results may differ from a plain program's by a relative error of at most 0.01.
Values may be sent and summed in bfloat16 or wider, within the bound.
No kernel may reach another device: no remote copies, remote signals or barrier semaphores. Data moves between devices by JAX's collectives and lax.ppermute only.
A program may use at most 64 MiB of HBM per device.

v0:
```python
import jax
import jax.numpy as jnp
from jax import lax
from jax.sharding import PartitionSpec as P


def prefix(x, axis, combine, identity, reverse):
    peers, mine = (lax.axis_size(axis), lax.axis_index(axis))
    everything = lax.all_gather(x, axis)
    start = jnp.broadcast_to(jnp.asarray(identity, x.dtype), x.shape)

    def lap(k, before):
        at = peers - 1 - k if reverse else k
        reached = at > mine if reverse else at < mine
        new = combine(before, everything[at])
        return jnp.where(reached, new, before)

    return lax.fori_loop(0, peers, lap, start)


def from_behind(value, axis, steps):
    count = lax.axis_size(axis)
    initial, last = (max(0, -steps), min(count, count - steps))
    return lax.ppermute(value, axis, [(source, source + steps) for source in range(initial, last)])


def complex_product(left_side, right_side, pattern, stack_axis):
    left_real = left_side[:, :, 0]
    left_imag = left_side[:, :, 1]
    right_real = right_side[:, :, 0]
    right_imag = right_side[:, :, 1]
    real_part = jnp.einsum(
        pattern, left_real, right_real, preferred_element_type=jnp.float32
    ) - jnp.einsum(pattern, left_imag, right_imag, preferred_element_type=jnp.float32)
    imag_part = jnp.einsum(
        pattern, left_real, right_imag, preferred_element_type=jnp.float32
    ) + jnp.einsum(pattern, left_imag, right_real, preferred_element_type=jnp.float32)
    return jnp.stack([real_part, imag_part], axis=stack_axis)


def add_pair(earlier, later):
    return earlier + later


def carry_products(products):
    running = lax.cumsum(products, axis=1)
    before = prefix(running[:, -1], "depth", add_pair, jnp.zeros_like(running[:, -1]), False)
    prefix_all = running + before[:, None]
    previous = from_behind(prefix_all[:, -1], "depth", 1)
    return jnp.concatenate([previous[:, None], prefix_all[:, :-1]], axis=1).astype(jnp.bfloat16)


def shards(recorded, vertical):
    local_depths = recorded.shape[1]
    row_count = recorded.shape[3]
    depth_cells = lax.axis_size("depth") * local_depths
    depth_step = 1.0 / depth_cells
    first_row = lax.axis_index("col") * row_count
    row_wave = lax.dynamic_slice_in_dim(vertical, first_row, row_count, 1)
    depth_f = (
        lax.axis_index("depth") * local_depths + jnp.arange(local_depths, dtype=jnp.int32)
    ).astype(jnp.float32)
    phase_angle = (row_wave[:, None, :, None] + vertical[:, None, None, :]) * depth_f[
        None, :, None, None
    ]
    cosine = jnp.cos(phase_angle)
    sine_part = jnp.sin(phase_angle)
    real_in = recorded[:, :, 0].astype(jnp.float32)
    imag_in = recorded[:, :, 1].astype(jnp.float32)
    plus32 = (
        jnp.stack(
            [real_in * cosine - imag_in * sine_part, real_in * sine_part + imag_in * cosine], axis=2
        )
        * depth_step
    )
    minus_phase = (
        jnp.stack(
            [real_in * cosine + imag_in * sine_part, imag_in * cosine - real_in * sine_part], axis=2
        )
        * depth_step
    ).astype(jnp.bfloat16)
    plus_phase = plus32.astype(jnp.bfloat16)
    inner_sum = lax.cumsum(plus32, axis=1, reverse=True)
    beyond = prefix(inner_sum[:, 0], "depth", add_pair, jnp.zeros_like(inner_sum[:, 0]), True)
    suffix_all = inner_sum + beyond[:, None]
    following = from_behind(suffix_all[:, 0], "depth", -1)
    tail_sum = jnp.concatenate([suffix_all[:, 1:], following[:, None]], axis=1).astype(jnp.bfloat16)
    columns = minus_phase
    products = complex_product(
        columns, lax.all_gather(tail_sum, "col", axis=3, tiled=True), "wzrk,wzkc->wzrc", 2
    )
    lagged = carry_products(products)
    columns = plus_phase
    partial_pred = complex_product(
        columns, lax.all_gather(lagged, "col", axis=3, tiled=True), "wzrk,wzkc->wrc", 1
    )
    return lax.psum_scatter(partial_pred, "depth", scatter_dimension=3, tiled=True)


def solution(mesh):
    in_specs = (P(None, "depth", None, "col", None), P())
    out_specs = P(None, None, "col", "depth")
    return jax.shard_map(shards, mesh=mesh, in_specs=in_specs, out_specs=out_specs, check_vma=False)
```

profile of v0, /device:TPU:8, one launch (start us, length us, event | category | flops | bytes accessed | tf_op | source)
XLA Modules:
  0.0 773.7 jit_solution(15379393343514793894)
XLA Ops:
  9.2 3.1 fusion.51
  13.7 190.7 %all-gather.11.cloned.1.call-done = f32[64,1,2,32,512]{4,3,0,2,1:T(8,128)} async-done(((f32[4,1,2,32,512]{4,3,0,2,1:T(8,128)}), f32[64,1,2,32,512]{4,3,0,2,1:T(8,128)}) %all-gather.11.cloned.1.call-update) | async-done | bytes 8388624 | tf_op jit(solution)/shard_map/all_gather | solution.py:9
  204.4 20.2 %while.30 = (s32[]{:T(128)}, f32[4,2,32,512]{3,2,1,0:T(8,128)S(1)}, s32[]{:T(128)}, f32[16,4,2,32,512]{4,3,1,0,2:T(8,128)}, s32[]{:T(128)}, /*index=5*/s32[]{:T(128)}, s32[]{:T(128)}, s32[]{:T(128)}) while((s32[]{:T(128)}, f32[4,2,32,512]{3,2,1,0:T(8,128)S(1)}, s32[]{:T(128)}, f32[16,4,2,32,512]{4,3,1,0,2:T(8,128)}, s32[]{:T(128)}, ...), condition=%wide.region_2.3_spmd.clone, body=%wide.region_1.2_spmd.clone.sunk | while | flops 393224 | bytes 1573027 | solution.py:18
  205.6 1.2 add_select_fusion.4
  206.9 1.2 add_select_fusion.4
  208.2 1.2 add_select_fusion.4
  209.4 1.2 add_select_fusion.4
  210.7 1.2 add_select_fusion.4
  212.0 1.2 add_select_fusion.4
  213.2 1.2 add_select_fusion.4
  214.5 1.2 add_select_fusion.4
  215.8 1.2 add_select_fusion.4
  217.0 1.2 add_select_fusion.4
  218.3 1.2 add_select_fusion.4
  219.6 1.2 add_select_fusion.4
  220.8 1.2 add_select_fusion.4
  222.1 1.2 add_select_fusion.4
  223.3 1.2 add_select_fusion.4
  224.8 1.3 collective-permute-start
  226.1 8.4 %collective-permute-done = bf16[4,2,32,512]{3,2,0,1:T(8,128)(2,1)S(1)} collective-permute-done((bf16[4,2,32,512]{3,2,0,1:T(8,128)(2,1)S(1)}, bf16[4,2,32,512]{3,2,0,1:T(8,128)(2,1)S(1)}, u32[]{:S(2)}, u32[]{:S(2)}) %collective-permute-start) | collective-permute-done | bytes 262176 | tf_op jit(solution)/shard_map/ppermute | solution.py:24
  236.7 106.7 %all-gather.7.cloned.1.call-done = bf16[4,2,2,512,512]{4,3,1,0,2:T(8,128)(2,1)} async-done(((bf16[4,2,2,32,512]{4,3,1,0,2:T(8,128)(2,1)}), bf16[4,2,2,512,512]{4,3,1,0,2:T(8,128)(2,1)}) %all-gather.7.cloned.1.call-update) | async-done | bytes 8388624 | tf_op jit(solution)/shard_map/all_gather | solution.py:90
  343.4 3.1 fusion
  346.5 3.5 fusion.1
  353.0 183.7 %all-gather.13.cloned.1.call-done = f32[64,1,2,32,512]{4,3,1,0,2:T(8,128)} async-done(((f32[4,1,2,32,512]{4,3,1,0,2:T(8,128)}), f32[64,1,2,32,512]{4,3,1,0,2:T(8,128)}) %all-gather.13.cloned.1.call-update) | async-done | bytes 8388624 | tf_op jit(solution)/shard_map/all_gather | solution.py:9
  536.6 20.1 %while.31 = (s32[]{:T(128)}, f32[4,2,32,512]{3,2,1,0:T(8,128)S(1)}, s32[]{:T(128)}, f32[16,4,2,32,512]{4,3,1,0,2:T(8,128)}, s32[]{:T(128)}, /*index=5*/s32[]{:T(128)}) while((s32[]{:T(128)}, f32[4,2,32,512]{3,2,1,0:T(8,128)S(1)}, s32[]{:T(128)}, f32[16,4,2,32,512]{4,3,1,0,2:T(8,128)}, s32[]{:T(128)}, /*index=5*/s32[]{:T(128)}) %tuple.96), condition=%wide.region_5.6_spmd.clone, body=%wide.region_4.5_spmd.clone.sunk | while | flops 393220 | bytes 1572965 | solution.py:18
  537.9 1.2 add_select_fusion.5
  557.0 1.3 collective-permute-start.1
  558.3 5.6 collective-permute-done.1
  565.0 109.7 %all-gather.9.cloned.1.call-done = bf16[4,2,2,512,512]{4,3,1,0,2:T(8,128)(2,1)} async-done(((bf16[4,2,2,32,512]{4,3,1,0,2:T(8,128)(2,1)}), bf16[4,2,2,512,512]{4,3,1,0,2:T(8,128)(2,1)}) %all-gather.9.cloned.1.call-update) | async-done | bytes 8388624 | tf_op jit(solution)/shard_map/all_gather | solution.py:95
  674.7 3.8 slice_bitcast_fusion
  682.9 2.0 reshape.30
  685.0 80.6 %reduce-scatter.4.cloned.1.call-done = f32[32,256]{1,0:T(8,128)} async-done(((f32[512,256]{1,0:T(8,128)}), f32[32,256]{1,0:T(8,128)}) %reduce-scatter.4.cloned.1.call-update) | async-done | bytes 32784
  (57 shorter events, 36.2 us)
Async XLA Ops:
  6.5 197.9 %all-gather.11.cloned.1.call-start = ((), (), s32[]{:S(2)}) async-start(), calls=%async_computation.3 | async-start | bytes 8912896 | tf_op jit(solution)/shard_map/all_gather | solution.py:9
  13.6 329.8 %all-gather.7.cloned.1.call-start = ((), (), s32[]{:S(2)}) async-start(), calls=%async_computation.1 | async-start | bytes 8912896 | tf_op jit(solution)/shard_map/all_gather | solution.py:90
  224.8 9.7 %collective-permute-start = (bf16[4,2,32,512]{3,2,0,1:T(8,128)(2,1)S(1)}, bf16[4,2,32,512]{3,2,0,1:T(8,128)(2,1)S(1)}, u32[]{:S(2)}, u32[]{:S(2)}) collective-permute-start(bf16[4,2,32,512]{3,2,0,1:T(8,128)(2,1)S(1)} %get-tuple-element.269), channel_id=1, source_target_pairs={{16,0},{32,16},{48,32},{64,48},{80,64},{96,80},{112,96},{128,112},... | collective-permute-start | bytes 786440 | tf_op jit(solution)/shard_map/ppermute | solution.py:24
  235.4 301.2 %all-gather.13.cloned.1.call-start = ((), (), s32[]{:S(2)}) async-start(), calls=%async_computation.4 | async-start | bytes 8912896 | tf_op jit(solution)/shard_map/all_gather | solution.py:9
  343.4 6.6 copy-start
  352.9 321.8 %all-gather.9.cloned.1.call-start = ((), (), s32[]{:S(2)}) async-start(), calls=%async_computation.2 | async-start | bytes 8912896 | tf_op jit(solution)/shard_map/all_gather | solution.py:95
  557.0 6.9 collective-permute-start.1
  564.8 200.7 %reduce-scatter.4.cloned.1.call-start = ((), (), s32[]{:S(2)}) async-start(), calls=%async_computation.5 | async-start | bytes 557056
Sparse Core Ops, SparseCore 0:
  13.7 190.6 all-gather.10
  235.6 107.7 all-gather.6
  353.0 183.5 all-gather.12
  564.9 109.7 all-gather.8
  685.1 80.4 reduce-scatter.3
where the time goes:
time: 776 us; the launch traced here: 774 us
  waiting for transfers between devices  685 us (88%)
  other arithmetic  47.8 us (6%)
  between operations  13.3 us (2%)
  local copies, waits for them, and re-layouts  12.3 us (2%)
  matrix products  11.2 us (1%)
    all_gather x2, waiting for transfers between devices, prefix(): everything = lax.all_gather(x, axis)  374 us
    all_gather x1, waiting for transfers between devices, shards(): lax.all_gather(lagged, 'col', axis=3, tiled=True)  110 us
    all_gather x1, waiting for transfers between devices, shards(): lax.all_gather(tail_sum, 'col', axis=3, tiled=True)  107 us
    unnamed x6, waiting for transfers between devices  80.7 us
    select_n x32, other arithmetic, lap(): return jnp.where(reached, new, before)  39.5 us
  transfers between devices with their start and end apart: 7, of which 7 were waited for; matrix products, arithmetic and copies ran while one was open for 0% of the time, Pallas kernels for 0%

commit v1 on v0

v1 whole, which is shorter than its diff:
```python
import jax
import jax.numpy as jnp
from jax import lax
from jax.experimental import pallas as pl
from jax.experimental.pallas import tpu as pltpu
from jax.sharding import Mesh, PartitionSpec as P

NAMES = ("x", "zl", "zh", "y", "core")
SIZES = (4, 4, 2, 4, 2)
NZ = 32
BF16, F32 = jnp.bfloat16, jnp.float32


def scan_kernel(rec_ref, vert_ref, out_ref):
    w = lax.axis_index("zl")
    first_col = lax.axis_index("x") * 128
    first_row = (
        lax.axis_index("zh") * 8 + lax.axis_index("y") * 2 + lax.axis_index("core")
    ) * 32

    def of_frequency(rows):
        picked = lax.broadcasted_iota(jnp.int32, rows.shape, 0) == w
        return jnp.sum(jnp.where(picked, rows, 0.0), axis=0, keepdims=True)

    waves = of_frequency(vert_ref[...])
    row = lax.broadcasted_iota(jnp.int32, (32, 512), 0)
    lane = lax.broadcasted_iota(jnp.int32, (32, 512), 1)
    mine = lane == row + first_row
    row_wave = jnp.sum(jnp.where(mine, waves, 0.0), axis=1, keepdims=True)
    col_wave = of_frequency(vert_ref[:, pl.ds(pl.multiple_of(first_col, 128), 128)])
    angle = row_wave + col_wave
    step_re, step_im = jnp.cos(angle), jnp.sin(angle)
    last = angle * float(NZ - 1)
    scale = 1.0 / NZ
    c, s = jnp.cos(last) * scale, jnp.sin(last) * scale
    tail_re = jnp.zeros((32, 128), F32)
    tail_im = jnp.zeros((32, 128), F32)
    for z in range(NZ - 1, -1, -1):
        re = rec_ref[z, 0].astype(F32)
        im = rec_ref[z, 1].astype(F32)
        rc, rs, ic, is_ = re * c, re * s, im * c, im * s
        out_ref[z, 0, 0] = tail_re.astype(BF16)
        out_ref[z, 0, 1] = tail_im.astype(BF16)
        out_ref[z, 1, 0] = (rc + is_).astype(BF16)
        out_ref[z, 1, 1] = (ic - rs).astype(BF16)
        tail_re = tail_re + (rc - is_)
        tail_im = tail_im + (rs + ic)
        c, s = c * step_re + s * step_im, s * step_re - c * step_im


def unit_kernel(mine_ref, other_ref, out_ref, t_ref, m_ref, sems):
    h = lax.axis_index("core")

    def fetch(t_from, m_from):
        copies = [
            pltpu.make_async_copy(t_from, t_ref, sems.at[0]),
            pltpu.make_async_copy(m_from, m_ref, sems.at[1]),
        ]
        for copy in copies:
            copy.start()
        for copy in copies:
            copy.wait()

    @pl.when(h == 0)
    def _():
        fetch(mine_ref, other_ref)

    @pl.when(h == 1)
    def _():
        fetch(other_ref, mine_ref)

    def whole(ref, part):
        return jnp.concatenate([ref[b, :, :, part].reshape(512, 128) for b in range(4)], axis=1)

    def rows(part):
        return jnp.concatenate(
            [t_ref[b, :, pl.ds(h, 1), part].reshape(256, 128) for b in range(4)], axis=1
        )

    def dot(a, b):
        return jnp.dot(a, b, preferred_element_type=F32)

    left = jnp.concatenate([rows(0), rows(1)], axis=0)
    by_re = dot(left, whole(m_ref, 0))
    by_im = dot(left, whole(m_ref, 1))
    mid_re = (by_re[:256] - by_im[256:]).astype(BF16)
    mid_im = (by_im[:256] + by_re[256:]).astype(BF16)
    mid = jnp.concatenate([mid_re, mid_im], axis=0)
    by_re = dot(mid, whole(t_ref, 0))
    by_im = dot(mid, whole(t_ref, 1))
    parts = (by_re[:256] - by_im[256:], by_im[:256] + by_re[256:])

    lane = lax.broadcasted_iota(jnp.int32, (8, 8, 128), 2)
    low, even = lane < 64, (lane // 32) % 2 == 0
    for x in range(4):
        packed = []
        for part in parts:
            cols = part[:, x * 128 : (x + 1) * 128].reshape(8, 4, 8, 128)
            g = [cols[:, k] for k in range(4)]
            for a, b in ((0, 2), (1, 3)):
                g[a], g[b] = (
                    jnp.where(low, g[a], pltpu.roll(g[b], 64, 2)),
                    jnp.where(low, pltpu.roll(g[a], 64, 2), g[b]),
                )
            for a, b in ((0, 1), (2, 3)):
                g[a], g[b] = (
                    jnp.where(even, g[a], pltpu.roll(g[b], 32, 2)),
                    jnp.where(even, pltpu.roll(g[a], 96, 2), g[b]),
                )
            packed.append(g)
        for zl in range(4):
            out_ref[x, zl] = jnp.concatenate([packed[0][zl], packed[1][zl]], axis=1).astype(BF16)


def sum_kernel(parts_ref, out_ref):
    for w in range(4):
        total = jnp.sum(parts_ref[0, w].astype(F32), axis=0)
        for x in range(1, 4):
            total = total + jnp.sum(parts_ref[x, w].astype(F32), axis=0)
        for part in range(2):
            for g in range(4):
                out_ref[w, part, g * 8 : (g + 1) * 8, :] = total[
                    part * 8 : (part + 1) * 8, g * 32 : (g + 1) * 32
                ]


def vmem(n):
    return [pl.BlockSpec(memory_space=pltpu.VMEM)] * n


def call(kernel, shape, dtype, in_specs, args, scratch=(), limit=16, flops=0, moved=0):
    return pl.pallas_call(
        kernel,
        out_shape=jax.ShapeDtypeStruct(shape, dtype),
        in_specs=in_specs,
        out_specs=pl.BlockSpec(memory_space=pltpu.VMEM),
        scratch_shapes=list(scratch),
        compiler_params=pltpu.CompilerParams(vmem_limit_bytes=limit << 20),
        cost_estimate=pl.CostEstimate(flops=flops, bytes_accessed=moved, transcendentals=0),
    )(*args)


def shards(recorded, vertical):
    blocks = recorded.reshape(4, 2, 2, 32, 4, 128).transpose(4, 0, 1, 2, 3, 5)
    sections = lax.all_to_all(
        blocks.reshape(16, 2, 2, 32, 128), ("x", "zl"), 0, 0, tiled=True
    )
    phased = call(
        scan_kernel,
        (NZ, 2, 2, 32, 128),
        BF16,
        vmem(2),
        (sections.reshape(NZ, 2, 32, 128), vertical),
        moved=3 << 19,
    )
    mine = lax.all_to_all(
        phased.reshape(64, 2, 32, 128), ("x", "zh", "y", "core"), 0, 0, tiled=True
    )
    mine = mine.reshape(4, 8, 2, 2, 32, 128)
    other = lax.ppermute(mine, "core", [(0, 1), (1, 0)])
    partial = call(
        unit_kernel,
        (4, 4, 8, 16, 128),
        BF16,
        [pl.BlockSpec(memory_space=pl.ANY)] * 2,
        (mine, other),
        scratch=[
            pltpu.VMEM((4, 8, 2, 2, 32, 128), BF16),
            pltpu.VMEM((4, 8, 2, 2, 32, 128), BF16),
            pltpu.SemaphoreType.DMA((2,)),
        ],
        limit=40,
        flops=1 << 30,
        moved=5 << 19,
    )
    parts = lax.all_to_all(
        partial.reshape(128, 16, 128), ("x", "zl", "zh", "y"), 0, 0, tiled=True
    )
    return call(
        sum_kernel,
        (4, 2, 32, 32),
        F32,
        vmem(1),
        (parts.reshape(4, 4, 8, 16, 128),),
        moved=1 << 19,
    )


def solution(mesh):
    chips = Mesh(mesh.devices.reshape(SIZES), NAMES)
    depth, col = ("x", "zl"), ("zh", "y", "core")
    return jax.shard_map(
        shards,
        mesh=chips,
        in_specs=(P(None, depth, None, col, None), P()),
        out_specs=P(None, None, col, depth),
        check_vma=False,
    )
```

time: 776 us -> 99.6 us (0.13)
  waiting for transfers between devices: 685 us -> 2.66 us
  blocking collectives: 0 us -> 91.5 us
  other arithmetic: 47.8 us -> 0 us
  between operations: 13.3 us -> 0.04 us
  matrix products: 11.2 us -> 0 us
  local copies, waits for them, and re-layouts: 12.3 us -> 1.28 us
    all_gather x4 -> x0, waiting for transfers between devices: 591 us -> none  [the longest x2 374 us: prefix(): everything = lax.all_gather(x, axis)]
    all_to_all x0 -> x3, blocking collectives: none -> 91.5 us  [the longest x1 36.4 us: shards(): lax.all_to_all(phased.reshape(64, 2, 32, 128), ('x', 'zh', 'y', 'core'),...]
    unnamed x6 -> x0, waiting for transfers between devices: 80.7 us -> none
    select_n x32 -> x0, other arithmetic: 39.5 us -> none  [lap(): return jnp.where(reached, new, before)]
    ppermute x2 -> x1, waiting for transfers between devices: 14 us -> 2.66 us  [shards(): other = lax.ppermute(mine, 'core', [(0, 1), (1, 0)])]
    dot_general x8 -> x0, matrix products: 11.2 us -> none  [the longest x2 4.32 us: complex_product(): jnp.einsum(pattern, left_real, right_real, preferred_element_type=jnp.flo...]
  transfers between devices with their start and end apart: 7 -> 1, of which waited for: 7 -> 1; matrix products, arithmetic and copies ran while one was open for 0% -> 0% of each run, Pallas kernels for 0% -> 0%
where the time goes in v1:
time: 99.6 us; the launch traced here: 98.6 us
  blocking collectives  91.5 us (92%)
  Pallas kernels  3.08 us (3%)
  waiting for transfers between devices  2.66 us (3%)
  local copies, waits for them, and re-layouts  1.28 us (1%)
    all_to_all x1, blocking collectives, shards(): lax.all_to_all(phased.reshape(64, 2, 32, 128), ('x', 'zh', 'y', 'core'),...  36.4 us
    all_to_all x1, blocking collectives, shards(): lax.all_to_all(partial.reshape(128, 16, 128), ('x', 'zl', 'zh', 'y'), 0,...  30.3 us
    all_to_all x1, blocking collectives, shards(): lax.all_to_all(blocks.reshape(16, 2, 2, 32, 128), ('x', 'zl'), 0, 0, tile...  24.8 us
    pallas_call x3, Pallas kernels, call(): pl.pallas_call(kernel, out_shape=jax.ShapeDtypeStruct(shape, dtype), in_s...  3.08 us
    ppermute x1, waiting for transfers between devices, shards(): other = lax.ppermute(mine, 'core', [(0, 1), (1, 0)])  2.66 us
  transfers between devices with their start and end apart: 1, of which 1 were waited for; matrix products, arithmetic and copies ran while one was open for 0% of the time, Pallas kernels for 0%

profile of v1, /device:TPU:8, one launch (start us, length us, event | category | flops | bytes accessed | tf_op | source)
XLA Modules:
  0.0 98.6 jit_solution(18354382458270771013)
XLA Ops:
  0.0 1.2 %reshape.21 = bf16[4,2,2,32,4,128]{5,4,3,2,1,0:T(4,128)(2,1)S(1)} reshape(bf16[4,2,2,32,512]{4,3,2,1,0:T(8,128)(2,1)} %param.2) | data formatting | bytes 1048576 | tf_op jit(solution)/shard_map/reshape | solution.py:144
  1.2 0.1 copy.3
  1.3 0.0 copy-start
  1.3 24.8 %all_to_all.15 = bf16[16,2,2,32,128]{4,3,2,1,0:T(8,128)(2,1)S(1)} all-to-all(bf16[16,2,2,32,128]{4,3,2,1,0:T(8,128)(2,1)S(1)} %bitcast.15), channel_id=1, replica_groups=mesh['x'=4,'zl'=4,'zh'=2,'y'=4,'core'=2] {'x','zl'}, dimensions={0} | all-to-all | bytes 1048576 | tf_op jit(solution)/shard_map/all_to_all | solution.py:145
  26.1 0.0 copy-done
  26.1 0.5 shard_map.28
  26.6 36.4 %all_to_all.16 = bf16[64,2,32,128]{3,2,1,0:T(8,128)(2,1)S(1)} all-to-all(bf16[64,2,32,128]{3,2,1,0:T(8,128)(2,1)S(1)} %bitcast.9), channel_id=1, replica_groups=mesh['x'=4,'zl'=4,'zh'=2,'y'=4,'core'=2] {'x','zh','y','core'}, dimensions={0} | all-to-all | bytes 2097152 | tf_op jit(solution)/shard_map/all_to_all | solution.py:156
  63.1 0.0 collective-permute-start
  63.1 2.7 %collective-permute-done.other_ref = bf16[4,8,2,2,32,128]{5,4,3,2,1,0:T(8,128)(2,1)S(1)} collective-permute-done((bf16[4,8,2,2,32,128]{5,4,3,2,1,0:T(8,128)(2,1)S(1)}, bf16[4,8,2,2,32,128]{5,4,3,2,1,0:T(8,128)(2,1)S(1)}, u32[]{:S(2)}, u32[]{:S(2)}) %collective-permute-start) | collective-permute-done | bytes 1048608 | tf_op jit(solution)/shard_map/ppermute | solution.py:160
  65.7 1.7 %shard_map.29 = bf16[4,4,8,16,128]{4,3,2,1,0:T(8,128)(2,1)S(1)} custom-call(bf16[4,8,2,2,32,128]{5,4,3,2,1,0:T(8,128)(2,1)S(1)} %bitcast.13, bf16[4,8,2,2,32,128]{5,4,3,2,1,0:T(8,128)(2,1)S(1)} %collective-permute-done.other_ref), custom_call_target="tpu_custom_call" | custom-call | flops 1073741824 | bytes 2621440 | tf_op jit(solution)/shard_map/pallas_call | solution.py:132
  67.5 30.3 %all_to_all.17 = bf16[128,16,128]{2,1,0:T(8,128)(2,1)S(1)} all-to-all(bf16[128,16,128]{2,1,0:T(8,128)(2,1)S(1)} %bitcast.14), channel_id=1, replica_groups=mesh['x'=4,'zl'=4,'zh'=2,'y'=4,'core'=2] {'x','zl','zh','y'}, dimensions={0} | all-to-all | bytes 1048576 | tf_op jit(solution)/shard_map/all_to_all | solution.py:176
  97.8 0.8 shard_map.30
Async XLA Ops:
  1.3 24.8 %copy-start = (f32[4,512]{1,0:T(4,128)S(1)}, f32[4,512]{1,0:T(4,128)}, u32[]{:S(2)}) copy-start(f32[4,512]{1,0:T(4,128)} %vert_ref.1) | copy-start | bytes 24580
  63.1 2.7 %collective-permute-start = (bf16[4,8,2,2,32,128]{5,4,3,2,1,0:T(8,128)(2,1)S(1)}, bf16[4,8,2,2,32,128]{5,4,3,2,1,0:T(8,128)(2,1)S(1)}, u32[]{:S(2)}, u32[]{:S(2)}) collective-permute-start(bf16[4,8,2,2,32,128]{5,4,3,2,1,0:T(8,128)(2,1)S(1)} %bitcast.12), channel_id=1, source_target_pairs={{0,1},{1,0},{2,3},{3,2},{4,5},{5,4},{6,7},{7,6},{8,9},{9,8},{10,11... | collective-permute-start | bytes 3145736 | tf_op jit(solution)/shard_map/ppermute | solution.py:160

commit v2 on v1

v2 whole, which is shorter than its diff:
```python
import jax
import jax.numpy as jnp
from jax import lax
from jax.experimental import pallas as pl
from jax.experimental.pallas import tpu as pltpu
from jax.sharding import Mesh, PartitionSpec as P

NAMES = ("x", "za", "zb", "zh", "y", "core")
SIZES = (4, 2, 2, 2, 4, 2)
NZ = 32
BF16, F32 = jnp.bfloat16, jnp.float32


def scan_kernel(rec_ref, vert_ref, out_ref):
    w = lax.axis_index("zh") * 2 + lax.axis_index("za")
    first_col = lax.axis_index("x") * 128
    first_row = (
        lax.axis_index("y") * 2 + lax.axis_index("core")
    ) * 32 + lax.axis_index("zb") * 16

    def of_frequency(rows):
        picked = lax.broadcasted_iota(jnp.int32, rows.shape, 0) == w
        return jnp.sum(jnp.where(picked, rows, 0.0), axis=0, keepdims=True)

    waves = of_frequency(vert_ref[...])
    row = lax.broadcasted_iota(jnp.int32, (32, 512), 0)
    lane = lax.broadcasted_iota(jnp.int32, (32, 512), 1)
    mine = lane == (row % 16) + (row // 16) * 256 + first_row
    row_wave = jnp.sum(jnp.where(mine, waves, 0.0), axis=1, keepdims=True)
    col_wave = of_frequency(vert_ref[:, pl.ds(pl.multiple_of(first_col, 128), 128)])
    angle = row_wave + col_wave
    step_re, step_im = jnp.cos(angle), jnp.sin(angle)
    last = angle * float(NZ - 1)
    scale = 1.0 / NZ
    c, s = jnp.cos(last) * scale, jnp.sin(last) * scale
    tail_re = jnp.zeros((32, 128), F32)
    tail_im = jnp.zeros((32, 128), F32)
    for z in range(NZ - 1, -1, -1):
        x, za, zb, j = z // 8, z // 4 % 2, z // 2 % 2, z % 2
        re, im = [rec_ref[x, :, za, zb, j, p].reshape(32, 128).astype(F32) for p in range(2)]
        rc, rs, ic, is_ = re * c, re * s, im * c, im * s
        values = ((tail_re, tail_im), (rc + is_, ic - rs))
        for kind in range(2):
            for part in range(2):
                out_ref[z, kind, part] = values[kind][part].astype(BF16).reshape(2, 16, 128)
        tail_re = tail_re + (rc - is_)
        tail_im = tail_im + (rs + ic)
        c, s = c * step_re + s * step_im, s * step_re - c * step_im


def unit_kernel(mine_ref, other_ref, out_ref, held_ref, sems):
    h = lax.axis_index("core")
    copies = [
        pltpu.make_async_copy(mine_ref, held_ref.at[h], sems.at[0]),
        pltpu.make_async_copy(other_ref, held_ref.at[1 - h], sems.at[1]),
    ]
    for copy in copies:
        copy.start()
    for copy in copies:
        copy.wait()

    def matrix(kind, part, cores):
        return jnp.concatenate(
            [
                jnp.concatenate(
                    [
                        held_ref[core, b, half, y, kind, part, zh]
                        for zh in range(2)
                        for y in range(4)
                        for core in cores
                        for half in range(2)
                    ],
                    axis=0,
                )
                for b in range(4)
            ],
            axis=1,
        )

    def whole(kind, part):
        return matrix(kind, part, (0, 1))

    def dot(a, b):
        return jnp.dot(a, b, preferred_element_type=F32)

    left = jnp.concatenate([matrix(0, 0, (h,)), matrix(0, 1, (h,))], axis=0)
    by_re = dot(left, whole(1, 0))
    by_im = dot(left, whole(1, 1))
    mid_re = (by_re[:256] - by_im[256:]).astype(BF16)
    mid_im = (by_im[:256] + by_re[256:]).astype(BF16)
    mid = jnp.concatenate([mid_re, mid_im], axis=0)
    by_re = dot(mid, whole(0, 0))
    by_im = dot(mid, whole(0, 1))
    parts = (by_re[:256] - by_im[256:], by_im[:256] + by_re[256:])

    lane = lax.broadcasted_iota(jnp.int32, (8, 8, 128), 2)
    low, even = lane < 64, (lane // 32) % 2 == 0
    for x in range(4):
        packed = []
        for part in parts:
            cols = part[:, x * 128 : (x + 1) * 128].reshape(8, 4, 8, 128)
            g = [cols[:, k] for k in range(4)]
            for a, b in ((0, 2), (1, 3)):
                g[a], g[b] = (
                    jnp.where(low, g[a], pltpu.roll(g[b], 64, 2)),
                    jnp.where(low, pltpu.roll(g[a], 64, 2), g[b]),
                )
            for a, b in ((0, 1), (2, 3)):
                g[a], g[b] = (
                    jnp.where(even, g[a], pltpu.roll(g[b], 32, 2)),
                    jnp.where(even, pltpu.roll(g[a], 96, 2), g[b]),
                )
            packed.append(g)
        for zl in range(4):
            both = jnp.concatenate([packed[0][zl], packed[1][zl]], axis=1).astype(BF16)
            for zh in range(2):
                out_ref[x, :, zl, zh] = both[zh * 4 : (zh + 1) * 4]


def sum_kernel(parts_ref, out_ref):
    for zl in range(4):
        for zh in range(2):
            total = jnp.sum(parts_ref[:, zl, zh].astype(F32), axis=0)
            out_ref[zh, zl] = total.astype(BF16)


def last_kernel(parts_ref, out_ref):
    for w in range(4):
        total = parts_ref[w, 0].astype(F32) + parts_ref[w, 1].astype(F32)
        for part in range(2):
            for g in range(4):
                out_ref[w, part, g * 8 : (g + 1) * 8, :] = total[
                    part * 8 : (part + 1) * 8, g * 32 : (g + 1) * 32
                ]


def vmem(n):
    return [pl.BlockSpec(memory_space=pltpu.VMEM)] * n


def call(kernel, shape, dtype, in_specs, args, scratch=(), limit=16, flops=0, moved=0):
    return pl.pallas_call(
        kernel,
        out_shape=jax.ShapeDtypeStruct(shape, dtype),
        in_specs=in_specs,
        out_specs=pl.BlockSpec(memory_space=pltpu.VMEM),
        scratch_shapes=list(scratch),
        compiler_params=pltpu.CompilerParams(vmem_limit_bytes=limit << 20),
        cost_estimate=pl.CostEstimate(flops=flops, bytes_accessed=moved, transcendentals=0),
    )(*args)


def exchange(x, axes):
    return lax.all_to_all(x, axes, 0, 0, tiled=True)


def shards(recorded, vertical):
    blocks = recorded.reshape(4, 2, 2, 2, 16, 4, 128).transpose(5, 0, 3, 1, 2, 4, 6)
    sections = exchange(blocks.reshape(32, 2, 2, 16, 128), ("x", "zh", "za", "zb"))
    phased = call(
        scan_kernel,
        (NZ, 2, 2, 2, 16, 128),
        BF16,
        vmem(2),
        (sections.reshape(4, 2, 2, 2, 2, 2, 16, 128), vertical),
        moved=3 << 19,
    )
    mine = exchange(phased, ("x", "zb", "y")).reshape(4, 2, 4, 2, 2, 2, 16, 128)
    other = lax.ppermute(mine, "core", [(0, 1), (1, 0)])
    partial = call(
        unit_kernel,
        (4, 4, 4, 2, 16, 128),
        BF16,
        [pl.BlockSpec(memory_space=pl.ANY)] * 2,
        (mine, other),
        scratch=[
            pltpu.VMEM((2, 4, 2, 4, 2, 2, 2, 16, 128), BF16),
            pltpu.SemaphoreType.DMA((2,)),
        ],
        limit=40,
        flops=1 << 30,
        moved=5 << 19,
    )
    parts = exchange(partial.reshape(16, 4, 2, 16, 128), ("x", "y"))
    summed = call(sum_kernel, (2, 4, 16, 128), BF16, vmem(1), (parts,), moved=1 << 19)
    last = exchange(summed.reshape(8, 16, 128), ("zh", "za", "zb"))
    return call(last_kernel, (4, 2, 32, 32), F32, vmem(1), (last.reshape(4, 2, 16, 128),))


def solution(mesh):
    chips = Mesh(mesh.devices.reshape(SIZES), NAMES)
    depth, col = ("x", "za", "zb"), ("zh", "y", "core")
    return jax.shard_map(
        shards,
        mesh=chips,
        in_specs=(P(None, depth, None, col, None), P()),
        out_specs=P(None, None, col, depth),
        check_vma=False,
    )
```

time: 99.6 us -> 84.8 us (0.85)
  blocking collectives: 91.5 us -> 77.4 us
    all_to_all x3 -> x4, blocking collectives: 91.5 us -> 77.4 us  [exchange(): return lax.all_to_all(x, axes, 0, 0, tiled=True)]
    pallas_call x3 -> x4, Pallas kernels: 3.08 us -> 3.12 us  [call(): pl.pallas_call(kernel, out_shape=jax.ShapeDtypeStruct(shape, dtype), in_s...]
where the time goes in v2:
time: 84.8 us; the launch traced here: 84.5 us
  blocking collectives  77.4 us (91%)
  Pallas kernels  3.12 us (4%)
  waiting for transfers between devices  2.66 us (3%)
  local copies, waits for them, and re-layouts  1.28 us (2%)
    all_to_all x4, blocking collectives, exchange(): return lax.all_to_all(x, axes, 0, 0, tiled=True)  77.4 us
    pallas_call x4, Pallas kernels, call(): pl.pallas_call(kernel, out_shape=jax.ShapeDtypeStruct(shape, dtype), in_s...  3.12 us
    ppermute x1, waiting for transfers between devices, shards(): other = lax.ppermute(mine, 'core', [(0, 1), (1, 0)])  2.66 us
  transfers between devices with their start and end apart: 1, of which 1 were waited for; matrix products, arithmetic and copies ran while one was open for 0% of the time, Pallas kernels for 0%

profile of v2, /device:TPU:8, one launch (start us, length us, event | category | flops | bytes accessed | tf_op | source)
XLA Modules:
  0.0 84.5 jit_solution(9920221648236249130)
XLA Ops:
  0.0 1.2 %reshape.21 = bf16[4,2,2,2,16,4,128]{6,5,4,3,2,1,0:T(4,128)(2,1)S(1)} reshape(bf16[4,2,2,32,512]{4,3,2,1,0:T(8,128)(2,1)} %param.2) | data formatting | bytes 1048576 | tf_op jit(solution)/shard_map/reshape | solution.py:158
  1.2 0.1 copy.3
  1.3 0.0 copy-start
  1.3 28.0 %all_to_all.20 = bf16[32,2,2,16,128]{4,3,2,1,0:T(8,128)(2,1)S(1)} all-to-all(bf16[32,2,2,16,128]{4,3,2,1,0:T(8,128)(2,1)S(1)} %bitcast.15), channel_id=1, replica_groups=mesh['x'=4,'za'=2,'zb'=2,'zh'=2,'y'=4,'core'=2] {'x','zh','za','zb'}, dimensions={0} | all-to-all | bytes 1048576 | tf_op jit(solution)/shard_map/all_to_all | solution.py:154
  29.3 0.0 copy-done
  29.3 0.6 shard_map.28
  29.8 22.4 %all_to_all.21 = bf16[32,2,2,2,16,128]{5,4,3,2,1,0:T(8,128)(2,1)S(1)} all-to-all(bf16[32,2,2,2,16,128]{5,4,3,2,1,0:T(8,128)(2,1)S(1)} %shard_map.28), channel_id=1, replica_groups=mesh['x'=4,'za'=2,'zb'=2,'zh'=2,'y'=4,'core'=2] {'x','zb','y'}, dimensions={0} | all-to-all | bytes 2097152 | tf_op jit(solution)/shard_map/all_to_all | solution.py:154
  52.2 0.0 collective-permute-start
  52.2 2.7 %collective-permute-done.other_ref = bf16[4,2,4,2,2,2,16,128]{7,6,5,4,3,2,1,0:T(8,128)(2,1)S(1)} collective-permute-done((bf16[4,2,4,2,2,2,16,128]{7,6,5,4,3,2,1,0:T(8,128)(2,1)S(1)}, bf16[4,2,4,2,2,2,16,128]{7,6,5,4,3,2,1,0:T(8,128)(2,1)S(1)}, u32[]{:S(2)}, u32[]{:S(2)}) %collective-permute-start) | collective-permute-done | bytes 1048608 | tf_op jit(solution)/shard_map/ppermute | solution.py:169
  54.9 1.7 %shard_map.29 = bf16[4,4,4,2,16,128]{5,4,3,2,1,0:T(8,128)(2,1)S(1)} custom-call(bf16[4,2,4,2,2,2,16,128]{7,6,5,4,3,2,1,0:T(8,128)(2,1)S(1)} %bitcast.11, bf16[4,2,4,2,2,2,16,128]{7,6,5,4,3,2,1,0:T(8,128)(2,1)S(1)} %collective-permute-done.other_ref), custom_call_target="tpu_custom_call" | custom-call | flops 1073741824 | bytes 2621440 | tf_op jit(solution)/shard_map/pallas_call | solution.py:142
  56.6 15.2 %all_to_all.22.parts_ref = bf16[16,4,2,16,128]{4,3,2,1,0:T(8,128)(2,1)S(1)} all-to-all(bf16[16,4,2,16,128]{4,3,2,1,0:T(8,128)(2,1)S(1)} %bitcast.12), channel_id=1, replica_groups=mesh['x'=4,'za'=2,'zb'=2,'zh'=2,'y'=4,'core'=2] {'x','y'}, dimensions={0} | all-to-all | bytes 1048576 | tf_op jit(solution)/shard_map/all_to_all | solution.py:154
  71.8 0.1 shard_map.30
  71.9 11.9 %all_to_all.23 = bf16[8,16,128]{2,1,0:T(8,128)(2,1)S(1)} all-to-all(bf16[8,16,128]{2,1,0:T(8,128)(2,1)S(1)} %bitcast.13), channel_id=1, replica_groups=mesh['x'=4,'za'=2,'zb'=2,'zh'=2,'y'=4,'core'=2] {'zh','za','zb'}, dimensions={0} | all-to-all | bytes 65536 | tf_op jit(solution)/shard_map/all_to_all | solution.py:154
  83.8 0.7 shard_map.31
Async XLA Ops:
  1.3 28.0 %copy-start = (f32[4,512]{1,0:T(4,128)S(1)}, f32[4,512]{1,0:T(4,128)}, u32[]{:S(2)}) copy-start(f32[4,512]{1,0:T(4,128)} %vert_ref.1) | copy-start | bytes 24580
  52.2 2.7 %collective-permute-start = (bf16[4,2,4,2,2,2,16,128]{7,6,5,4,3,2,1,0:T(8,128)(2,1)S(1)}, bf16[4,2,4,2,2,2,16,128]{7,6,5,4,3,2,1,0:T(8,128)(2,1)S(1)}, u32[]{:S(2)}, u32[]{:S(2)}) collective-permute-start(bf16[4,2,4,2,2,2,16,128]{7,6,5,4,3,2,1,0:T(8,128)(2,1)S(1)} %bitcast.10), channel_id=1, source_target_pairs={{0,1},{1,0},{2,3},{3,2},{4,5},{5,4},{6,7},{7,6},{8,9},{9,8},{10,11... | collective-permute-start | bytes 3145736 | tf_op jit(solution)/shard_map/ppermute | solution.py:169

commit v3 on v2

--- a/solution.py
+++ b/solution.py
@@ -9,6 +9,22 @@
 SIZES = (4, 2, 2, 2, 4, 2)
 NZ = 32
 BF16, F32 = jnp.bfloat16, jnp.float32
+
+
+def split_kernel(rec_ref, out_ref, sems):
+    copies = [
+        pltpu.make_async_copy(
+            rec_ref.at[:, :, :, :, pl.ds(zb * 16, 16), pl.ds(x * 128, 128)],
+            out_ref.at[zb, :, x],
+            sems.at[zb * 4 + x],
+        )
+        for zb in range(2)
+        for x in range(4)
+    ]
+    for copy in copies:
+        copy.start()
+    for copy in copies:
+        copy.wait()
 
 
 def scan_kernel(rec_ref, vert_ref, out_ref):
@@ -37,7 +53,7 @@
     tail_im = jnp.zeros((32, 128), F32)
     for z in range(NZ - 1, -1, -1):
         x, za, zb, j = z // 8, z // 4 % 2, z // 2 % 2, z % 2
-        re, im = [rec_ref[x, :, za, zb, j, p].reshape(32, 128).astype(F32) for p in range(2)]
+        re, im = [rec_ref[zb, :, x, za, j, p].reshape(32, 128).astype(F32) for p in range(2)]
         rc, rs, ic, is_ = re * c, re * s, im * c, im * s
         values = ((tail_re, tail_im), (rc + is_, ic - rs))
         for kind in range(2):
@@ -48,26 +64,28 @@
         c, s = c * step_re + s * step_im, s * step_re - c * step_im
 
 
-def unit_kernel(mine_ref, other_ref, out_ref, held_ref, sems):
+def unit_kernel(mine_ref, other_ref, out_ref):
     h = lax.axis_index("core")
-    copies = [
-        pltpu.make_async_copy(mine_ref, held_ref.at[h], sems.at[0]),
-        pltpu.make_async_copy(other_ref, held_ref.at[1 - h], sems.at[1]),
-    ]
-    for copy in copies:
-        copy.start()
-    for copy in copies:
-        copy.wait()
-
-    def matrix(kind, part, cores):
+
+    @pl.when(h == 0)
+    def _():
+        unit(mine_ref, (mine_ref, other_ref), out_ref)
+
+    @pl.when(h == 1)
+    def _():
+        unit(mine_ref, (other_ref, mine_ref), out_ref)
+
+
+def unit(mine, cores, out_ref):
+    def matrix(kind, part, refs):
         return jnp.concatenate(
             [
                 jnp.concatenate(
                     [
-                        held_ref[core, b, half, y, kind, part, zh]
+                        ref[y, half, b, kind, part, zh]
                         for zh in range(2)
                         for y in range(4)
-                        for core in cores
+                        for ref in refs
                         for half in range(2)
                     ],
                     axis=0,
@@ -77,20 +95,17 @@
             axis=1,
         )
 
-    def whole(kind, part):
-        return matrix(kind, part, (0, 1))
-
     def dot(a, b):
         return jnp.dot(a, b, preferred_element_type=F32)
 
-    left = jnp.concatenate([matrix(0, 0, (h,)), matrix(0, 1, (h,))], axis=0)
-    by_re = dot(left, whole(1, 0))
-    by_im = dot(left, whole(1, 1))
+    left = jnp.concatenate([matrix(0, 0, (mine,)), matrix(0, 1, (mine,))], axis=0)
+    by_re = dot(left, matrix(1, 0, cores))
+    by_im = dot(left, matrix(1, 1, cores))
     mid_re = (by_re[:256] - by_im[256:]).astype(BF16)
     mid_im = (by_im[:256] + by_re[256:]).astype(BF16)
     mid = jnp.concatenate([mid_re, mid_im], axis=0)
-    by_re = dot(mid, whole(0, 0))
-    by_im = dot(mid, whole(0, 1))
+    by_re = dot(mid, matrix(0, 0, cores))
+    by_im = dot(mid, matrix(0, 1, cores))
     parts = (by_re[:256] - by_im[256:], by_im[:256] + by_re[256:])
 
     lane = lax.broadcasted_iota(jnp.int32, (8, 8, 128), 2)
@@ -155,28 +170,32 @@
 
 
 def shards(recorded, vertical):
-    blocks = recorded.reshape(4, 2, 2, 2, 16, 4, 128).transpose(5, 0, 3, 1, 2, 4, 6)
-    sections = exchange(blocks.reshape(32, 2, 2, 16, 128), ("x", "zh", "za", "zb"))
+    blocks = call(
+        split_kernel,
+        (2, 2, 4, 2, 2, 2, 16, 128),
+        BF16,
+        [pl.BlockSpec(memory_space=pltpu.HBM)],
+        (recorded.reshape(2, 2, 2, 2, 32, 512),),
+        scratch=[pltpu.SemaphoreType.DMA((8,))],
+        moved=1 << 20,
+    )
+    sections = exchange(blocks.reshape(32, 2, 2, 16, 128), ("zb", "zh", "x", "za"))
     phased = call(
         scan_kernel,
         (NZ, 2, 2, 2, 16, 128),
         BF16,
         vmem(2),
-        (sections.reshape(4, 2, 2, 2, 2, 2, 16, 128), vertical),
+        (sections.reshape(2, 2, 4, 2, 2, 2, 16, 128), vertical),
         moved=3 << 19,
     )
-    mine = exchange(phased, ("x", "zb", "y")).reshape(4, 2, 4, 2, 2, 2, 16, 128)
+    mine = exchange(phased, ("y", "zb", "x")).reshape(4, 2, 4, 2, 2, 2, 16, 128)
     other = lax.ppermute(mine, "core", [(0, 1), (1, 0)])
     partial = call(
         unit_kernel,
         (4, 4, 4, 2, 16, 128),
         BF16,
-        [pl.BlockSpec(memory_space=pl.ANY)] * 2,
+        vmem(2),
         (mine, other),
-        scratch=[
-            pltpu.VMEM((2, 4, 2, 4, 2, 2, 2, 16, 128), BF16),
-            pltpu.SemaphoreType.DMA((2,)),
-        ],
         limit=40,
         flops=1 << 30,
         moved=5 << 19,

time: 84.8 us -> 84 us (level)
    reshape x1 -> x0, local copies, waits for them, and re-layouts: 1.16 us -> none  [shards(): recorded.reshape(4, 2, 2, 2, 16, 4, 128).transpose(5, 0, 3, 1, 2, 4, 6)]
    unnamed x2 -> x4, local copies, waits for them, and re-layouts: 0.01 us -> 1.05 us
    pallas_call x4 -> x5, Pallas kernels: 3.12 us -> 3.13 us  [call(): pl.pallas_call(kernel, out_shape=jax.ShapeDtypeStruct(shape, dtype), in_s...]
where the time goes in v3:
time: 84 us; the launch traced here: 83.7 us
  blocking collectives  76.8 us (91%)
  Pallas kernels  3.13 us (4%)
  waiting for transfers between devices  2.66 us (3%)
  local copies, waits for them, and re-layouts  1.05 us (1%)
    all_to_all x4, blocking collectives, exchange(): return lax.all_to_all(x, axes, 0, 0, tiled=True)  76.8 us
    pallas_call x5, Pallas kernels, call(): pl.pallas_call(kernel, out_shape=jax.ShapeDtypeStruct(shape, dtype), in_s...  3.13 us
    ppermute x1, waiting for transfers between devices, shards(): other = lax.ppermute(mine, 'core', [(0, 1), (1, 0)])  2.66 us
  transfers between devices with their start and end apart: 1, of which 1 were waited for; matrix products, arithmetic and copies ran while one was open for 0% of the time, Pallas kernels for 0%

profile of v3, /device:TPU:8, one launch (start us, length us, event | category | flops | bytes accessed | tf_op | source)
XLA Modules:
  0.0 83.7 jit_solution(16428132661117806715)
XLA Ops:
  0.0 0.0 copy-start
  0.0 1.0 %copy-done = bf16[4,2,2,32,512]{4,3,2,1,0:T(8,128)(2,1)S(1)} copy-done((bf16[4,2,2,32,512]{4,3,2,1,0:T(8,128)(2,1)S(1)}, bf16[4,2,2,32,512]{4,3,2,1,0:T(8,128)(2,1)}, u32[]{:S(2)}) %copy-start) | copy-done | bytes 524312
  1.0 0.2 shard_map.28
  1.2 0.0 copy-start.1
  1.2 29.1 %all_to_all.20 = bf16[32,2,2,16,128]{4,3,2,1,0:T(8,128)(2,1)S(1)} all-to-all(bf16[32,2,2,16,128]{4,3,2,1,0:T(8,128)(2,1)S(1)} %bitcast.8), channel_id=1, replica_groups=mesh['x'=4,'za'=2,'zb'=2,'zh'=2,'y'=4,'core'=2] {'zb','zh','x','za'}, dimensions={0} | all-to-all | bytes 1048576 | tf_op jit(solution)/shard_map/all_to_all | solution.py:169
  30.3 0.0 copy-done.1
  30.3 0.6 shard_map.29
  30.9 20.1 %all_to_all.21 = bf16[32,2,2,2,16,128]{5,4,3,2,1,0:T(8,128)(2,1)S(1)} all-to-all(bf16[32,2,2,2,16,128]{5,4,3,2,1,0:T(8,128)(2,1)S(1)} %shard_map.29), channel_id=1, replica_groups=mesh['x'=4,'za'=2,'zb'=2,'zh'=2,'y'=4,'core'=2] {'y','zb','x'}, dimensions={0} | all-to-all | bytes 2097152 | tf_op jit(solution)/shard_map/all_to_all | solution.py:169
  51.0 0.0 collective-permute-start
  51.0 2.7 %collective-permute-done.other_ref = bf16[4,2,4,2,2,2,16,128]{7,6,5,4,3,2,1,0:T(8,128)(2,1)S(1)} collective-permute-done((bf16[4,2,4,2,2,2,16,128]{7,6,5,4,3,2,1,0:T(8,128)(2,1)S(1)}, bf16[4,2,4,2,2,2,16,128]{7,6,5,4,3,2,1,0:T(8,128)(2,1)S(1)}, u32[]{:S(2)}, u32[]{:S(2)}) %collective-permute-start) | collective-permute-done | bytes 1048608 | tf_op jit(solution)/shard_map/ppermute | solution.py:192
  53.6 1.6 %shard_map.30 = bf16[4,4,4,2,16,128]{5,4,3,2,1,0:T(8,128)(2,1)S(1)} custom-call(bf16[4,2,4,2,2,2,16,128]{7,6,5,4,3,2,1,0:T(8,128)(2,1)S(1)} %bitcast.10, bf16[4,2,4,2,2,2,16,128]{7,6,5,4,3,2,1,0:T(8,128)(2,1)S(1)} %collective-permute-done.other_ref), custom_call_target="tpu_custom_call" | custom-call | flops 1073741824 | bytes 2621440 | tf_op jit(solution)/shard_map/pallas_call | solution.py:157
  55.2 15.8 %all_to_all.22.parts_ref = bf16[16,4,2,16,128]{4,3,2,1,0:T(8,128)(2,1)S(1)} all-to-all(bf16[16,4,2,16,128]{4,3,2,1,0:T(8,128)(2,1)S(1)} %bitcast.12), channel_id=1, replica_groups=mesh['x'=4,'za'=2,'zb'=2,'zh'=2,'y'=4,'core'=2] {'x','y'}, dimensions={0} | all-to-all | bytes 1048576 | tf_op jit(solution)/shard_map/all_to_all | solution.py:169
  71.1 0.1 shard_map.31
  71.1 11.8 %all_to_all.23 = bf16[8,16,128]{2,1,0:T(8,128)(2,1)S(1)} all-to-all(bf16[8,16,128]{2,1,0:T(8,128)(2,1)S(1)} %bitcast.13), channel_id=1, replica_groups=mesh['x'=4,'za'=2,'zb'=2,'zh'=2,'y'=4,'core'=2] {'zh','za','zb'}, dimensions={0} | all-to-all | bytes 65536 | tf_op jit(solution)/shard_map/all_to_all | solution.py:169
  83.0 0.7 shard_map.32
Async XLA Ops:
  0.0 1.0 %copy-start = (bf16[4,2,2,32,512]{4,3,2,1,0:T(8,128)(2,1)S(1)}, bf16[4,2,2,32,512]{4,3,2,1,0:T(8,128)(2,1)}, u32[]{:S(2)}) copy-start(bf16[4,2,2,32,512]{4,3,2,1,0:T(8,128)(2,1)} %param.2) | copy-start | bytes 1572868
  1.2 29.1 %copy-start.1 = (f32[4,512]{1,0:T(4,128)S(1)}, f32[4,512]{1,0:T(4,128)}, u32[]{:S(2)}) copy-start(f32[4,512]{1,0:T(4,128)} %vert_ref.1) | copy-start | bytes 24580
  51.0 2.7 %collective-permute-start = (bf16[4,2,4,2,2,2,16,128]{7,6,5,4,3,2,1,0:T(8,128)(2,1)S(1)}, bf16[4,2,4,2,2,2,16,128]{7,6,5,4,3,2,1,0:T(8,128)(2,1)S(1)}, u32[]{:S(2)}, u32[]{:S(2)}) collective-permute-start(bf16[4,2,4,2,2,2,16,128]{7,6,5,4,3,2,1,0:T(8,128)(2,1)S(1)} %bitcast.9), channel_id=1, source_target_pairs={{0,1},{1,0},{2,3},{3,2},{4,5},{5,4},{6,7},{7,6},{8,9},{9,8},{10,11... | collective-permute-start | bytes 3145736 | tf_op jit(solution)/shard_map/ppermute | solution.py:192

commit v4 on v3

--- a/solution.py
+++ b/solution.py
@@ -165,8 +165,9 @@
     )(*args)
 
 
-def exchange(x, axes):
-    return lax.all_to_all(x, axes, 0, 0, tiled=True)
+def exchange(x, axes, peers):
+    flat = x.reshape(peers, -1, 128)
+    return lax.all_to_all(flat, axes, 0, 0, tiled=True)
 
 
 def shards(recorded, vertical):
@@ -177,9 +178,10 @@
         [pl.BlockSpec(memory_space=pltpu.HBM)],
         (recorded.reshape(2, 2, 2, 2, 32, 512),),
         scratch=[pltpu.SemaphoreType.DMA((8,))],
+        limit=60,
         moved=1 << 20,
     )
-    sections = exchange(blocks.reshape(32, 2, 2, 16, 128), ("zb", "zh", "x", "za"))
+    sections = exchange(blocks, ("zb", "zh", "x", "za"), 32)
     phased = call(
         scan_kernel,
         (NZ, 2, 2, 2, 16, 128),
@@ -188,7 +190,7 @@
         (sections.reshape(2, 2, 4, 2, 2, 2, 16, 128), vertical),
         moved=3 << 19,
     )
-    mine = exchange(phased, ("y", "zb", "x")).reshape(4, 2, 4, 2, 2, 2, 16, 128)
+    mine = exchange(phased, ("y", "zb", "x"), 32).reshape(4, 2, 4, 2, 2, 2, 16, 128)
     other = lax.ppermute(mine, "core", [(0, 1), (1, 0)])
     partial = call(
         unit_kernel,
@@ -200,9 +202,9 @@
         flops=1 << 30,
         moved=5 << 19,
     )
-    parts = exchange(partial.reshape(16, 4, 2, 16, 128), ("x", "y"))
+    parts = exchange(partial, ("x", "y"), 16).reshape(16, 4, 2, 16, 128)
     summed = call(sum_kernel, (2, 4, 16, 128), BF16, vmem(1), (parts,), moved=1 << 19)
-    last = exchange(summed.reshape(8, 16, 128), ("zh", "za", "zb"))
+    last = exchange(summed, ("zh", "za", "zb"), 8)
     return call(last_kernel, (4, 2, 32, 32), F32, vmem(1), (last.reshape(4, 2, 16, 128),))
 
 

time: 84 us -> 85 us (1.012)
  Pallas kernels: 3.13 us -> 4.88 us
  local copies, waits for them, and re-layouts: 1.05 us -> 0.01 us
    pallas_call x5, Pallas kernels: 3.13 us -> 4.88 us  [call(): pl.pallas_call(kernel, out_shape=jax.ShapeDtypeStruct(shape, dtype), in_s...]
    unnamed x4 -> x2, local copies, waits for them, and re-layouts: 1.05 us -> 0.01 us
where the time goes in v4:
time: 85 us; the launch traced here: 84.6 us
  blocking collectives  77 us (91%)
  Pallas kernels  4.88 us (6%)
  waiting for transfers between devices  2.66 us (3%)
    all_to_all x4, blocking collectives, exchange(): return lax.all_to_all(flat, axes, 0, 0, tiled=True)  77 us
    pallas_call x5, Pallas kernels, call(): pl.pallas_call(kernel, out_shape=jax.ShapeDtypeStruct(shape, dtype), in_s...  4.88 us
    ppermute x1, waiting for transfers between devices, shards(): other = lax.ppermute(mine, 'core', [(0, 1), (1, 0)])  2.66 us
  transfers between devices with their start and end apart: 1, of which 1 were waited for; matrix products, arithmetic and copies ran while one was open for 0% of the time, Pallas kernels for 0%

profile of v4, /device:TPU:8, one launch (start us, length us, event | category | flops | bytes accessed | tf_op | source)
XLA Modules:
  0.0 84.6 jit_solution(7206055253364165211)
XLA Ops:
  0.0 1.9 %shard_map.28 = bf16[2,2,4,2,2,2,16,128]{7,6,5,4,3,2,1,0:T(8,128)(2,1)} custom-call(bf16[2,2,2,2,32,512]{5,4,3,2,1,0:T(8,128)(2,1)} %bitcast.18), custom_call_target="tpu_custom_call" | custom-call | bytes 1048576 | tf_op jit(solution)/shard_map/pallas_call | solution.py:157
  1.9 0.0 copy-start
  1.9 29.3 %all_to_all.20 = bf16[32,64,128]{2,1,0:T(8,128)(2,1)S(1)} all-to-all(bf16[32,64,128]{2,1,0:T(8,128)(2,1)} %bitcast.17), channel_id=1, replica_groups=mesh['x'=4,'za'=2,'zb'=2,'zh'=2,'y'=4,'core'=2] {'zb','zh','x','za'}, dimensions={0} | all-to-all | bytes 1048576 | tf_op jit(solution)/shard_map/all_to_all | solution.py:170
  31.2 0.0 copy-done
  31.2 0.6 shard_map.29
  31.8 20.1 %all_to_all.21 = bf16[32,128,128]{2,1,0:T(8,128)(2,1)S(1)} all-to-all(bf16[32,128,128]{2,1,0:T(8,128)(2,1)S(1)} %bitcast.9), channel_id=1, replica_groups=mesh['x'=4,'za'=2,'zb'=2,'zh'=2,'y'=4,'core'=2] {'y','zb','x'}, dimensions={0} | all-to-all | bytes 2097152 | tf_op jit(solution)/shard_map/all_to_all | solution.py:170
  51.9 0.0 collective-permute-start
  51.9 2.7 %collective-permute-done.other_ref = bf16[4,2,4,2,2,2,16,128]{7,6,5,4,3,2,1,0:T(8,128)(2,1)S(1)} collective-permute-done((bf16[4,2,4,2,2,2,16,128]{7,6,5,4,3,2,1,0:T(8,128)(2,1)S(1)}, bf16[4,2,4,2,2,2,16,128]{7,6,5,4,3,2,1,0:T(8,128)(2,1)S(1)}, u32[]{:S(2)}, u32[]{:S(2)}) %collective-permute-start) | collective-permute-done | bytes 1048608 | tf_op jit(solution)/shard_map/ppermute | solution.py:194
  54.5 1.6 %shard_map.30 = bf16[4,4,4,2,16,128]{5,4,3,2,1,0:T(8,128)(2,1)S(1)} custom-call(bf16[4,2,4,2,2,2,16,128]{7,6,5,4,3,2,1,0:T(8,128)(2,1)S(1)} %bitcast.13, bf16[4,2,4,2,2,2,16,128]{7,6,5,4,3,2,1,0:T(8,128)(2,1)S(1)} %collective-permute-done.other_ref), custom_call_target="tpu_custom_call" | custom-call | flops 1073741824 | bytes 2621440 | tf_op jit(solution)/shard_map/pallas_call | solution.py:157
  56.1 15.8 %all_to_all.22 = bf16[16,128,128]{2,1,0:T(8,128)(2,1)S(1)} all-to-all(bf16[16,128,128]{2,1,0:T(8,128)(2,1)S(1)} %bitcast.14), channel_id=1, replica_groups=mesh['x'=4,'za'=2,'zb'=2,'zh'=2,'y'=4,'core'=2] {'x','y'}, dimensions={0} | all-to-all | bytes 1048576 | tf_op jit(solution)/shard_map/all_to_all | solution.py:170
  72.0 0.1 shard_map.31
  72.0 11.8 %all_to_all.23 = bf16[8,16,128]{2,1,0:T(8,128)(2,1)S(1)} all-to-all(bf16[8,16,128]{2,1,0:T(8,128)(2,1)S(1)} %bitcast.15), channel_id=1, replica_groups=mesh['x'=4,'za'=2,'zb'=2,'zh'=2,'y'=4,'core'=2] {'zh','za','zb'}, dimensions={0} | all-to-all | bytes 65536 | tf_op jit(solution)/shard_map/all_to_all | solution.py:170
  83.9 0.7 shard_map.32
Async XLA Ops:
  1.9 29.3 %copy-start = (f32[4,512]{1,0:T(4,128)S(1)}, f32[4,512]{1,0:T(4,128)}, u32[]{:S(2)}) copy-start(f32[4,512]{1,0:T(4,128)} %vert_ref.1) | copy-start | bytes 24580
  51.9 2.7 %collective-permute-start = (bf16[4,2,4,2,2,2,16,128]{7,6,5,4,3,2,1,0:T(8,128)(2,1)S(1)}, bf16[4,2,4,2,2,2,16,128]{7,6,5,4,3,2,1,0:T(8,128)(2,1)S(1)}, u32[]{:S(2)}, u32[]{:S(2)}) collective-permute-start(bf16[4,2,4,2,2,2,16,128]{7,6,5,4,3,2,1,0:T(8,128)(2,1)S(1)} %bitcast.12), channel_id=1, source_target_pairs={{0,1},{1,0},{2,3},{3,2},{4,5},{5,4},{6,7},{7,6},{8,9},{9,8},{10,11... | collective-permute-start | bytes 3145736 | tf_op jit(solution)/shard_map/ppermute | solution.py:194

commit v5 on v4

--- a/solution.py
+++ b/solution.py
@@ -127,21 +127,15 @@
                 )
             packed.append(g)
         for zl in range(4):
-            both = jnp.concatenate([packed[0][zl], packed[1][zl]], axis=1).astype(BF16)
-            for zh in range(2):
-                out_ref[x, :, zl, zh] = both[zh * 4 : (zh + 1) * 4]
+            out_ref[x, zl] = jnp.concatenate([packed[0][zl], packed[1][zl]], axis=1).astype(BF16)
 
 
 def sum_kernel(parts_ref, out_ref):
-    for zl in range(4):
-        for zh in range(2):
-            total = jnp.sum(parts_ref[:, zl, zh].astype(F32), axis=0)
-            out_ref[zh, zl] = total.astype(BF16)
-
-
-def last_kernel(parts_ref, out_ref):
     for w in range(4):
-        total = parts_ref[w, 0].astype(F32) + parts_ref[w, 1].astype(F32)
+        total = jnp.zeros((16, 128), F32)
+        for x in range(4):
+            for zb in range(2):
+                total = total + jnp.sum(parts_ref[x, w % 2, zb, w // 2].astype(F32), axis=0)
         for part in range(2):
             for g in range(4):
                 out_ref[w, part, g * 8 : (g + 1) * 8, :] = total[
@@ -178,7 +172,6 @@
         [pl.BlockSpec(memory_space=pltpu.HBM)],
         (recorded.reshape(2, 2, 2, 2, 32, 512),),
         scratch=[pltpu.SemaphoreType.DMA((8,))],
-        limit=60,
         moved=1 << 20,
     )
     sections = exchange(blocks, ("zb", "zh", "x", "za"), 32)
@@ -194,7 +187,7 @@
     other = lax.ppermute(mine, "core", [(0, 1), (1, 0)])
     partial = call(
         unit_kernel,
-        (4, 4, 4, 2, 16, 128),
+        (4, 4, 8, 16, 128),
         BF16,
         vmem(2),
         (mine, other),
@@ -202,10 +195,15 @@
         flops=1 << 30,
         moved=5 << 19,
     )
-    parts = exchange(partial, ("x", "y"), 16).reshape(16, 4, 2, 16, 128)
-    summed = call(sum_kernel, (2, 4, 16, 128), BF16, vmem(1), (parts,), moved=1 << 19)
-    last = exchange(summed, ("zh", "za", "zb"), 8)
-    return call(last_kernel, (4, 2, 32, 32), F32, vmem(1), (last.reshape(4, 2, 16, 128),))
+    parts = exchange(partial, ("x", "za", "zb", "zh", "y"), 128)
+    return call(
+        sum_kernel,
+        (4, 2, 32, 32),
+        F32,
+        vmem(1),
+        (parts.reshape(4, 2, 2, 2, 4, 16, 128),),
+        moved=1 << 19,
+    )
 
 
 def solution(mesh):

time: 85 us -> 84.6 us (level)
  Pallas kernels: 4.88 us -> 3.1 us
  local copies, waits for them, and re-layouts: 0.01 us -> 1.05 us
    pallas_call x5 -> x4, Pallas kernels: 4.88 us -> 3.1 us  [call(): pl.pallas_call(kernel, out_shape=jax.ShapeDtypeStruct(shape, dtype), in_s...]
    unnamed x2 -> x4, local copies, waits for them, and re-layouts: 0.01 us -> 1.05 us
    all_to_all x4 -> x3, blocking collectives: 77 us -> 76.7 us  [exchange(): return lax.all_to_all(flat, axes, 0, 0, tiled=True)]
where the time goes in v5:
time: 84.6 us; the launch traced here: 83.6 us
  blocking collectives  76.7 us (91%)
  Pallas kernels  3.1 us (4%)
  waiting for transfers between devices  2.66 us (3%)
  local copies, waits for them, and re-layouts  1.05 us (1%)
    all_to_all x3, blocking collectives, exchange(): return lax.all_to_all(flat, axes, 0, 0, tiled=True)  76.7 us
    pallas_call x4, Pallas kernels, call(): pl.pallas_call(kernel, out_shape=jax.ShapeDtypeStruct(shape, dtype), in_s...  3.1 us
    ppermute x1, waiting for transfers between devices, shards(): other = lax.ppermute(mine, 'core', [(0, 1), (1, 0)])  2.66 us
  transfers between devices with their start and end apart: 1, of which 1 were waited for; matrix products, arithmetic and copies ran while one was open for 0% of the time, Pallas kernels for 0%

profile of v5, /device:TPU:8, one launch (start us, length us, event | category | flops | bytes accessed | tf_op | source)
XLA Modules:
  0.0 83.6 jit_solution(13022945783232197235)
XLA Ops:
  0.0 0.0 copy-start
  0.0 1.0 %copy-done = bf16[4,2,2,32,512]{4,3,2,1,0:T(8,128)(2,1)S(1)} copy-done((bf16[4,2,2,32,512]{4,3,2,1,0:T(8,128)(2,1)S(1)}, bf16[4,2,2,32,512]{4,3,2,1,0:T(8,128)(2,1)}, u32[]{:S(2)}) %copy-start) | copy-done | bytes 524312
  1.0 0.2 shard_map.28
  1.2 0.0 copy-start.1
  1.2 29.1 %all_to_all.15 = bf16[32,64,128]{2,1,0:T(8,128)(2,1)S(1)} all-to-all(bf16[32,64,128]{2,1,0:T(8,128)(2,1)S(1)} %bitcast.10), channel_id=1, replica_groups=mesh['x'=4,'za'=2,'zb'=2,'zh'=2,'y'=4,'core'=2] {'zb','zh','x','za'}, dimensions={0} | all-to-all | bytes 1048576 | tf_op jit(solution)/shard_map/all_to_all | solution.py:164
  30.3 0.0 copy-done.1
  30.3 0.6 shard_map.29
  30.9 20.1 %all_to_all.16 = bf16[32,128,128]{2,1,0:T(8,128)(2,1)S(1)} all-to-all(bf16[32,128,128]{2,1,0:T(8,128)(2,1)S(1)} %bitcast.7), channel_id=1, replica_groups=mesh['x'=4,'za'=2,'zb'=2,'zh'=2,'y'=4,'core'=2] {'y','zb','x'}, dimensions={0} | all-to-all | bytes 2097152 | tf_op jit(solution)/shard_map/all_to_all | solution.py:164
  51.0 0.0 collective-permute-start
  51.0 2.7 %collective-permute-done.other_ref = bf16[4,2,4,2,2,2,16,128]{7,6,5,4,3,2,1,0:T(8,128)(2,1)S(1)} collective-permute-done((bf16[4,2,4,2,2,2,16,128]{7,6,5,4,3,2,1,0:T(8,128)(2,1)S(1)}, bf16[4,2,4,2,2,2,16,128]{7,6,5,4,3,2,1,0:T(8,128)(2,1)S(1)}, u32[]{:S(2)}, u32[]{:S(2)}) %collective-permute-start) | collective-permute-done | bytes 1048608 | tf_op jit(solution)/shard_map/ppermute | solution.py:187
  53.6 1.6 %shard_map.30 = bf16[4,4,8,16,128]{4,3,2,1,0:T(8,128)(2,1)S(1)} custom-call(bf16[4,2,4,2,2,2,16,128]{7,6,5,4,3,2,1,0:T(8,128)(2,1)S(1)} %bitcast.12, bf16[4,2,4,2,2,2,16,128]{7,6,5,4,3,2,1,0:T(8,128)(2,1)S(1)} %collective-permute-done.other_ref), custom_call_target="tpu_custom_call" | custom-call | flops 1073741824 | bytes 2621440 | tf_op jit(solution)/shard_map/pallas_call | solution.py:151
  55.2 27.6 %all_to_all.17 = bf16[128,16,128]{2,1,0:T(8,128)(2,1)S(1)} all-to-all(bf16[128,16,128]{2,1,0:T(8,128)(2,1)S(1)} %bitcast.14), channel_id=1, replica_groups=mesh['x'=4,'za'=2,'zb'=2,'zh'=2,'y'=4,'core'=2] {'x','za','zb','zh','y'}, dimensions={0} | all-to-all | bytes 1048576 | tf_op jit(solution)/shard_map/all_to_all | solution.py:164
  82.8 0.8 shard_map.31
Async XLA Ops:
  0.0 1.0 %copy-start = (bf16[4,2,2,32,512]{4,3,2,1,0:T(8,128)(2,1)S(1)}, bf16[4,2,2,32,512]{4,3,2,1,0:T(8,128)(2,1)}, u32[]{:S(2)}) copy-start(bf16[4,2,2,32,512]{4,3,2,1,0:T(8,128)(2,1)} %param.2) | copy-start | bytes 1572868
  1.2 29.1 %copy-start.1 = (f32[4,512]{1,0:T(4,128)S(1)}, f32[4,512]{1,0:T(4,128)}, u32[]{:S(2)}) copy-start(f32[4,512]{1,0:T(4,128)} %vert_ref.1) | copy-start | bytes 24580
  51.0 2.7 %collective-permute-start = (bf16[4,2,4,2,2,2,16,128]{7,6,5,4,3,2,1,0:T(8,128)(2,1)S(1)}, bf16[4,2,4,2,2,2,16,128]{7,6,5,4,3,2,1,0:T(8,128)(2,1)S(1)}, u32[]{:S(2)}, u32[]{:S(2)}) collective-permute-start(bf16[4,2,4,2,2,2,16,128]{7,6,5,4,3,2,1,0:T(8,128)(2,1)S(1)} %bitcast.11), channel_id=1, source_target_pairs={{0,1},{1,0},{2,3},{3,2},{4,5},{5,4},{6,7},{7,6},{8,9},{9,8},{10,11... | collective-permute-start | bytes 3145736 | tf_op jit(solution)/shard_map/ppermute | solution.py:187

commit v6 on v4

v6 whole, which is shorter than its diff:
```python
import jax
import jax.numpy as jnp
from jax import lax
from jax.experimental import pallas as pl
from jax.experimental.pallas import tpu as pltpu
from jax.sharding import Mesh, PartitionSpec as P

NAMES = ("x", "za", "zb", "zh", "y", "core")
SIZES = (4, 2, 2, 2, 4, 2)
NZ = 32
BF16, F32 = jnp.bfloat16, jnp.float32


def split_kernel(rec_ref, out_ref, sems):
    copies = [
        pltpu.make_async_copy(
            rec_ref.at[:, :, :, pl.ds(zb * 16, 16), :], out_ref.at[:, zb], sems.at[zb]
        )
        for zb in range(2)
    ]
    for copy in copies:
        copy.start()
    for copy in copies:
        copy.wait()


def phases(vert_ref):
    w = lax.axis_index("zh") * 2 + lax.axis_index("za")
    first_row = (
        lax.axis_index("y") * 2 + lax.axis_index("core")
    ) * 32 + lax.axis_index("zb") * 16
    rows = vert_ref[...]
    picked = lax.broadcasted_iota(jnp.int32, rows.shape, 0) == w
    waves = jnp.sum(jnp.where(picked, rows, 0.0), axis=0, keepdims=True)
    row = lax.broadcasted_iota(jnp.int32, (32, 512), 0)
    lane = lax.broadcasted_iota(jnp.int32, (32, 512), 1)
    mine = lane == (row % 16) + (row // 16) * 256 + first_row
    row_wave = jnp.sum(jnp.where(mine, waves, 0.0), axis=1, keepdims=True)
    last = (lax.axis_index("x") * 8 + 7).astype(F32)
    return row_wave + waves, last


def phase_kernel(vert_ref, out_ref):
    angle, last = phases(vert_ref)
    out_ref[0], out_ref[1] = jnp.cos(angle), jnp.sin(angle)
    out_ref[2], out_ref[3] = jnp.cos(last * angle) * (1.0 / NZ), jnp.sin(last * angle) * (1.0 / NZ)


def sections(rec_ref, phase_ref, b, visit):
    cols = slice(b * 128, (b + 1) * 128)
    step_re, step_im, c, s = [phase_ref[k, :, cols] for k in range(4)]
    for z in range(7, -1, -1):
        re, im = [
            rec_ref[:, z // 4, z // 2 % 2, z % 2, p, :, cols].reshape(32, 128).astype(F32)
            for p in range(2)
        ]
        visit(z, cols, re * c, re * s, im * c, im * s)
        c, s = c * step_re + s * step_im, s * step_re - c * step_im


def minus_kernel(rec_ref, phase_ref, minus_ref, sum_ref):
    for b in range(4):
        total = [jnp.zeros((32, 128), F32)] * 2

        def visit(z, cols, rc, rs, ic, is_):
            minus_ref[z, 0, :, :, cols] = (rc + is_).astype(BF16).reshape(2, 16, 128)
            minus_ref[z, 1, :, :, cols] = (ic - rs).astype(BF16).reshape(2, 16, 128)
            total[0] = total[0] + (rc - is_)
            total[1] = total[1] + (rs + ic)

        sections(rec_ref, phase_ref, b, visit)
        for part in range(2):
            sum_ref[part, :, b * 128 : (b + 1) * 128] = total[part].astype(BF16)


def tail_kernel(rec_ref, phase_ref, one_ref, two_ref, three_ref, tail_ref):
    for b in range(4):
        tail = [
            sum(ref[part, :, b * 128 : (b + 1) * 128].astype(F32) for ref in (one_ref, two_ref, three_ref))
            for part in range(2)
        ]

        def visit(z, cols, rc, rs, ic, is_):
            for part in range(2):
                tail_ref[z, part, :, :, cols] = tail[part].astype(BF16).reshape(2, 16, 128)
            tail[0] = tail[0] + (rc - is_)
            tail[1] = tail[1] + (rs + ic)

        sections(rec_ref, phase_ref, b, visit)


def matrix(part, refs):
    return jnp.concatenate(
        [
            ref[half, y, part, zh]
            for zh in range(2)
            for y in range(4)
            for ref in refs
            for half in range(2)
        ],
        axis=0,
    )


def dot(a, b):
    return jnp.dot(a, b, preferred_element_type=F32)


def each_core(body, mine, other):
    h = lax.axis_index("core")

    @pl.when(h == 0)
    def _():
        body((mine, other))

    @pl.when(h == 1)
    def _():
        body((other, mine))


def left_kernel(tail_ref, mine_ref, other_ref, out_ref):
    def body(minus):
        left = jnp.concatenate([matrix(0, (tail_ref,)), matrix(1, (tail_ref,))], axis=0)
        by_re = dot(left, matrix(0, minus))
        by_im = dot(left, matrix(1, minus))
        out_ref[:256] = (by_re[:256] - by_im[256:]).astype(BF16)
        out_ref[256:] = (by_im[:256] + by_re[256:]).astype(BF16)

    each_core(body, mine_ref, other_ref)


def right_kernel(left_ref, mine_ref, other_ref, out_ref):
    def body(tail):
        by_re = dot(left_ref[...], matrix(0, tail))
        by_im = dot(left_ref[...], matrix(1, tail))
        pack((by_re[:256] - by_im[256:], by_im[:256] + by_re[256:]), out_ref)

    each_core(body, mine_ref, other_ref)


def pack(parts, out_ref):
    lane = lax.broadcasted_iota(jnp.int32, (8, 8, 128), 2)
    low, even = lane < 64, (lane // 32) % 2 == 0
    for x in range(4):
        packed = []
        for part in parts:
            cols = part[:, x * 128 : (x + 1) * 128].reshape(8, 4, 8, 128)
            g = [cols[:, k] for k in range(4)]
            for a, b in ((0, 2), (1, 3)):
                g[a], g[b] = (
                    jnp.where(low, g[a], pltpu.roll(g[b], 64, 2)),
                    jnp.where(low, pltpu.roll(g[a], 64, 2), g[b]),
                )
            for a, b in ((0, 1), (2, 3)):
                g[a], g[b] = (
                    jnp.where(even, g[a], pltpu.roll(g[b], 32, 2)),
                    jnp.where(even, pltpu.roll(g[a], 96, 2), g[b]),
                )
            packed.append(g)
        for zl in range(4):
            both = jnp.concatenate([packed[0][zl], packed[1][zl]], axis=1).astype(BF16)
            for zh in range(2):
                out_ref[x, :, zl, zh] = both[zh * 4 : (zh + 1) * 4]


def sum_kernel(parts_ref, out_ref):
    for zl in range(4):
        for zh in range(2):
            total = jnp.sum(parts_ref[:, zl, zh].astype(F32), axis=0)
            out_ref[zh, zl] = total.astype(BF16)


def last_kernel(parts_ref, out_ref):
    for w in range(4):
        total = parts_ref[w, 0].astype(F32) + parts_ref[w, 1].astype(F32)
        for part in range(2):
            for g in range(4):
                out_ref[w, part, g * 8 : (g + 1) * 8, :] = total[
                    part * 8 : (part + 1) * 8, g * 32 : (g + 1) * 32
                ]


def vmem(n):
    return [pl.BlockSpec(memory_space=pltpu.VMEM)] * n


def call(kernel, shapes, args, in_specs=None, scratch=(), limit=16, flops=0, moved=0):
    outs = [jax.ShapeDtypeStruct(shape, dtype) for shape, dtype in shapes]
    specs = [pl.BlockSpec(memory_space=pltpu.VMEM)] * len(outs)
    return pl.pallas_call(
        kernel,
        out_shape=outs if len(outs) > 1 else outs[0],
        in_specs=in_specs or vmem(len(args)),
        out_specs=specs if len(outs) > 1 else specs[0],
        scratch_shapes=list(scratch),
        compiler_params=pltpu.CompilerParams(vmem_limit_bytes=limit << 20),
        cost_estimate=pl.CostEstimate(flops=flops, bytes_accessed=moved, transcendentals=0),
    )(*args)


def exchange(x, axes, peers):
    flat = x.reshape(peers, -1, x.shape[-1])
    return lax.all_to_all(flat, axes, 0, 0, tiled=True)


def swap(x):
    return lax.ppermute(x, "core", [(0, 1), (1, 0)])


def shards(recorded, vertical):
    blocks = call(
        split_kernel,
        [((4, 2, 2, 2, 16, 512), BF16)],
        (recorded,),
        in_specs=[pl.BlockSpec(memory_space=pl.ANY)],
        scratch=[pltpu.SemaphoreType.DMA((2,))],
        moved=1 << 20,
    )
    phase = call(phase_kernel, [((4, 32, 512), F32)], (vertical,), moved=1 << 18)
    rec = exchange(blocks, ("zh", "za", "zb"), 8).reshape(2, 2, 2, 2, 2, 16, 512)
    unit = (8, 2, 2, 16, 512)
    minus, block_sum = call(
        minus_kernel, [(unit, BF16), ((2, 32, 512), BF16)], (rec, phase), moved=1 << 20
    )
    deeper = [
        lax.ppermute(block_sum, "x", [(x, x - step) for x in range(step, 4)]) for step in (1, 2, 3)
    ]
    minus = exchange(minus, ("zb", "y"), 8).reshape(2, 4, 2, 2, 16, 512)
    tail = call(tail_kernel, [(unit, BF16)], (rec, phase, *deeper), moved=1 << 20)
    tail = exchange(tail, ("zb", "y"), 8).reshape(2, 4, 2, 2, 16, 512)
    left = call(
        left_kernel,
        [((512, 512), BF16)],
        (tail, minus, swap(minus)),
        limit=30,
        flops=1 << 29,
        moved=2 << 20,
    )
    partial = call(
        right_kernel,
        [((4, 4, 4, 2, 16, 128), BF16)],
        (left, tail, swap(tail)),
        limit=30,
        flops=1 << 29,
        moved=2 << 20,
    )
    parts = exchange(partial, ("x", "y"), 16).reshape(16, 4, 2, 16, 128)
    summed = call(sum_kernel, [((2, 4, 16, 128), BF16)], (parts,), moved=1 << 19)
    last = exchange(summed, ("zh", "za", "zb"), 8)
    return call(last_kernel, [((4, 2, 32, 32), F32)], (last.reshape(4, 2, 16, 128),))


def solution(mesh):
    chips = Mesh(mesh.devices.reshape(SIZES), NAMES)
    depth, col = ("x", "za", "zb"), ("zh", "y", "core")
    return jax.shard_map(
        shards,
        mesh=chips,
        in_specs=(P(None, depth, None, col, None), P()),
        out_specs=P(None, None, col, depth),
        check_vma=False,
    )
```

time: 85 us -> 89 us (1.047)
  blocking collectives: 77 us -> 25.4 us
  waiting for transfers between devices: 2.66 us -> 32.9 us
  starting transfers between devices: 0.01 us -> 23 us
  Pallas kernels: 4.88 us -> 6.09 us
  local copies, waits for them, and re-layouts: 0.01 us -> 1.05 us
    all_to_all x4 -> x2, blocking collectives: 77 us -> 25.4 us  [exchange(): return lax.all_to_all(flat, axes, 0, 0, tiled=True)]
    all_to_all x0 -> x3, waiting for transfers between devices: none -> 23.5 us  [exchange(): return lax.all_to_all(flat, axes, 0, 0, tiled=True)]
    all_to_all x0 -> x3, starting transfers between devices: none -> 19.1 us  [exchange(): return lax.all_to_all(flat, axes, 0, 0, tiled=True)]
    ppermute x1 -> x5, waiting for transfers between devices: 2.66 us -> 9.34 us  [the longest x3 8.15 us: shards(): lax.ppermute(block_sum, 'x', [(x, x - step) for x in range(step, 4)])]
    ppermute x1 -> x5, starting transfers between devices: 0.01 us -> 3.87 us  [the longest x3 3.86 us: shards(): lax.ppermute(block_sum, 'x', [(x, x - step) for x in range(step, 4)])]
    pallas_call x5 -> x8, Pallas kernels: 4.88 us -> 6.09 us  [call(): pl.pallas_call(kernel, out_shape=outs if len(outs) > 1 else outs[0], in_s...]
    unnamed x2 -> x4, local copies, waits for them, and re-layouts: 0.01 us -> 1.05 us
  transfers between devices with their start and end apart: 1 -> 8, of which waited for: 1 -> 6; matrix products, arithmetic and copies ran while one was open for 0% -> 0% of each run, Pallas kernels for 0% -> 3%
where the time goes in v6:
time: 89 us; the launch traced here: 88.5 us
  waiting for transfers between devices  32.9 us (37%)
  blocking collectives  25.4 us (29%)
  starting transfers between devices  23 us (26%)
  Pallas kernels  6.09 us (7%)
  local copies, waits for them, and re-layouts  1.05 us (1%)
    all_to_all x2, blocking collectives, exchange(): return lax.all_to_all(flat, axes, 0, 0, tiled=True)  25.4 us
    all_to_all x3, waiting for transfers between devices, exchange(): return lax.all_to_all(flat, axes, 0, 0, tiled=True)  23.5 us
    all_to_all x3, starting transfers between devices, exchange(): return lax.all_to_all(flat, axes, 0, 0, tiled=True)  19.1 us
    ppermute x3, waiting for transfers between devices, shards(): lax.ppermute(block_sum, 'x', [(x, x - step) for x in range(step, 4)])  8.15 us
    pallas_call x8, Pallas kernels, call(): pl.pallas_call(kernel, out_shape=outs if len(outs) > 1 else outs[0], in_s...  6.09 us
    ppermute x3, starting transfers between devices, shards(): lax.ppermute(block_sum, 'x', [(x, x - step) for x in range(step, 4)])  3.86 us
  transfers between devices with their start and end apart: 8, of which 6 were waited for; matrix products, arithmetic and copies ran while one was open for 0% of the time, Pallas kernels for 3%

profile of v6, /device:TPU:8, one launch (start us, length us, event | category | flops | bytes accessed | tf_op | source)
XLA Modules:
  0.0 88.5 jit_solution(6161009232539316504)
XLA Ops:
  0.0 0.0 copy-start
  0.0 1.0 %copy-done = bf16[4,2,2,32,512]{4,3,2,1,0:T(8,128)(2,1)S(1)} copy-done((bf16[4,2,2,32,512]{4,3,2,1,0:T(8,128)(2,1)S(1)}, bf16[4,2,2,32,512]{4,3,2,1,0:T(8,128)(2,1)}, u32[]{:S(2)}) %copy-start) | copy-done | bytes 524312
  1.0 0.9 shard_map.28
  1.9 0.0 copy-start.1
  1.9 8.5 %all-to-all-start = ((bf16[8,64,512]{2,1,0:T(8,128)(2,1)}), bf16[8,64,512]{2,1,0:T(8,128)(2,1)S(1)}, u32[]{:S(2)}, u32[]{:S(2)}) async-start(bf16[8,64,512]{2,1,0:T(8,128)(2,1)} %bitcast), calls=%async_computation | async-start | bytes 1048576 | tf_op jit(solution)/shard_map/all_to_all | solution.py:203
  10.4 0.0 copy-done.1
  10.4 0.6 shard_map.29.phase_ref
  11.0 16.9 %all-to-all-done = bf16[8,64,512]{2,1,0:T(8,128)(2,1)S(1)} async-done(((bf16[8,64,512]{2,1,0:T(8,128)(2,1)}), bf16[8,64,512]{2,1,0:T(8,128)(2,1)S(1)}, u32[]{:S(2)}, u32[]{:S(2)}) %all-to-all-start) | async-done | bytes 524320 | tf_op jit(solution)/shard_map/all_to_all | solution.py:203
  27.9 1.1 %shard_map.30 = (bf16[8,2,2,16,512]{4,3,2,1,0:T(8,128)(2,1)}, bf16[2,32,512]{2,1,0:T(8,128)(2,1)S(1)}) custom-call(bf16[2,2,2,2,2,16,512]{6,5,4,3,2,1,0:T(8,128)(2,1)S(1)} %bitcast.10, f32[4,32,512]{2,1,0:T(8,128)S(1)} %shard_map.29.phase_ref), custom_call_target="tpu_custom_call" | custom-call | bytes 1048576 | tf_op jit(solution)/shard_map/pallas_call | solution.py:190
  29.0 4.9 %all-to-all-start.2 = ((bf16[8,64,512]{2,1,0:T(8,128)(2,1)}), bf16[8,64,512]{2,1,0:T(8,128)(2,1)S(1)}, u32[]{:S(2)}, u32[]{:S(2)}) async-start(bf16[8,64,512]{2,1,0:T(8,128)(2,1)} %bitcast.4), calls=%async_computation.2 | async-start | bytes 1048576 | tf_op jit(solution)/shard_map/all_to_all | solution.py:203
  33.9 1.3 %collective-permute-start = (bf16[2,32,512]{2,1,0:T(8,128)(2,1)S(1)}, bf16[2,32,512]{2,1,0:T(8,128)(2,1)S(1)}, u32[]{:S(2)}, u32[]{:S(2)}) collective-permute-start(bf16[2,32,512]{2,1,0:T(8,128)(2,1)S(1)} %get-tuple-element.7), channel_id=1, source_target_pairs={{64,0},{128,64},{192,128},{65,1},{129,65},{193,129},{66,2},{130,66... | collective-permute-start | bytes 196616 | tf_op jit(solution)/shard_map/ppermute | solution.py:226
  35.2 1.3 %collective-permute-start.1 = (bf16[2,32,512]{2,1,0:T(8,128)(2,1)S(1)}, bf16[2,32,512]{2,1,0:T(8,128)(2,1)S(1)}, u32[]{:S(2)}, u32[]{:S(2)}) collective-permute-start(bf16[2,32,512]{2,1,0:T(8,128)(2,1)S(1)} %get-tuple-element.7), channel_id=1, source_target_pairs={{128,0},{192,64},{129,1},{193,65},{130,2},{194,66},{131,3},{195,67... | collective-permute-start | bytes 196616 | tf_op jit(solution)/shard_map/ppermute | solution.py:226
  36.5 1.3 %collective-permute-start.2 = (bf16[2,32,512]{2,1,0:T(8,128)(2,1)S(1)}, bf16[2,32,512]{2,1,0:T(8,128)(2,1)S(1)}, u32[]{:S(2)}, u32[]{:S(2)}) collective-permute-start(bf16[2,32,512]{2,1,0:T(8,128)(2,1)S(1)} %get-tuple-element.7), channel_id=1, source_target_pairs={{192,0},{193,1},{194,2},{195,3},{196,4},{197,5},{198,6},{199,7},{2... | collective-permute-start | bytes 196616 | tf_op jit(solution)/shard_map/ppermute | solution.py:226
  37.8 2.3 %collective-permute-done.one_ref = bf16[2,32,512]{2,1,0:T(8,128)(2,1)S(1)} collective-permute-done((bf16[2,32,512]{2,1,0:T(8,128)(2,1)S(1)}, bf16[2,32,512]{2,1,0:T(8,128)(2,1)S(1)}, u32[]{:S(2)}, u32[]{:S(2)}) %collective-permute-start) | collective-permute-done | bytes 65568 | tf_op jit(solution)/shard_map/ppermute | solution.py:226
  40.1 2.8 %collective-permute-done.1.two_ref = bf16[2,32,512]{2,1,0:T(8,128)(2,1)S(1)} collective-permute-done((bf16[2,32,512]{2,1,0:T(8,128)(2,1)S(1)}, bf16[2,32,512]{2,1,0:T(8,128)(2,1)S(1)}, u32[]{:S(2)}, u32[]{:S(2)}) %collective-permute-start.1) | collective-permute-done | bytes 65568 | tf_op jit(solution)/shard_map/ppermute | solution.py:226
  42.9 3.1 %collective-permute-done.2.three_ref = bf16[2,32,512]{2,1,0:T(8,128)(2,1)S(1)} collective-permute-done((bf16[2,32,512]{2,1,0:T(8,128)(2,1)S(1)}, bf16[2,32,512]{2,1,0:T(8,128)(2,1)S(1)}, u32[]{:S(2)}, u32[]{:S(2)}) %collective-permute-start.2) | collective-permute-done | bytes 65568 | tf_op jit(solution)/shard_map/ppermute | solution.py:226
  45.9 1.1 %shard_map.31 = bf16[8,2,2,16,512]{4,3,2,1,0:T(8,128)(2,1)} custom-call(bf16[2,2,2,2,2,16,512]{6,5,4,3,2,1,0:T(8,128)(2,1)S(1)} %bitcast.11, f32[4,32,512]{2,1,0:T(8,128)S(1)} %shard_map.29.phase_ref, bf16[2,32,512]{2,1,0:T(8,128)(2,1)S(1)} %collective-permute-done.one_ref, bf16[2,32,512]{2,1,0:T(8,128)(2,1)S(1)} %collective-permute-done.1.two_ref, ...), custom_call_target="tpu_custom_call" | custom-call | bytes 1048576 | tf_op jit(solution)/shard_map/pallas_call | solution.py:190
  47.0 0.0 all-to-all-done.2
  47.0 5.7 %all-to-all-start.1 = ((bf16[8,64,512]{2,1,0:T(8,128)(2,1)}), bf16[8,64,512]{2,1,0:T(8,128)(2,1)S(1)}, u32[]{:S(2)}, u32[]{:S(2)}) async-start(bf16[8,64,512]{2,1,0:T(8,128)(2,1)} %bitcast.2), calls=%async_computation.1 | async-start | bytes 1048576 | tf_op jit(solution)/shard_map/all_to_all | solution.py:203
  52.7 0.0 collective-permute-start.3
  52.7 6.6 %all-to-all-done.1 = bf16[8,64,512]{2,1,0:T(8,128)(2,1)S(1)} async-done(((bf16[8,64,512]{2,1,0:T(8,128)(2,1)}), bf16[8,64,512]{2,1,0:T(8,128)(2,1)S(1)}, u32[]{:S(2)}, u32[]{:S(2)}) %all-to-all-start.1) | async-done | bytes 524320 | tf_op jit(solution)/shard_map/all_to_all | solution.py:203
  59.4 0.0 collective-permute-start.4
  59.4 0.0 collective-permute-done.3.other_ref
  59.4 0.7 shard_map.32.left_ref
  60.1 1.2 %collective-permute-done.4.other_ref = bf16[2,4,2,2,16,512]{5,4,3,2,1,0:T(8,128)(2,1)S(1)} collective-permute-done((bf16[2,4,2,2,16,512]{5,4,3,2,1,0:T(8,128)(2,1)S(1)}, bf16[2,4,2,2,16,512]{5,4,3,2,1,0:T(8,128)(2,1)S(1)}, u32[]{:S(2)}, u32[]{:S(2)}) %collective-permute-start.4) | collective-permute-done | bytes 524320 | tf_op jit(solution)/shard_map/ppermute | solution.py:207
  61.3 1.0 %shard_map.33 = bf16[4,4,4,2,16,128]{5,4,3,2,1,0:T(8,128)(2,1)S(1)} custom-call(bf16[512,512]{1,0:T(8,128)(2,1)S(1)} %shard_map.32.left_ref, bf16[2,4,2,2,16,512]{5,4,3,2,1,0:T(8,128)(2,1)S(1)} %bitcast.14, bf16[2,4,2,2,16,512]{5,4,3,2,1,0:T(8,128)(2,1)S(1)} %collective-permute-done.4.other_ref), custom_call_target="tpu_custom_call" | custom-call | flops 536870912 | bytes 2097152 | tf_op jit(solution)/shard_map/pallas_call | solution.py:190
  62.2 14.9 %all_to_all.25 = bf16[16,128,128]{2,1,0:T(8,128)(2,1)S(1)} all-to-all(bf16[16,128,128]{2,1,0:T(8,128)(2,1)S(1)} %bitcast.18), channel_id=1, replica_groups=mesh['x'=4,'za'=2,'zb'=2,'zh'=2,'y'=4,'core'=2] {'x','y'}, dimensions={0} | all-to-all | bytes 1048576 | tf_op jit(solution)/shard_map/all_to_all | solution.py:203
  77.1 0.1 shard_map.34
  77.2 10.5 %all_to_all.26 = bf16[8,16,128]{2,1,0:T(8,128)(2,1)S(1)} all-to-all(bf16[8,16,128]{2,1,0:T(8,128)(2,1)S(1)} %bitcast.19), channel_id=1, replica_groups=mesh['x'=4,'za'=2,'zb'=2,'zh'=2,'y'=4,'core'=2] {'zh','za','zb'}, dimensions={0} | all-to-all | bytes 65536 | tf_op jit(solution)/shard_map/all_to_all | solution.py:203
  87.7 0.7 shard_map.35
Async XLA Ops:
  0.0 1.0 %copy-start = (bf16[4,2,2,32,512]{4,3,2,1,0:T(8,128)(2,1)S(1)}, bf16[4,2,2,32,512]{4,3,2,1,0:T(8,128)(2,1)}, u32[]{:S(2)}) copy-start(bf16[4,2,2,32,512]{4,3,2,1,0:T(8,128)(2,1)} %rec_ref.1) | copy-start | bytes 1572868
  1.9 8.5 %copy-start.1 = (f32[4,512]{1,0:T(4,128)S(1)}, f32[4,512]{1,0:T(4,128)}, u32[]{:S(2)}) copy-start(f32[4,512]{1,0:T(4,128)} %vert_ref.1) | copy-start | bytes 24580
  1.9 26.0 %all-to-all-start = ((bf16[8,64,512]{2,1,0:T(8,128)(2,1)}), bf16[8,64,512]{2,1,0:T(8,128)(2,1)S(1)}, u32[]{:S(2)}, u32[]{:S(2)}) async-start(bf16[8,64,512]{2,1,0:T(8,128)(2,1)} %bitcast), calls=%async_computation | async-start | bytes 1048576 | tf_op jit(solution)/shard_map/all_to_all | solution.py:203
  29.0 18.0 %all-to-all-start.2 = ((bf16[8,64,512]{2,1,0:T(8,128)(2,1)}), bf16[8,64,512]{2,1,0:T(8,128)(2,1)S(1)}, u32[]{:S(2)}, u32[]{:S(2)}) async-start(bf16[8,64,512]{2,1,0:T(8,128)(2,1)} %bitcast.4), calls=%async_computation.2 | async-start | bytes 1048576 | tf_op jit(solution)/shard_map/all_to_all | solution.py:203
  33.9 6.1 %collective-permute-start = (bf16[2,32,512]{2,1,0:T(8,128)(2,1)S(1)}, bf16[2,32,512]{2,1,0:T(8,128)(2,1)S(1)}, u32[]{:S(2)}, u32[]{:S(2)}) collective-permute-start(bf16[2,32,512]{2,1,0:T(8,128)(2,1)S(1)} %get-tuple-element.7), channel_id=1, source_target_pairs={{64,0},{128,64},{192,128},{65,1},{129,65},{193,129},{66,2},{130,66... | collective-permute-start | bytes 196616 | tf_op jit(solution)/shard_map/ppermute | solution.py:226
  35.2 7.7 %collective-permute-start.1 = (bf16[2,32,512]{2,1,0:T(8,128)(2,1)S(1)}, bf16[2,32,512]{2,1,0:T(8,128)(2,1)S(1)}, u32[]{:S(2)}, u32[]{:S(2)}) collective-permute-start(bf16[2,32,512]{2,1,0:T(8,128)(2,1)S(1)} %get-tuple-element.7), channel_id=1, source_target_pairs={{128,0},{192,64},{129,1},{193,65},{130,2},{194,66},{131,3},{195,67... | collective-permute-start | bytes 196616 | tf_op jit(solution)/shard_map/ppermute | solution.py:226
  36.5 9.4 %collective-permute-start.2 = (bf16[2,32,512]{2,1,0:T(8,128)(2,1)S(1)}, bf16[2,32,512]{2,1,0:T(8,128)(2,1)S(1)}, u32[]{:S(2)}, u32[]{:S(2)}) collective-permute-start(bf16[2,32,512]{2,1,0:T(8,128)(2,1)S(1)} %get-tuple-element.7), channel_id=1, source_target_pairs={{192,0},{193,1},{194,2},{195,3},{196,4},{197,5},{198,6},{199,7},{2... | collective-permute-start | bytes 196616 | tf_op jit(solution)/shard_map/ppermute | solution.py:226
  47.0 12.3 %all-to-all-start.1 = ((bf16[8,64,512]{2,1,0:T(8,128)(2,1)}), bf16[8,64,512]{2,1,0:T(8,128)(2,1)S(1)}, u32[]{:S(2)}, u32[]{:S(2)}) async-start(bf16[8,64,512]{2,1,0:T(8,128)(2,1)} %bitcast.2), calls=%async_computation.1 | async-start | bytes 1048576 | tf_op jit(solution)/shard_map/all_to_all | solution.py:203
  52.7 6.6 %collective-permute-start.3 = (bf16[2,4,2,2,16,512]{5,4,3,2,1,0:T(8,128)(2,1)S(1)}, bf16[2,4,2,2,16,512]{5,4,3,2,1,0:T(8,128)(2,1)S(1)}, u32[]{:S(2)}, u32[]{:S(2)}) collective-permute-start(bf16[2,4,2,2,16,512]{5,4,3,2,1,0:T(8,128)(2,1)S(1)} %bitcast.16), channel_id=1, source_target_pairs={{0,1},{1,0},{2,3},{3,2},{4,5},{5,4},{6,7},{7,6},{8,9},{9,8},{10,11... | collective-permute-start | bytes 1572872 | tf_op jit(solution)/shard_map/ppermute | solution.py:207
  59.4 1.9 %collective-permute-start.4 = (bf16[2,4,2,2,16,512]{5,4,3,2,1,0:T(8,128)(2,1)S(1)}, bf16[2,4,2,2,16,512]{5,4,3,2,1,0:T(8,128)(2,1)S(1)}, u32[]{:S(2)}, u32[]{:S(2)}) collective-permute-start(bf16[2,4,2,2,16,512]{5,4,3,2,1,0:T(8,128)(2,1)S(1)} %bitcast.12), channel_id=1, source_target_pairs={{0,1},{1,0},{2,3},{3,2},{4,5},{5,4},{6,7},{7,6},{8,9},{9,8},{10,11... | collective-permute-start | bytes 1572872 | tf_op jit(solution)/shard_map/ppermute | solution.py:207

commit v7 on v6

--- a/solution.py
+++ b/solution.py
@@ -40,12 +40,6 @@
     return row_wave + waves, last
 
 
-def phase_kernel(vert_ref, out_ref):
-    angle, last = phases(vert_ref)
-    out_ref[0], out_ref[1] = jnp.cos(angle), jnp.sin(angle)
-    out_ref[2], out_ref[3] = jnp.cos(last * angle) * (1.0 / NZ), jnp.sin(last * angle) * (1.0 / NZ)
-
-
 def sections(rec_ref, phase_ref, b, visit):
     cols = slice(b * 128, (b + 1) * 128)
     step_re, step_im, c, s = [phase_ref[k, :, cols] for k in range(4)]
@@ -58,13 +52,15 @@
         c, s = c * step_re + s * step_im, s * step_re - c * step_im
 
 
-def minus_kernel(rec_ref, phase_ref, minus_ref, sum_ref):
+def block_kernel(rec_ref, vert_ref, phase_ref, sum_ref):
+    angle, last = phases(vert_ref)
+    phase_ref[0], phase_ref[1] = jnp.cos(angle), jnp.sin(angle)
+    phase_ref[2] = jnp.cos(last * angle) * (1.0 / NZ)
+    phase_ref[3] = jnp.sin(last * angle) * (1.0 / NZ)
     for b in range(4):
         total = [jnp.zeros((32, 128), F32)] * 2
 
         def visit(z, cols, rc, rs, ic, is_):
-            minus_ref[z, 0, :, :, cols] = (rc + is_).astype(BF16).reshape(2, 16, 128)
-            minus_ref[z, 1, :, :, cols] = (ic - rs).astype(BF16).reshape(2, 16, 128)
             total[0] = total[0] + (rc - is_)
             total[1] = total[1] + (rs + ic)
 
@@ -73,69 +69,65 @@
             sum_ref[part, :, b * 128 : (b + 1) * 128] = total[part].astype(BF16)
 
 
-def tail_kernel(rec_ref, phase_ref, one_ref, two_ref, three_ref, tail_ref):
+def scan_kernel(rec_ref, phase_ref, one_ref, two_ref, three_ref, out_ref):
     for b in range(4):
+        cols = slice(b * 128, (b + 1) * 128)
         tail = [
-            sum(ref[part, :, b * 128 : (b + 1) * 128].astype(F32) for ref in (one_ref, two_ref, three_ref))
+            sum(ref[part, :, cols].astype(F32) for ref in (one_ref, two_ref, three_ref))
             for part in range(2)
         ]
 
         def visit(z, cols, rc, rs, ic, is_):
-            for part in range(2):
-                tail_ref[z, part, :, :, cols] = tail[part].astype(BF16).reshape(2, 16, 128)
+            values = (tail, (rc + is_, ic - rs))
+            for kind in range(2):
+                for part in range(2):
+                    out_ref[z, kind, part, :, :, cols] = (
+                        values[kind][part].astype(BF16).reshape(2, 16, 128)
+                    )
             tail[0] = tail[0] + (rc - is_)
             tail[1] = tail[1] + (rs + ic)
 
         sections(rec_ref, phase_ref, b, visit)
 
 
-def matrix(part, refs):
-    return jnp.concatenate(
-        [
-            ref[half, y, part, zh]
-            for zh in range(2)
-            for y in range(4)
-            for ref in refs
-            for half in range(2)
-        ],
-        axis=0,
-    )
-
-
 def dot(a, b):
     return jnp.dot(a, b, preferred_element_type=F32)
 
 
-def each_core(body, mine, other):
+def unit_kernel(mine_ref, other_ref, out_ref):
     h = lax.axis_index("core")
 
     @pl.when(h == 0)
     def _():
-        body((mine, other))
+        unit(mine_ref, (mine_ref, other_ref), out_ref)
 
     @pl.when(h == 1)
     def _():
-        body((other, mine))
-
-
-def left_kernel(tail_ref, mine_ref, other_ref, out_ref):
-    def body(minus):
-        left = jnp.concatenate([matrix(0, (tail_ref,)), matrix(1, (tail_ref,))], axis=0)
-        by_re = dot(left, matrix(0, minus))
-        by_im = dot(left, matrix(1, minus))
-        out_ref[:256] = (by_re[:256] - by_im[256:]).astype(BF16)
-        out_ref[256:] = (by_im[:256] + by_re[256:]).astype(BF16)
-
-    each_core(body, mine_ref, other_ref)
-
-
-def right_kernel(left_ref, mine_ref, other_ref, out_ref):
-    def body(tail):
-        by_re = dot(left_ref[...], matrix(0, tail))
-        by_im = dot(left_ref[...], matrix(1, tail))
-        pack((by_re[:256] - by_im[256:], by_im[:256] + by_re[256:]), out_ref)
-
-    each_core(body, mine_ref, other_ref)
+        unit(mine_ref, (other_ref, mine_ref), out_ref)
+
+
+def unit(mine, cores, out_ref):
+    def matrix(kind, part, refs):
+        return jnp.concatenate(
+            [
+                ref[half, y, kind, part, zh]
+                for zh in range(2)
+                for y in range(4)
+                for ref in refs
+                for half in range(2)
+            ],
+            axis=0,
+        )
+
+    left = jnp.concatenate([matrix(0, 0, (mine,)), matrix(0, 1, (mine,))], axis=0)
+    by_re = dot(left, matrix(1, 0, cores))
+    by_im = dot(left, matrix(1, 1, cores))
+    mid_re = (by_re[:256] - by_im[256:]).astype(BF16)
+    mid_im = (by_im[:256] + by_re[256:]).astype(BF16)
+    mid = jnp.concatenate([mid_re, mid_im], axis=0)
+    by_re = dot(mid, matrix(0, 0, cores))
+    by_im = dot(mid, matrix(0, 1, cores))
+    pack((by_re[:256] - by_im[256:], by_im[:256] + by_re[256:]), out_ref)
 
 
 def pack(parts, out_ref):
@@ -216,33 +208,30 @@
         scratch=[pltpu.SemaphoreType.DMA((2,))],
         moved=1 << 20,
     )
-    phase = call(phase_kernel, [((4, 32, 512), F32)], (vertical,), moved=1 << 18)
     rec = exchange(blocks, ("zh", "za", "zb"), 8).reshape(2, 2, 2, 2, 2, 16, 512)
-    unit = (8, 2, 2, 16, 512)
-    minus, block_sum = call(
-        minus_kernel, [(unit, BF16), ((2, 32, 512), BF16)], (rec, phase), moved=1 << 20
+    phase, block_sum = call(
+        block_kernel,
+        [((4, 32, 512), F32), ((2, 32, 512), BF16)],
+        (rec, vertical),
+        moved=1 << 20,
     )
     deeper = [
         lax.ppermute(block_sum, "x", [(x, x - step) for x in range(step, 4)]) for step in (1, 2, 3)
     ]
-    minus = exchange(minus, ("zb", "y"), 8).reshape(2, 4, 2, 2, 16, 512)
-    tail = call(tail_kernel, [(unit, BF16)], (rec, phase, *deeper), moved=1 << 20)
-    tail = exchange(tail, ("zb", "y"), 8).reshape(2, 4, 2, 2, 16, 512)
-    left = call(
-        left_kernel,
-        [((512, 512), BF16)],
-        (tail, minus, swap(minus)),
-        limit=30,
-        flops=1 << 29,
-        moved=2 << 20,
-    )
+    phased = call(
+        scan_kernel,
+        [((8, 2, 2, 2, 16, 512), BF16)],
+        (rec, phase, *deeper),
+        moved=1 << 20,
+    )
+    mine = exchange(phased, ("zb", "y"), 8).reshape(2, 4, 2, 2, 2, 16, 512)
     partial = call(
-        right_kernel,
+        unit_kernel,
         [((4, 4, 4, 2, 16, 128), BF16)],
-        (left, tail, swap(tail)),
-        limit=30,
-        flops=1 << 29,
-        moved=2 << 20,
+        (mine, swap(mine)),
+        limit=40,
+        flops=1 << 30,
+        moved=5 << 19,
     )
     parts = exchange(partial, ("x", "y"), 16).reshape(16, 4, 2, 16, 128)
     summed = call(sum_kernel, [((2, 4, 16, 128), BF16)], (parts,), moved=1 << 19)

time: 89 us -> 86.7 us (0.974)
  blocking collectives: 25.4 us -> 70 us
  waiting for transfers between devices: 32.9 us -> 7.72 us
  starting transfers between devices: 23 us -> 3.88 us
  Pallas kernels: 6.09 us -> 3.66 us
    all_to_all x2 -> x4, blocking collectives: 25.4 us -> 70 us  [exchange(): return lax.all_to_all(flat, axes, 0, 0, tiled=True)]
    all_to_all x3 -> x0, waiting for transfers between devices: 23.5 us -> none  [exchange(): return lax.all_to_all(flat, axes, 0, 0, tiled=True)]
    all_to_all x3 -> x0, starting transfers between devices: 19.1 us -> none  [exchange(): return lax.all_to_all(flat, axes, 0, 0, tiled=True)]
    ppermute x3, waiting for transfers between devices: 8.15 us -> 5.07 us  [shards(): lax.ppermute(block_sum, 'x', [(x, x - step) for x in range(step, 4)])]
    pallas_call x8 -> x6, Pallas kernels: 6.09 us -> 3.66 us  [call(): pl.pallas_call(kernel, out_shape=outs if len(outs) > 1 else outs[0], in_s...]
    ppermute x2 -> x1, waiting for transfers between devices: 1.19 us -> 2.66 us  [swap(): return lax.ppermute(x, 'core', [(0, 1), (1, 0)])]
  transfers between devices with their start and end apart: 8 -> 4, of which waited for: 6 -> 3; matrix products, arithmetic and copies ran while one was open for 0% -> 0% of each run, Pallas kernels for 3% -> 0%
where the time goes in v7:
time: 86.7 us; the launch traced here: 86.4 us
  blocking collectives  70 us (81%)
  waiting for transfers between devices  7.72 us (9%)
  starting transfers between devices  3.88 us (4%)
  Pallas kernels  3.66 us (4%)
  local copies, waits for them, and re-layouts  1.05 us (1%)
    all_to_all x4, blocking collectives, exchange(): return lax.all_to_all(flat, axes, 0, 0, tiled=True)  70 us
    ppermute x3, waiting for transfers between devices, shards(): lax.ppermute(block_sum, 'x', [(x, x - step) for x in range(step, 4)])  5.07 us
    ppermute x3, starting transfers between devices, shards(): lax.ppermute(block_sum, 'x', [(x, x - step) for x in range(step, 4)])  3.88 us
    pallas_call x6, Pallas kernels, call(): pl.pallas_call(kernel, out_shape=outs if len(outs) > 1 else outs[0], in_s...  3.66 us
    ppermute x1, waiting for transfers between devices, swap(): return lax.ppermute(x, 'core', [(0, 1), (1, 0)])  2.66 us
  transfers between devices with their start and end apart: 4, of which 3 were waited for; matrix products, arithmetic and copies ran while one was open for 0% of the time, Pallas kernels for 0%

profile of v7, /device:TPU:8, one launch (start us, length us, event | category | flops | bytes accessed | tf_op | source)
XLA Modules:
  0.0 86.4 jit_solution(5567292642922171458)
XLA Ops:
  0.0 0.0 copy-start
  0.0 1.0 %copy-done = bf16[4,2,2,32,512]{4,3,2,1,0:T(8,128)(2,1)S(1)} copy-done((bf16[4,2,2,32,512]{4,3,2,1,0:T(8,128)(2,1)S(1)}, bf16[4,2,2,32,512]{4,3,2,1,0:T(8,128)(2,1)}, u32[]{:S(2)}) %copy-start) | copy-done | bytes 524312
  1.0 0.1 shard_map.28
  1.1 0.0 copy-start.1
  1.1 25.8 %all_to_all.20 = bf16[8,64,512]{2,1,0:T(8,128)(2,1)S(1)} all-to-all(bf16[8,64,512]{2,1,0:T(8,128)(2,1)S(1)} %bitcast.12), channel_id=1, replica_groups=mesh['x'=4,'za'=2,'zb'=2,'zh'=2,'y'=4,'core'=2] {'zh','za','zb'}, dimensions={0} | all-to-all | bytes 1048576 | tf_op jit(solution)/shard_map/all_to_all | solution.py:195
  26.9 0.0 copy-done.1
  26.9 0.8 shard_map.29
  27.7 1.3 %collective-permute-start.2 = (bf16[2,32,512]{2,1,0:T(8,128)(2,1)S(1)}, bf16[2,32,512]{2,1,0:T(8,128)(2,1)S(1)}, u32[]{:S(2)}, u32[]{:S(2)}) collective-permute-start(bf16[2,32,512]{2,1,0:T(8,128)(2,1)S(1)} %get-tuple-element.8), channel_id=1, source_target_pairs={{192,0},{193,1},{194,2},{195,3},{196,4},{197,5},{198,6},{199,7},{2... | collective-permute-start | bytes 196616 | tf_op jit(solution)/shard_map/ppermute | solution.py:219
  29.0 1.3 %collective-permute-start.1 = (bf16[2,32,512]{2,1,0:T(8,128)(2,1)S(1)}, bf16[2,32,512]{2,1,0:T(8,128)(2,1)S(1)}, u32[]{:S(2)}, u32[]{:S(2)}) collective-permute-start(bf16[2,32,512]{2,1,0:T(8,128)(2,1)S(1)} %get-tuple-element.8), channel_id=1, source_target_pairs={{128,0},{192,64},{129,1},{193,65},{130,2},{194,66},{131,3},{195,67... | collective-permute-start | bytes 196616 | tf_op jit(solution)/shard_map/ppermute | solution.py:219
  30.3 1.3 %collective-permute-start = (bf16[2,32,512]{2,1,0:T(8,128)(2,1)S(1)}, bf16[2,32,512]{2,1,0:T(8,128)(2,1)S(1)}, u32[]{:S(2)}, u32[]{:S(2)}) collective-permute-start(bf16[2,32,512]{2,1,0:T(8,128)(2,1)S(1)} %get-tuple-element.8), channel_id=1, source_target_pairs={{64,0},{128,64},{192,128},{65,1},{129,65},{193,129},{66,2},{130,66... | collective-permute-start | bytes 196616 | tf_op jit(solution)/shard_map/ppermute | solution.py:219
  31.6 3.5 %collective-permute-done.2.three_ref = bf16[2,32,512]{2,1,0:T(8,128)(2,1)S(1)} collective-permute-done((bf16[2,32,512]{2,1,0:T(8,128)(2,1)S(1)}, bf16[2,32,512]{2,1,0:T(8,128)(2,1)S(1)}, u32[]{:S(2)}, u32[]{:S(2)}) %collective-permute-start.2) | collective-permute-done | bytes 65568 | tf_op jit(solution)/shard_map/ppermute | solution.py:219
  35.1 1.6 %collective-permute-done.1.two_ref = bf16[2,32,512]{2,1,0:T(8,128)(2,1)S(1)} collective-permute-done((bf16[2,32,512]{2,1,0:T(8,128)(2,1)S(1)}, bf16[2,32,512]{2,1,0:T(8,128)(2,1)S(1)}, u32[]{:S(2)}, u32[]{:S(2)}) %collective-permute-start.1) | collective-permute-done | bytes 65568 | tf_op jit(solution)/shard_map/ppermute | solution.py:219
  36.7 0.0 collective-permute-done.one_ref
  36.7 0.4 shard_map.30
  37.1 15.7 %all_to_all.21 = bf16[8,128,512]{2,1,0:T(8,128)(2,1)S(1)} all-to-all(bf16[8,128,512]{2,1,0:T(8,128)(2,1)S(1)} %bitcast.10), channel_id=1, replica_groups=mesh['x'=4,'za'=2,'zb'=2,'zh'=2,'y'=4,'core'=2] {'zb','y'}, dimensions={0} | all-to-all | bytes 2097152 | tf_op jit(solution)/shard_map/all_to_all | solution.py:195
  52.7 0.0 collective-permute-start.3
  52.7 2.7 %collective-permute-done.3.other_ref = bf16[2,4,2,2,2,16,512]{6,5,4,3,2,1,0:T(8,128)(2,1)S(1)} collective-permute-done((bf16[2,4,2,2,2,16,512]{6,5,4,3,2,1,0:T(8,128)(2,1)S(1)}, bf16[2,4,2,2,2,16,512]{6,5,4,3,2,1,0:T(8,128)(2,1)S(1)}, u32[]{:S(2)}, u32[]{:S(2)}) %collective-permute-start.3) | collective-permute-done | bytes 1048608 | tf_op jit(solution)/shard_map/ppermute | solution.py:199
  55.4 1.6 %shard_map.31 = bf16[4,4,4,2,16,128]{5,4,3,2,1,0:T(8,128)(2,1)S(1)} custom-call(bf16[2,4,2,2,2,16,512]{6,5,4,3,2,1,0:T(8,128)(2,1)S(1)} %bitcast.14, bf16[2,4,2,2,2,16,512]{6,5,4,3,2,1,0:T(8,128)(2,1)S(1)} %collective-permute-done.3.other_ref), custom_call_target="tpu_custom_call" | custom-call | flops 1073741824 | bytes 2621440 | tf_op jit(solution)/shard_map/pallas_call | solution.py:182
  57.0 17.3 %all_to_all.22 = bf16[16,128,128]{2,1,0:T(8,128)(2,1)S(1)} all-to-all(bf16[16,128,128]{2,1,0:T(8,128)(2,1)S(1)} %bitcast.15), channel_id=1, replica_groups=mesh['x'=4,'za'=2,'zb'=2,'zh'=2,'y'=4,'core'=2] {'x','y'}, dimensions={0} | all-to-all | bytes 1048576 | tf_op jit(solution)/shard_map/all_to_all | solution.py:195
  74.2 0.1 shard_map.32
  74.3 11.3 %all_to_all.23 = bf16[8,16,128]{2,1,0:T(8,128)(2,1)S(1)} all-to-all(bf16[8,16,128]{2,1,0:T(8,128)(2,1)S(1)} %bitcast.16), channel_id=1, replica_groups=mesh['x'=4,'za'=2,'zb'=2,'zh'=2,'y'=4,'core'=2] {'zh','za','zb'}, dimensions={0} | all-to-all | bytes 65536 | tf_op jit(solution)/shard_map/all_to_all | solution.py:195
  85.6 0.7 shard_map.33
Async XLA Ops:
  0.0 1.0 %copy-start = (bf16[4,2,2,32,512]{4,3,2,1,0:T(8,128)(2,1)S(1)}, bf16[4,2,2,32,512]{4,3,2,1,0:T(8,128)(2,1)}, u32[]{:S(2)}) copy-start(bf16[4,2,2,32,512]{4,3,2,1,0:T(8,128)(2,1)} %rec_ref.1) | copy-start | bytes 1572868
  1.1 25.8 %copy-start.1 = (f32[4,512]{1,0:T(4,128)S(1)}, f32[4,512]{1,0:T(4,128)}, u32[]{:S(2)}) copy-start(f32[4,512]{1,0:T(4,128)} %vert_ref.1) | copy-start | bytes 24580
  27.7 7.4 %collective-permute-start.2 = (bf16[2,32,512]{2,1,0:T(8,128)(2,1)S(1)}, bf16[2,32,512]{2,1,0:T(8,128)(2,1)S(1)}, u32[]{:S(2)}, u32[]{:S(2)}) collective-permute-start(bf16[2,32,512]{2,1,0:T(8,128)(2,1)S(1)} %get-tuple-element.8), channel_id=1, source_target_pairs={{192,0},{193,1},{194,2},{195,3},{196,4},{197,5},{198,6},{199,7},{2... | collective-permute-start | bytes 196616 | tf_op jit(solution)/shard_map/ppermute | solution.py:219
  29.0 7.7 %collective-permute-start.1 = (bf16[2,32,512]{2,1,0:T(8,128)(2,1)S(1)}, bf16[2,32,512]{2,1,0:T(8,128)(2,1)S(1)}, u32[]{:S(2)}, u32[]{:S(2)}) collective-permute-start(bf16[2,32,512]{2,1,0:T(8,128)(2,1)S(1)} %get-tuple-element.8), channel_id=1, source_target_pairs={{128,0},{192,64},{129,1},{193,65},{130,2},{194,66},{131,3},{195,67... | collective-permute-start | bytes 196616 | tf_op jit(solution)/shard_map/ppermute | solution.py:219
  30.3 6.4 %collective-permute-start = (bf16[2,32,512]{2,1,0:T(8,128)(2,1)S(1)}, bf16[2,32,512]{2,1,0:T(8,128)(2,1)S(1)}, u32[]{:S(2)}, u32[]{:S(2)}) collective-permute-start(bf16[2,32,512]{2,1,0:T(8,128)(2,1)S(1)} %get-tuple-element.8), channel_id=1, source_target_pairs={{64,0},{128,64},{192,128},{65,1},{129,65},{193,129},{66,2},{130,66... | collective-permute-start | bytes 196616 | tf_op jit(solution)/shard_map/ppermute | solution.py:219
  52.7 2.7 %collective-permute-start.3 = (bf16[2,4,2,2,2,16,512]{6,5,4,3,2,1,0:T(8,128)(2,1)S(1)}, bf16[2,4,2,2,2,16,512]{6,5,4,3,2,1,0:T(8,128)(2,1)S(1)}, u32[]{:S(2)}, u32[]{:S(2)}) collective-permute-start(bf16[2,4,2,2,2,16,512]{6,5,4,3,2,1,0:T(8,128)(2,1)S(1)} %bitcast.13), channel_id=1, source_target_pairs={{0,1},{1,0},{2,3},{3,2},{4,5},{5,4},{6,7},{7,6},{8,9},{9,8},{10,11... | collective-permute-start | bytes 3145736 | tf_op jit(solution)/shard_map/ppermute | solution.py:199

commit v8 on v3

--- a/solution.py
+++ b/solution.py
@@ -129,19 +129,17 @@
         for zl in range(4):
             both = jnp.concatenate([packed[0][zl], packed[1][zl]], axis=1).astype(BF16)
             for zh in range(2):
-                out_ref[x, :, zl, zh] = both[zh * 4 : (zh + 1) * 4]
+                out_ref[:, x, zh, zl] = both[zh * 4 : (zh + 1) * 4]
 
 
 def sum_kernel(parts_ref, out_ref):
-    for zl in range(4):
-        for zh in range(2):
-            total = jnp.sum(parts_ref[:, zl, zh].astype(F32), axis=0)
-            out_ref[zh, zl] = total.astype(BF16)
+    for x in range(4):
+        out_ref[x] = jnp.sum(parts_ref[:, x].astype(F32), axis=0).astype(BF16)
 
 
 def last_kernel(parts_ref, out_ref):
     for w in range(4):
-        total = parts_ref[w, 0].astype(F32) + parts_ref[w, 1].astype(F32)
+        total = jnp.sum(parts_ref[:, w].astype(F32), axis=(0, 1))
         for part in range(2):
             for g in range(4):
                 out_ref[w, part, g * 8 : (g + 1) * 8, :] = total[
@@ -192,7 +190,7 @@
     other = lax.ppermute(mine, "core", [(0, 1), (1, 0)])
     partial = call(
         unit_kernel,
-        (4, 4, 4, 2, 16, 128),
+        (4, 4, 2, 4, 16, 128),
         BF16,
         vmem(2),
         (mine, other),
@@ -200,10 +198,10 @@
         flops=1 << 30,
         moved=5 << 19,
     )
-    parts = exchange(partial.reshape(16, 4, 2, 16, 128), ("x", "y"))
-    summed = call(sum_kernel, (2, 4, 16, 128), BF16, vmem(1), (parts,), moved=1 << 19)
-    last = exchange(summed.reshape(8, 16, 128), ("zh", "za", "zb"))
-    return call(last_kernel, (4, 2, 32, 32), F32, vmem(1), (last.reshape(4, 2, 16, 128),))
+    parts = exchange(partial, "y")
+    summed = call(sum_kernel, (4, 2, 4, 16, 128), BF16, vmem(1), (parts,), moved=1 << 19)
+    last = exchange(summed.reshape(32, 16, 128), ("x", "zh", "za", "zb"))
+    return call(last_kernel, (4, 2, 32, 32), F32, vmem(1), (last.reshape(4, 4, 2, 16, 128),))
 
 
 def solution(mesh):

time: 84 us -> 84.9 us (1.011)
  no operation moved by 1% of the time
where the time goes in v8:
time: 84.9 us; the launch traced here: 84.4 us
  blocking collectives  77.5 us (91%)
  Pallas kernels  3.13 us (4%)
  waiting for transfers between devices  2.66 us (3%)
  local copies, waits for them, and re-layouts  1.05 us (1%)
    all_to_all x4, blocking collectives, exchange(): return lax.all_to_all(x, axes, 0, 0, tiled=True)  77.5 us
    pallas_call x5, Pallas kernels, call(): pl.pallas_call(kernel, out_shape=jax.ShapeDtypeStruct(shape, dtype), in_s...  3.13 us
    ppermute x1, waiting for transfers between devices, shards(): other = lax.ppermute(mine, 'core', [(0, 1), (1, 0)])  2.66 us
  transfers between devices with their start and end apart: 1, of which 1 were waited for; matrix products, arithmetic and copies ran while one was open for 0% of the time, Pallas kernels for 0%

profile of v8, /device:TPU:8, one launch (start us, length us, event | category | flops | bytes accessed | tf_op | source)
XLA Modules:
  0.0 84.4 jit_solution(15506628340091065349)
XLA Ops:
  0.0 0.0 copy-start
  0.0 1.0 %copy-done = bf16[4,2,2,32,512]{4,3,2,1,0:T(8,128)(2,1)S(1)} copy-done((bf16[4,2,2,32,512]{4,3,2,1,0:T(8,128)(2,1)S(1)}, bf16[4,2,2,32,512]{4,3,2,1,0:T(8,128)(2,1)}, u32[]{:S(2)}) %copy-start) | copy-done | bytes 524312
  1.0 0.2 shard_map.28
  1.2 0.0 copy-start.1
  1.2 29.1 %all_to_all.20 = bf16[32,2,2,16,128]{4,3,2,1,0:T(8,128)(2,1)S(1)} all-to-all(bf16[32,2,2,16,128]{4,3,2,1,0:T(8,128)(2,1)S(1)} %bitcast.7), channel_id=1, replica_groups=mesh['x'=4,'za'=2,'zb'=2,'zh'=2,'y'=4,'core'=2] {'zb','zh','x','za'}, dimensions={0} | all-to-all | bytes 1048576 | tf_op jit(solution)/shard_map/all_to_all | solution.py:167
  30.3 0.0 copy-done.1
  30.3 0.6 shard_map.29
  30.9 20.1 %all_to_all.21 = bf16[32,2,2,2,16,128]{5,4,3,2,1,0:T(8,128)(2,1)S(1)} all-to-all(bf16[32,2,2,2,16,128]{5,4,3,2,1,0:T(8,128)(2,1)S(1)} %shard_map.29), channel_id=1, replica_groups=mesh['x'=4,'za'=2,'zb'=2,'zh'=2,'y'=4,'core'=2] {'y','zb','x'}, dimensions={0} | all-to-all | bytes 2097152 | tf_op jit(solution)/shard_map/all_to_all | solution.py:167
  51.0 0.0 collective-permute-start
  51.0 2.7 %collective-permute-done.other_ref = bf16[4,2,4,2,2,2,16,128]{7,6,5,4,3,2,1,0:T(8,128)(2,1)S(1)} collective-permute-done((bf16[4,2,4,2,2,2,16,128]{7,6,5,4,3,2,1,0:T(8,128)(2,1)S(1)}, bf16[4,2,4,2,2,2,16,128]{7,6,5,4,3,2,1,0:T(8,128)(2,1)S(1)}, u32[]{:S(2)}, u32[]{:S(2)}) %collective-permute-start) | collective-permute-done | bytes 1048608 | tf_op jit(solution)/shard_map/ppermute | solution.py:190
  53.6 1.6 %shard_map.30 = bf16[4,4,2,4,16,128]{5,4,3,2,1,0:T(8,128)(2,1)S(1)} custom-call(bf16[4,2,4,2,2,2,16,128]{7,6,5,4,3,2,1,0:T(8,128)(2,1)S(1)} %bitcast.9, bf16[4,2,4,2,2,2,16,128]{7,6,5,4,3,2,1,0:T(8,128)(2,1)S(1)} %collective-permute-done.other_ref), custom_call_target="tpu_custom_call" | custom-call | flops 1073741824 | bytes 2621440 | tf_op jit(solution)/shard_map/pallas_call | solution.py:155
  55.2 12.4 %all_to_all.22.parts_ref = bf16[4,4,2,4,16,128]{5,4,3,2,1,0:T(8,128)(2,1)S(1)} all-to-all(bf16[4,4,2,4,16,128]{5,4,3,2,1,0:T(8,128)(2,1)S(1)} %shard_map.30), channel_id=1, replica_groups=mesh['x'=4,'za'=2,'zb'=2,'zh'=2,'y'=4,'core'=2] {'y'}, dimensions={0} | all-to-all | bytes 1048576 | tf_op jit(solution)/shard_map/all_to_all | solution.py:167
  67.6 0.1 shard_map.31
  67.7 15.9 %all_to_all.23 = bf16[32,16,128]{2,1,0:T(8,128)(2,1)S(1)} all-to-all(bf16[32,16,128]{2,1,0:T(8,128)(2,1)S(1)} %bitcast.10), channel_id=1, replica_groups=mesh['x'=4,'za'=2,'zb'=2,'zh'=2,'y'=4,'core'=2] {'x','zh','za','zb'}, dimensions={0} | all-to-all | bytes 262144 | tf_op jit(solution)/shard_map/all_to_all | solution.py:167
  83.6 0.8 shard_map.32
Async XLA Ops:
  0.0 1.0 %copy-start = (bf16[4,2,2,32,512]{4,3,2,1,0:T(8,128)(2,1)S(1)}, bf16[4,2,2,32,512]{4,3,2,1,0:T(8,128)(2,1)}, u32[]{:S(2)}) copy-start(bf16[4,2,2,32,512]{4,3,2,1,0:T(8,128)(2,1)} %param.2) | copy-start | bytes 1572868
  1.2 29.1 %copy-start.1 = (f32[4,512]{1,0:T(4,128)S(1)}, f32[4,512]{1,0:T(4,128)}, u32[]{:S(2)}) copy-start(f32[4,512]{1,0:T(4,128)} %vert_ref.1) | copy-start | bytes 24580
  51.0 2.7 %collective-permute-start = (bf16[4,2,4,2,2,2,16,128]{7,6,5,4,3,2,1,0:T(8,128)(2,1)S(1)}, bf16[4,2,4,2,2,2,16,128]{7,6,5,4,3,2,1,0:T(8,128)(2,1)S(1)}, u32[]{:S(2)}, u32[]{:S(2)}) collective-permute-start(bf16[4,2,4,2,2,2,16,128]{7,6,5,4,3,2,1,0:T(8,128)(2,1)S(1)} %bitcast.8), channel_id=1, source_target_pairs={{0,1},{1,0},{2,3},{3,2},{4,5},{5,4},{6,7},{7,6},{8,9},{9,8},{10,11... | collective-permute-start | bytes 3145736 | tf_op jit(solution)/shard_map/ppermute | solution.py:190

commit v9 on v3

--- a/solution.py
+++ b/solution.py
@@ -135,13 +135,12 @@
 def sum_kernel(parts_ref, out_ref):
     for zl in range(4):
         for zh in range(2):
-            total = jnp.sum(parts_ref[:, zl, zh].astype(F32), axis=0)
-            out_ref[zh, zl] = total.astype(BF16)
+            out_ref[zh, zl] = jnp.sum(parts_ref[:, zl, zh].astype(F32), axis=0)
 
 
 def last_kernel(parts_ref, out_ref):
     for w in range(4):
-        total = parts_ref[w, 0].astype(F32) + parts_ref[w, 1].astype(F32)
+        total = parts_ref[w, 0] + parts_ref[w, 1]
         for part in range(2):
             for g in range(4):
                 out_ref[w, part, g * 8 : (g + 1) * 8, :] = total[
@@ -201,7 +200,7 @@
         moved=5 << 19,
     )
     parts = exchange(partial.reshape(16, 4, 2, 16, 128), ("x", "y"))
-    summed = call(sum_kernel, (2, 4, 16, 128), BF16, vmem(1), (parts,), moved=1 << 19)
+    summed = call(sum_kernel, (2, 4, 16, 128), F32, vmem(1), (parts,), moved=1 << 19)
     last = exchange(summed.reshape(8, 16, 128), ("zh", "za", "zb"))
     return call(last_kernel, (4, 2, 32, 32), F32, vmem(1), (last.reshape(4, 2, 16, 128),))
 

time: 84 us -> 84.4 us (level)
  no operation moved by 1% of the time
where the time goes in v9:
time: 84.4 us; the launch traced here: 84.1 us
  blocking collectives  77.2 us (91%)
  Pallas kernels  3.13 us (4%)
  waiting for transfers between devices  2.66 us (3%)
  local copies, waits for them, and re-layouts  1.05 us (1%)
    all_to_all x4, blocking collectives, exchange(): return lax.all_to_all(x, axes, 0, 0, tiled=True)  77.2 us
    pallas_call x5, Pallas kernels, call(): pl.pallas_call(kernel, out_shape=jax.ShapeDtypeStruct(shape, dtype), in_s...  3.13 us
    ppermute x1, waiting for transfers between devices, shards(): other = lax.ppermute(mine, 'core', [(0, 1), (1, 0)])  2.66 us
  transfers between devices with their start and end apart: 1, of which 1 were waited for; matrix products, arithmetic and copies ran while one was open for 0% of the time, Pallas kernels for 0%

profile of v9, /device:TPU:8, one launch (start us, length us, event | category | flops | bytes accessed | tf_op | source)
XLA Modules:
  0.0 84.1 jit_solution(1393731603435806543)
XLA Ops:
  0.0 0.0 copy-start
  0.0 1.0 %copy-done = bf16[4,2,2,32,512]{4,3,2,1,0:T(8,128)(2,1)S(1)} copy-done((bf16[4,2,2,32,512]{4,3,2,1,0:T(8,128)(2,1)S(1)}, bf16[4,2,2,32,512]{4,3,2,1,0:T(8,128)(2,1)}, u32[]{:S(2)}) %copy-start) | copy-done | bytes 524312
  1.0 0.2 shard_map.28
  1.2 0.0 copy-start.1
  1.2 29.1 %all_to_all.20 = bf16[32,2,2,16,128]{4,3,2,1,0:T(8,128)(2,1)S(1)} all-to-all(bf16[32,2,2,16,128]{4,3,2,1,0:T(8,128)(2,1)S(1)} %bitcast.8), channel_id=1, replica_groups=mesh['x'=4,'za'=2,'zb'=2,'zh'=2,'y'=4,'core'=2] {'zb','zh','x','za'}, dimensions={0} | all-to-all | bytes 1048576 | tf_op jit(solution)/shard_map/all_to_all | solution.py:168
  30.3 0.0 copy-done.1
  30.3 0.6 shard_map.29
  30.9 20.1 %all_to_all.21 = bf16[32,2,2,2,16,128]{5,4,3,2,1,0:T(8,128)(2,1)S(1)} all-to-all(bf16[32,2,2,2,16,128]{5,4,3,2,1,0:T(8,128)(2,1)S(1)} %shard_map.29), channel_id=1, replica_groups=mesh['x'=4,'za'=2,'zb'=2,'zh'=2,'y'=4,'core'=2] {'y','zb','x'}, dimensions={0} | all-to-all | bytes 2097152 | tf_op jit(solution)/shard_map/all_to_all | solution.py:168
  51.0 0.0 collective-permute-start
  51.0 2.7 %collective-permute-done.other_ref = bf16[4,2,4,2,2,2,16,128]{7,6,5,4,3,2,1,0:T(8,128)(2,1)S(1)} collective-permute-done((bf16[4,2,4,2,2,2,16,128]{7,6,5,4,3,2,1,0:T(8,128)(2,1)S(1)}, bf16[4,2,4,2,2,2,16,128]{7,6,5,4,3,2,1,0:T(8,128)(2,1)S(1)}, u32[]{:S(2)}, u32[]{:S(2)}) %collective-permute-start) | collective-permute-done | bytes 1048608 | tf_op jit(solution)/shard_map/ppermute | solution.py:191
  53.6 1.6 %shard_map.30 = bf16[4,4,4,2,16,128]{5,4,3,2,1,0:T(8,128)(2,1)S(1)} custom-call(bf16[4,2,4,2,2,2,16,128]{7,6,5,4,3,2,1,0:T(8,128)(2,1)S(1)} %bitcast.10, bf16[4,2,4,2,2,2,16,128]{7,6,5,4,3,2,1,0:T(8,128)(2,1)S(1)} %collective-permute-done.other_ref), custom_call_target="tpu_custom_call" | custom-call | flops 1073741824 | bytes 2621440 | tf_op jit(solution)/shard_map/pallas_call | solution.py:156
  55.2 15.8 %all_to_all.22.parts_ref = bf16[16,4,2,16,128]{4,3,2,1,0:T(8,128)(2,1)S(1)} all-to-all(bf16[16,4,2,16,128]{4,3,2,1,0:T(8,128)(2,1)S(1)} %bitcast.12), channel_id=1, replica_groups=mesh['x'=4,'za'=2,'zb'=2,'zh'=2,'y'=4,'core'=2] {'x','y'}, dimensions={0} | all-to-all | bytes 1048576 | tf_op jit(solution)/shard_map/all_to_all | solution.py:168
  71.1 0.1 shard_map.31
  71.1 12.2 %all_to_all.23 = f32[8,16,128]{2,1,0:T(8,128)S(1)} all-to-all(f32[8,16,128]{2,1,0:T(8,128)S(1)} %bitcast.13), channel_id=1, replica_groups=mesh['x'=4,'za'=2,'zb'=2,'zh'=2,'y'=4,'core'=2] {'zh','za','zb'}, dimensions={0} | all-to-all | bytes 131072 | tf_op jit(solution)/shard_map/all_to_all | solution.py:168
  83.3 0.7 shard_map.32
Async XLA Ops:
  0.0 1.0 %copy-start = (bf16[4,2,2,32,512]{4,3,2,1,0:T(8,128)(2,1)S(1)}, bf16[4,2,2,32,512]{4,3,2,1,0:T(8,128)(2,1)}, u32[]{:S(2)}) copy-start(bf16[4,2,2,32,512]{4,3,2,1,0:T(8,128)(2,1)} %param.2) | copy-start | bytes 1572868
  1.2 29.1 %copy-start.1 = (f32[4,512]{1,0:T(4,128)S(1)}, f32[4,512]{1,0:T(4,128)}, u32[]{:S(2)}) copy-start(f32[4,512]{1,0:T(4,128)} %vert_ref.1) | copy-start | bytes 24580
  51.0 2.7 %collective-permute-start = (bf16[4,2,4,2,2,2,16,128]{7,6,5,4,3,2,1,0:T(8,128)(2,1)S(1)}, bf16[4,2,4,2,2,2,16,128]{7,6,5,4,3,2,1,0:T(8,128)(2,1)S(1)}, u32[]{:S(2)}, u32[]{:S(2)}) collective-permute-start(bf16[4,2,4,2,2,2,16,128]{7,6,5,4,3,2,1,0:T(8,128)(2,1)S(1)} %bitcast.9), channel_id=1, source_target_pairs={{0,1},{1,0},{2,3},{3,2},{4,5},{5,4},{6,7},{7,6},{8,9},{9,8},{10,11... | collective-permute-start | bytes 3145736 | tf_op jit(solution)/shard_map/ppermute | solution.py:191

commit v10 on v9

--- a/solution.py
+++ b/solution.py
@@ -77,7 +77,7 @@
 
 
 def unit(mine, cores, out_ref):
-    def matrix(kind, part, refs):
+    def matrix(kind, part, refs, blocks):
         return jnp.concatenate(
             [
                 jnp.concatenate(
@@ -90,46 +90,54 @@
                     ],
                     axis=0,
                 )
-                for b in range(4)
+                for b in blocks
             ],
             axis=1,
         )
 
-    def dot(a, b):
-        return jnp.dot(a, b, preferred_element_type=F32)
-
-    left = jnp.concatenate([matrix(0, 0, (mine,)), matrix(0, 1, (mine,))], axis=0)
-    by_re = dot(left, matrix(1, 0, cores))
-    by_im = dot(left, matrix(1, 1, cores))
-    mid_re = (by_re[:256] - by_im[256:]).astype(BF16)
-    mid_im = (by_im[:256] + by_re[256:]).astype(BF16)
-    mid = jnp.concatenate([mid_re, mid_im], axis=0)
-    by_re = dot(mid, matrix(0, 0, cores))
-    by_im = dot(mid, matrix(0, 1, cores))
-    parts = (by_re[:256] - by_im[256:], by_im[:256] + by_re[256:])
-
+    def product(left, kind, blocks):
+        by_re, by_im = [
+            jnp.dot(left, matrix(kind, part, cores, blocks), preferred_element_type=F32)
+            for part in range(2)
+        ]
+        return by_re[:256] - by_im[256:], by_im[:256] + by_re[256:]
+
+    left = jnp.concatenate([matrix(0, part, (mine,), range(4)) for part in range(2)], axis=0)
+    mid = jnp.concatenate(
+        [
+            jnp.concatenate(product(left, 1, blocks), axis=0).astype(BF16)
+            for blocks in ((0, 1), (2, 3))
+        ],
+        axis=1,
+    )
+    for blocks in ((0, 1), (2, 3)):
+        parts = product(mid, 0, blocks)
+        for k, x in enumerate(blocks):
+            pack([part[:, k * 128 : (k + 1) * 128] for part in parts], x, out_ref)
+
+
+def pack(parts, x, out_ref):
     lane = lax.broadcasted_iota(jnp.int32, (8, 8, 128), 2)
     low, even = lane < 64, (lane // 32) % 2 == 0
-    for x in range(4):
-        packed = []
-        for part in parts:
-            cols = part[:, x * 128 : (x + 1) * 128].reshape(8, 4, 8, 128)
-            g = [cols[:, k] for k in range(4)]
-            for a, b in ((0, 2), (1, 3)):
-                g[a], g[b] = (
-                    jnp.where(low, g[a], pltpu.roll(g[b], 64, 2)),
-                    jnp.where(low, pltpu.roll(g[a], 64, 2), g[b]),
-                )
-            for a, b in ((0, 1), (2, 3)):
-                g[a], g[b] = (
-                    jnp.where(even, g[a], pltpu.roll(g[b], 32, 2)),
-                    jnp.where(even, pltpu.roll(g[a], 96, 2), g[b]),
-                )
-            packed.append(g)
-        for zl in range(4):
-            both = jnp.concatenate([packed[0][zl], packed[1][zl]], axis=1).astype(BF16)
-            for zh in range(2):
-                out_ref[x, :, zl, zh] = both[zh * 4 : (zh + 1) * 4]
+    packed = []
+    for part in parts:
+        cols = part.reshape(8, 4, 8, 128)
+        g = [cols[:, k] for k in range(4)]
+        for a, b in ((0, 2), (1, 3)):
+            g[a], g[b] = (
+                jnp.where(low, g[a], pltpu.roll(g[b], 64, 2)),
+                jnp.where(low, pltpu.roll(g[a], 64, 2), g[b]),
+            )
+        for a, b in ((0, 1), (2, 3)):
+            g[a], g[b] = (
+                jnp.where(even, g[a], pltpu.roll(g[b], 32, 2)),
+                jnp.where(even, pltpu.roll(g[a], 96, 2), g[b]),
+            )
+        packed.append(g)
+    for zl in range(4):
+        both = jnp.concatenate([packed[0][zl], packed[1][zl]], axis=1).astype(BF16)
+        for zh in range(2):
+            out_ref[x, :, zl, zh] = both[zh * 4 : (zh + 1) * 4]
 
 
 def sum_kernel(parts_ref, out_ref):

time: 84.4 us -> 84.4 us (level)
  no operation moved by 1% of the time
where the time goes in v10:
time: 84.4 us; the launch traced here: 84.1 us
  blocking collectives  77.2 us (91%)
  Pallas kernels  3.13 us (4%)
  waiting for transfers between devices  2.66 us (3%)
  local copies, waits for them, and re-layouts  1.05 us (1%)
    all_to_all x4, blocking collectives, exchange(): return lax.all_to_all(x, axes, 0, 0, tiled=True)  77.2 us
    pallas_call x5, Pallas kernels, call(): pl.pallas_call(kernel, out_shape=jax.ShapeDtypeStruct(shape, dtype), in_s...  3.13 us
    ppermute x1, waiting for transfers between devices, shards(): other = lax.ppermute(mine, 'core', [(0, 1), (1, 0)])  2.66 us
  transfers between devices with their start and end apart: 1, of which 1 were waited for; matrix products, arithmetic and copies ran while one was open for 0% of the time, Pallas kernels for 0%

profile of v10, /device:TPU:8, one launch (start us, length us, event | category | flops | bytes accessed | tf_op | source)
XLA Modules:
  0.0 84.1 jit_solution(5450203243692582268)
XLA Ops:
  0.0 0.0 copy-start
  0.0 1.0 %copy-done = bf16[4,2,2,32,512]{4,3,2,1,0:T(8,128)(2,1)S(1)} copy-done((bf16[4,2,2,32,512]{4,3,2,1,0:T(8,128)(2,1)S(1)}, bf16[4,2,2,32,512]{4,3,2,1,0:T(8,128)(2,1)}, u32[]{:S(2)}) %copy-start) | copy-done | bytes 524312
  1.0 0.2 shard_map.28
  1.2 0.0 copy-start.1
  1.2 29.1 %all_to_all.20 = bf16[32,2,2,16,128]{4,3,2,1,0:T(8,128)(2,1)S(1)} all-to-all(bf16[32,2,2,16,128]{4,3,2,1,0:T(8,128)(2,1)S(1)} %bitcast.8), channel_id=1, replica_groups=mesh['x'=4,'za'=2,'zb'=2,'zh'=2,'y'=4,'core'=2] {'zb','zh','x','za'}, dimensions={0} | all-to-all | bytes 1048576 | tf_op jit(solution)/shard_map/all_to_all | solution.py:176
  30.3 0.0 copy-done.1
  30.3 0.6 shard_map.29
  30.9 20.1 %all_to_all.21 = bf16[32,2,2,2,16,128]{5,4,3,2,1,0:T(8,128)(2,1)S(1)} all-to-all(bf16[32,2,2,2,16,128]{5,4,3,2,1,0:T(8,128)(2,1)S(1)} %shard_map.29), channel_id=1, replica_groups=mesh['x'=4,'za'=2,'zb'=2,'zh'=2,'y'=4,'core'=2] {'y','zb','x'}, dimensions={0} | all-to-all | bytes 2097152 | tf_op jit(solution)/shard_map/all_to_all | solution.py:176
  51.0 0.0 collective-permute-start
  51.0 2.7 %collective-permute-done.other_ref = bf16[4,2,4,2,2,2,16,128]{7,6,5,4,3,2,1,0:T(8,128)(2,1)S(1)} collective-permute-done((bf16[4,2,4,2,2,2,16,128]{7,6,5,4,3,2,1,0:T(8,128)(2,1)S(1)}, bf16[4,2,4,2,2,2,16,128]{7,6,5,4,3,2,1,0:T(8,128)(2,1)S(1)}, u32[]{:S(2)}, u32[]{:S(2)}) %collective-permute-start) | collective-permute-done | bytes 1048608 | tf_op jit(solution)/shard_map/ppermute | solution.py:199
  53.6 1.6 %shard_map.30 = bf16[4,4,4,2,16,128]{5,4,3,2,1,0:T(8,128)(2,1)S(1)} custom-call(bf16[4,2,4,2,2,2,16,128]{7,6,5,4,3,2,1,0:T(8,128)(2,1)S(1)} %bitcast.10, bf16[4,2,4,2,2,2,16,128]{7,6,5,4,3,2,1,0:T(8,128)(2,1)S(1)} %collective-permute-done.other_ref), custom_call_target="tpu_custom_call" | custom-call | flops 1073741824 | bytes 2621440 | tf_op jit(solution)/shard_map/pallas_call | solution.py:164
  55.2 15.8 %all_to_all.22.parts_ref = bf16[16,4,2,16,128]{4,3,2,1,0:T(8,128)(2,1)S(1)} all-to-all(bf16[16,4,2,16,128]{4,3,2,1,0:T(8,128)(2,1)S(1)} %bitcast.12), channel_id=1, replica_groups=mesh['x'=4,'za'=2,'zb'=2,'zh'=2,'y'=4,'core'=2] {'x','y'}, dimensions={0} | all-to-all | bytes 1048576 | tf_op jit(solution)/shard_map/all_to_all | solution.py:176
  71.1 0.1 shard_map.31
  71.1 12.2 %all_to_all.23 = f32[8,16,128]{2,1,0:T(8,128)S(1)} all-to-all(f32[8,16,128]{2,1,0:T(8,128)S(1)} %bitcast.13), channel_id=1, replica_groups=mesh['x'=4,'za'=2,'zb'=2,'zh'=2,'y'=4,'core'=2] {'zh','za','zb'}, dimensions={0} | all-to-all | bytes 131072 | tf_op jit(solution)/shard_map/all_to_all | solution.py:176
  83.3 0.7 shard_map.32
Async XLA Ops:
  0.0 1.0 %copy-start = (bf16[4,2,2,32,512]{4,3,2,1,0:T(8,128)(2,1)S(1)}, bf16[4,2,2,32,512]{4,3,2,1,0:T(8,128)(2,1)}, u32[]{:S(2)}) copy-start(bf16[4,2,2,32,512]{4,3,2,1,0:T(8,128)(2,1)} %param.2) | copy-start | bytes 1572868
  1.2 29.1 %copy-start.1 = (f32[4,512]{1,0:T(4,128)S(1)}, f32[4,512]{1,0:T(4,128)}, u32[]{:S(2)}) copy-start(f32[4,512]{1,0:T(4,128)} %vert_ref.1) | copy-start | bytes 24580
  51.0 2.7 %collective-permute-start = (bf16[4,2,4,2,2,2,16,128]{7,6,5,4,3,2,1,0:T(8,128)(2,1)S(1)}, bf16[4,2,4,2,2,2,16,128]{7,6,5,4,3,2,1,0:T(8,128)(2,1)S(1)}, u32[]{:S(2)}, u32[]{:S(2)}) collective-permute-start(bf16[4,2,4,2,2,2,16,128]{7,6,5,4,3,2,1,0:T(8,128)(2,1)S(1)} %bitcast.9), channel_id=1, source_target_pairs={{0,1},{1,0},{2,3},{3,2},{4,5},{5,4},{6,7},{7,6},{8,9},{9,8},{10,11... | collective-permute-start | bytes 3145736 | tf_op jit(solution)/shard_map/ppermute | solution.py:199

commit v11 on v10

v11 whole, which is shorter than its diff:
```python
import jax
import jax.numpy as jnp
from jax import lax
from jax.experimental import pallas as pl
from jax.experimental.pallas import tpu as pltpu
from jax.sharding import Mesh, PartitionSpec as P

NAMES = ("xh", "xl", "za", "zb", "zh", "y", "core")
SIZES = (2, 2, 2, 2, 2, 4, 2)
NZ = 32
BF16, F32 = jnp.bfloat16, jnp.float32


def half_of(xl):
    return lax.rem(xl + lax.axis_index("xh"), 2)


def split_kernel(rec_ref, out_ref, sems):
    copies = [
        pltpu.make_async_copy(
            rec_ref.at[
                :, :, :, :, pl.ds(zb * 16, 16), pl.ds(pl.multiple_of(half_of(xl) * 256, 256), 256)
            ],
            out_ref.at[zb, :, xl],
            sems.at[zb * 2 + xl],
        )
        for zb in range(2)
        for xl in range(2)
    ]
    for copy in copies:
        copy.start()
    for copy in copies:
        copy.wait()


def phases(vert_ref):
    w = lax.axis_index("zh") * 2 + lax.axis_index("za")
    first_col = half_of(lax.axis_index("xl")) * 256
    first_row = (
        lax.axis_index("y") * 2 + lax.axis_index("core")
    ) * 32 + lax.axis_index("zb") * 16

    def of_frequency(rows):
        picked = lax.broadcasted_iota(jnp.int32, rows.shape, 0) == w
        return jnp.sum(jnp.where(picked, rows, 0.0), axis=0, keepdims=True)

    waves = of_frequency(vert_ref[...])
    row = lax.broadcasted_iota(jnp.int32, (32, 512), 0)
    lane = lax.broadcasted_iota(jnp.int32, (32, 512), 1)
    mine = lane == (row % 16) + (row // 16) * 256 + first_row
    row_wave = jnp.sum(jnp.where(mine, waves, 0.0), axis=1, keepdims=True)
    return row_wave + of_frequency(vert_ref[:, pl.ds(pl.multiple_of(first_col, 256), 256)])


def sections(rec_ref, phase_ref, b, visit):
    cols = slice(b * 128, (b + 1) * 128)
    step_re, step_im, c, s = [phase_ref[k, :, cols] for k in range(4)]
    for z in range(15, -1, -1):
        xl, za, zb, j = z // 8, z // 4 % 2, z // 2 % 2, z % 2
        re, im = [
            rec_ref[zb, :, xl, za, j, p, :, cols].reshape(32, 128).astype(F32) for p in range(2)
        ]
        visit(z, cols, re * c, re * s, im * c, im * s)
        c, s = c * step_re + s * step_im, s * step_re - c * step_im


def block_kernel(rec_ref, vert_ref, phase_ref, sum_ref):
    angle = phases(vert_ref)
    last = angle * (lax.axis_index("xh") * 16 + 15).astype(F32)
    phase_ref[0], phase_ref[1] = jnp.cos(angle), jnp.sin(angle)
    phase_ref[2], phase_ref[3] = jnp.cos(last) * (1.0 / NZ), jnp.sin(last) * (1.0 / NZ)
    for b in range(2):
        total = [jnp.zeros((32, 128), F32)] * 2

        def visit(z, cols, rc, rs, ic, is_):
            total[0] = total[0] + (rc - is_)
            total[1] = total[1] + (rs + ic)

        sections(rec_ref, phase_ref, b, visit)
        for part in range(2):
            sum_ref[part, :, b * 128 : (b + 1) * 128] = total[part].astype(BF16)


def scan_kernel(rec_ref, phase_ref, deeper_ref, out_ref):
    for b in range(2):
        tail = [deeper_ref[part, :, b * 128 : (b + 1) * 128].astype(F32) for part in range(2)]

        def visit(z, cols, rc, rs, ic, is_):
            values = (tail, (rc + is_, ic - rs))
            for kind in range(2):
                for part in range(2):
                    out_ref[z, kind, part, :, :, cols] = (
                        values[kind][part].astype(BF16).reshape(2, 16, 128)
                    )
            tail[0] = tail[0] + (rc - is_)
            tail[1] = tail[1] + (rs + ic)

        sections(rec_ref, phase_ref, b, visit)


def unit_kernel(mine_ref, other_ref, out_ref):
    h = lax.axis_index("core")

    @pl.when(h == 0)
    def _():
        unit(mine_ref, (mine_ref, other_ref), out_ref)

    @pl.when(h == 1)
    def _():
        unit(mine_ref, (other_ref, mine_ref), out_ref)


def unit(mine, cores, out_ref):
    def matrix(kind, part, refs, half):
        xl = half_of(half)
        return jnp.concatenate(
            [
                ref[y, row_half, xl, kind, part, zh]
                for zh in range(2)
                for y in range(4)
                for ref in refs
                for row_half in range(2)
            ],
            axis=0,
        )

    def product(left, kind, half):
        by_re, by_im = [
            jnp.dot(left, matrix(kind, part, cores, half), preferred_element_type=F32)
            for part in range(2)
        ]
        return by_re[:256] - by_im[256:], by_im[:256] + by_re[256:]

    left = jnp.concatenate(
        [
            jnp.concatenate([matrix(0, part, (mine,), half) for half in range(2)], axis=1)
            for part in range(2)
        ],
        axis=0,
    )
    mid = jnp.concatenate(
        [jnp.concatenate(product(left, 1, half), axis=0).astype(BF16) for half in range(2)],
        axis=1,
    )
    for half in range(2):
        parts = product(mid, 0, half)
        for k in range(2):
            pack([part[:, k * 128 : (k + 1) * 128] for part in parts], half * 2 + k, out_ref)


def pack(parts, x, out_ref):
    lane = lax.broadcasted_iota(jnp.int32, (8, 8, 128), 2)
    low, even = lane < 64, (lane // 32) % 2 == 0
    packed = []
    for part in parts:
        cols = part.reshape(8, 4, 8, 128)
        g = [cols[:, k] for k in range(4)]
        for a, b in ((0, 2), (1, 3)):
            g[a], g[b] = (
                jnp.where(low, g[a], pltpu.roll(g[b], 64, 2)),
                jnp.where(low, pltpu.roll(g[a], 64, 2), g[b]),
            )
        for a, b in ((0, 1), (2, 3)):
            g[a], g[b] = (
                jnp.where(even, g[a], pltpu.roll(g[b], 32, 2)),
                jnp.where(even, pltpu.roll(g[a], 96, 2), g[b]),
            )
        packed.append(g)
    for zl in range(4):
        both = jnp.concatenate([packed[0][zl], packed[1][zl]], axis=1).astype(BF16)
        for zh in range(2):
            out_ref[x, :, zl, zh] = both[zh * 4 : (zh + 1) * 4]


def sum_kernel(parts_ref, out_ref):
    for zl in range(4):
        for zh in range(2):
            out_ref[zh, zl] = jnp.sum(parts_ref[:, zl, zh].astype(F32), axis=0)


def last_kernel(parts_ref, out_ref):
    for w in range(4):
        total = parts_ref[w, 0] + parts_ref[w, 1]
        for part in range(2):
            for g in range(4):
                out_ref[w, part, g * 8 : (g + 1) * 8, :] = total[
                    part * 8 : (part + 1) * 8, g * 32 : (g + 1) * 32
                ]


def vmem(n):
    return [pl.BlockSpec(memory_space=pltpu.VMEM)] * n


def call(kernel, shapes, args, in_specs=None, scratch=(), limit=16, flops=0, moved=0):
    outs = [jax.ShapeDtypeStruct(shape, dtype) for shape, dtype in shapes]
    specs = vmem(len(outs))
    return pl.pallas_call(
        kernel,
        out_shape=outs if len(outs) > 1 else outs[0],
        in_specs=in_specs or vmem(len(args)),
        out_specs=specs if len(outs) > 1 else specs[0],
        scratch_shapes=list(scratch),
        compiler_params=pltpu.CompilerParams(vmem_limit_bytes=limit << 20),
        cost_estimate=pl.CostEstimate(flops=flops, bytes_accessed=moved, transcendentals=0),
    )(*args)


def exchange(x, axes):
    return lax.all_to_all(x, axes, 0, 0, tiled=True)


def shards(recorded, vertical):
    blocks = call(
        split_kernel,
        [((2, 2, 2, 2, 2, 2, 16, 256), BF16)],
        (recorded.reshape(2, 2, 2, 2, 32, 512),),
        in_specs=[pl.BlockSpec(memory_space=pl.ANY)],
        scratch=[pltpu.SemaphoreType.DMA((4,))],
        moved=1 << 20,
    )
    rec = exchange(blocks.reshape(16, 2, 2, 16, 256), ("zb", "zh", "xl", "za"))
    rec = rec.reshape(2, 2, 2, 2, 2, 2, 16, 256)
    phase, block_sum = call(
        block_kernel,
        [((4, 32, 256), F32), ((2, 32, 256), BF16)],
        (rec, vertical),
        moved=1 << 20,
    )
    deeper = lax.ppermute(block_sum, ("xh", "xl"), [(3, 0), (2, 1)])
    phased = call(
        scan_kernel,
        [((16, 2, 2, 2, 16, 256), BF16)],
        (rec, phase, deeper),
        moved=3 << 19,
    )
    mine = exchange(phased, ("y", "zb", "xl")).reshape(4, 2, 2, 2, 2, 2, 16, 256)
    other = lax.ppermute(mine, "core", [(0, 1), (1, 0)])
    partial = call(
        unit_kernel,
        [((4, 4, 4, 2, 16, 128), BF16)],
        (mine, other),
        limit=40,
        flops=1 << 30,
        moved=5 << 19,
    )
    parts = exchange(partial.reshape(16, 4, 2, 16, 128), ("xh", "xl", "y"))
    summed = call(sum_kernel, [((2, 4, 16, 128), F32)], (parts,), moved=1 << 19)
    last = exchange(summed.reshape(8, 16, 128), ("zh", "za", "zb"))
    return call(last_kernel, [((4, 2, 32, 32), F32)], (last.reshape(4, 2, 16, 128),))


def solution(mesh):
    chips = Mesh(mesh.devices.reshape(SIZES), NAMES)
    depth, col = ("xh", "xl", "za", "zb"), ("zh", "y", "core")
    return jax.shard_map(
        shards,
        mesh=chips,
        in_specs=(P(None, depth, None, col, None), P()),
        out_specs=P(None, None, col, depth),
        check_vma=False,
    )
```

time: 84.4 us -> 84.9 us (level)
  blocking collectives: 77.2 us -> 70.4 us
  waiting for transfers between devices: 2.66 us -> 8.38 us
  starting transfers between devices: 0.01 us -> 1.29 us
    all_to_all x4, blocking collectives: 77.2 us -> 70.4 us  [exchange(): return lax.all_to_all(x, axes, 0, 0, tiled=True)]
    ppermute x0 -> x1, waiting for transfers between devices: none -> 5.72 us  [shards(): deeper = lax.ppermute(block_sum, ('xh', 'xl'), [(3, 0), (2, 1)])]
    ppermute x0 -> x1, starting transfers between devices: none -> 1.29 us  [shards(): deeper = lax.ppermute(block_sum, ('xh', 'xl'), [(3, 0), (2, 1)])]
    pallas_call x5 -> x6, Pallas kernels: 3.13 us -> 3.44 us  [call(): pl.pallas_call(kernel, out_shape=outs if len(outs) > 1 else outs[0], in_s...]
  transfers between devices with their start and end apart: 1 -> 2, of which waited for: 1 -> 2; matrix products, arithmetic and copies ran while one was open for 0% -> 0% of each run, Pallas kernels for 0% -> 0%
where the time goes in v11:
time: 84.9 us; the launch traced here: 84.6 us
  blocking collectives  70.4 us (83%)
  waiting for transfers between devices  8.38 us (10%)
  Pallas kernels  3.44 us (4%)
  starting transfers between devices  1.29 us (2%)
  local copies, waits for them, and re-layouts  1.05 us (1%)
    all_to_all x4, blocking collectives, exchange(): return lax.all_to_all(x, axes, 0, 0, tiled=True)  70.4 us
    ppermute x1, waiting for transfers between devices, shards(): deeper = lax.ppermute(block_sum, ('xh', 'xl'), [(3, 0), (2, 1)])  5.72 us
    pallas_call x6, Pallas kernels, call(): pl.pallas_call(kernel, out_shape=outs if len(outs) > 1 else outs[0], in_s...  3.44 us
    ppermute x1, waiting for transfers between devices, shards(): other = lax.ppermute(mine, 'core', [(0, 1), (1, 0)])  2.66 us
  transfers between devices with their start and end apart: 2, of which 2 were waited for; matrix products, arithmetic and copies ran while one was open for 0% of the time, Pallas kernels for 0%

profile of v11, /device:TPU:8, one launch (start us, length us, event | category | flops | bytes accessed | tf_op | source)
XLA Modules:
  0.0 84.6 jit_solution(4781562625823005525)
XLA Ops:
  0.0 0.0 copy-start
  0.0 1.0 %copy-done = bf16[4,2,2,32,512]{4,3,2,1,0:T(8,128)(2,1)S(1)} copy-done((bf16[4,2,2,32,512]{4,3,2,1,0:T(8,128)(2,1)S(1)}, bf16[4,2,2,32,512]{4,3,2,1,0:T(8,128)(2,1)}, u32[]{:S(2)}) %copy-start) | copy-done | bytes 524312
  1.0 0.1 shard_map.28
  1.1 0.0 copy-start.1
  1.1 24.7 %all_to_all.20 = bf16[16,2,2,16,256]{4,3,2,1,0:T(8,128)(2,1)S(1)} all-to-all(bf16[16,2,2,16,256]{4,3,2,1,0:T(8,128)(2,1)S(1)} %bitcast.9), channel_id=1, replica_groups=mesh['xh'=2,'xl'=2,'za'=2,'zb'=2,'zh'=2,'y'=4,'core'=2] {'zb','zh','xl',..., dimensions={0} | all-to-all | bytes 1048576 | tf_op jit(solution)/shard_map/all_to_all | solution.py:210
  25.9 0.0 copy-done.1
  25.9 0.6 shard_map.29
  26.5 1.3 %collective-permute-start = (bf16[2,32,256]{2,1,0:T(8,128)(2,1)S(1)}, bf16[2,32,256]{2,1,0:T(8,128)(2,1)S(1)}, u32[]{:S(2)}, u32[]{:S(2)}) collective-permute-start(bf16[2,32,256]{2,1,0:T(8,128)(2,1)S(1)} %get-tuple-element.8), channel_id=1, source_target_pairs={{192,0},{128,64},{193,1},{129,65},{194,2},{130,66},{195,3},{131,67... | collective-permute-start | bytes 98312 | tf_op jit(solution)/shard_map/ppermute | solution.py:230
  27.8 5.7 %collective-permute-done.deeper_ref = bf16[2,32,256]{2,1,0:T(8,128)(2,1)S(1)} collective-permute-done((bf16[2,32,256]{2,1,0:T(8,128)(2,1)S(1)}, bf16[2,32,256]{2,1,0:T(8,128)(2,1)S(1)}, u32[]{:S(2)}, u32[]{:S(2)}) %collective-permute-start) | collective-permute-done | bytes 32800 | tf_op jit(solution)/shard_map/ppermute | solution.py:230
  33.5 0.4 shard_map.30
  33.9 17.4 %all_to_all.21 = bf16[16,2,2,2,16,256]{5,4,3,2,1,0:T(8,128)(2,1)S(1)} all-to-all(bf16[16,2,2,2,16,256]{5,4,3,2,1,0:T(8,128)(2,1)S(1)} %shard_map.30), channel_id=1, replica_groups=mesh['xh'=2,'xl'=2,'za'=2,'zb'=2,'zh'=2,'y'=4,'core'=2] {'y','zb','xl'}, dimensions={0} | all-to-all | bytes 2097152 | tf_op jit(solution)/shard_map/all_to_all | solution.py:210
  51.3 0.0 collective-permute-start.1
  51.3 2.7 %collective-permute-done.1.other_ref = bf16[4,2,2,2,2,2,16,256]{7,6,5,4,3,2,1,0:T(8,128)(2,1)S(1)} collective-permute-done((bf16[4,2,2,2,2,2,16,256]{7,6,5,4,3,2,1,0:T(8,128)(2,1)S(1)}, bf16[4,2,2,2,2,2,16,256]{7,6,5,4,3,2,1,0:T(8,128)(2,1)S(1)}, u32[]{:S(2)}, u32[]{:S(2)}) %collective-permute-start.1) | collective-permute-done | bytes 1048608 | tf_op jit(solution)/shard_map/ppermute | solution.py:238
  54.0 1.6 %shard_map.31 = bf16[4,4,4,2,16,128]{5,4,3,2,1,0:T(8,128)(2,1)S(1)} custom-call(bf16[4,2,2,2,2,2,16,256]{7,6,5,4,3,2,1,0:T(8,128)(2,1)S(1)} %bitcast.11, bf16[4,2,2,2,2,2,16,256]{7,6,5,4,3,2,1,0:T(8,128)(2,1)S(1)} %collective-permute-done.1.other_ref), custom_call_target="tpu_custom_call" | custom-call | flops 1073741824 | bytes 2621440 | tf_op jit(solution)/shard_map/pallas_call | solution.py:198
  55.5 14.8 %all_to_all.22.parts_ref = bf16[16,4,2,16,128]{4,3,2,1,0:T(8,128)(2,1)S(1)} all-to-all(bf16[16,4,2,16,128]{4,3,2,1,0:T(8,128)(2,1)S(1)} %bitcast.13), channel_id=1, replica_groups=mesh['xh'=2,'xl'=2,'za'=2,'zb'=2,'zh'=2,'y'=4,'core'=2] {'xh','xl','y'}, dimensions={0} | all-to-all | bytes 1048576 | tf_op jit(solution)/shard_map/all_to_all | solution.py:210
  70.3 0.1 shard_map.32
  70.4 13.5 %all_to_all.23 = f32[8,16,128]{2,1,0:T(8,128)S(1)} all-to-all(f32[8,16,128]{2,1,0:T(8,128)S(1)} %bitcast.14), channel_id=1, replica_groups=mesh['xh'=2,'xl'=2,'za'=2,'zb'=2,'zh'=2,'y'=4,'core'=2] {'zh','za','zb'}, dimensions={0} | all-to-all | bytes 131072 | tf_op jit(solution)/shard_map/all_to_all | solution.py:210
  83.9 0.7 shard_map.33
Async XLA Ops:
  0.0 1.0 %copy-start = (bf16[4,2,2,32,512]{4,3,2,1,0:T(8,128)(2,1)S(1)}, bf16[4,2,2,32,512]{4,3,2,1,0:T(8,128)(2,1)}, u32[]{:S(2)}) copy-start(bf16[4,2,2,32,512]{4,3,2,1,0:T(8,128)(2,1)} %param.2) | copy-start | bytes 1572868
  1.1 24.8 %copy-start.1 = (f32[4,512]{1,0:T(4,128)S(1)}, f32[4,512]{1,0:T(4,128)}, u32[]{:S(2)}) copy-start(f32[4,512]{1,0:T(4,128)} %vert_ref.1) | copy-start | bytes 24580
  26.5 7.0 %collective-permute-start = (bf16[2,32,256]{2,1,0:T(8,128)(2,1)S(1)}, bf16[2,32,256]{2,1,0:T(8,128)(2,1)S(1)}, u32[]{:S(2)}, u32[]{:S(2)}) collective-permute-start(bf16[2,32,256]{2,1,0:T(8,128)(2,1)S(1)} %get-tuple-element.8), channel_id=1, source_target_pairs={{192,0},{128,64},{193,1},{129,65},{194,2},{130,66},{195,3},{131,67... | collective-permute-start | bytes 98312 | tf_op jit(solution)/shard_map/ppermute | solution.py:230
  51.3 2.7 %collective-permute-start.1 = (bf16[4,2,2,2,2,2,16,256]{7,6,5,4,3,2,1,0:T(8,128)(2,1)S(1)}, bf16[4,2,2,2,2,2,16,256]{7,6,5,4,3,2,1,0:T(8,128)(2,1)S(1)}, u32[]{:S(2)}, u32[]{:S(2)}) collective-permute-start(bf16[4,2,2,2,2,2,16,256]{7,6,5,4,3,2,1,0:T(8,128)(2,1)S(1)} %bitcast.10), channel_id=1, source_target_pairs={{0,1},{1,0},{2,3},{3,2},{4,5},{5,4},{6,7},{7,6},{8,9},{9,8},{10,11... | collective-permute-start | bytes 3145736 | tf_op jit(solution)/shard_map/ppermute | solution.py:238

commit v12 on v10

--- a/solution.py
+++ b/solution.py
@@ -64,16 +64,18 @@
         c, s = c * step_re + s * step_im, s * step_re - c * step_im
 
 
-def unit_kernel(mine_ref, other_ref, out_ref):
+def unit_kernel(mine_ref, low_ref, high_ref, out_ref):
     h = lax.axis_index("core")
+    mine = [mine_ref.at[y] for y in range(4)]
+    other = [ref.at[y] for ref in (low_ref, high_ref) for y in range(2)]
 
     @pl.when(h == 0)
     def _():
-        unit(mine_ref, (mine_ref, other_ref), out_ref)
+        unit(mine, (mine, other), out_ref)
 
     @pl.when(h == 1)
     def _():
-        unit(mine_ref, (other_ref, mine_ref), out_ref)
+        unit(mine, (other, mine), out_ref)
 
 
 def unit(mine, cores, out_ref):
@@ -82,7 +84,7 @@
             [
                 jnp.concatenate(
                     [
-                        ref[y, half, b, kind, part, zh]
+                        ref[y][half, b, kind, part, zh]
                         for zh in range(2)
                         for y in range(4)
                         for ref in refs
@@ -196,13 +198,13 @@
         moved=3 << 19,
     )
     mine = exchange(phased, ("y", "zb", "x")).reshape(4, 2, 4, 2, 2, 2, 16, 128)
-    other = lax.ppermute(mine, "core", [(0, 1), (1, 0)])
+    low, high = [lax.ppermute(rows, "core", [(0, 1), (1, 0)]) for rows in (mine[:2], mine[2:])]
     partial = call(
         unit_kernel,
         (4, 4, 4, 2, 16, 128),
         BF16,
-        vmem(2),
-        (mine, other),
+        vmem(3),
+        (mine, low, high),
         limit=40,
         flops=1 << 30,
         moved=5 << 19,

time: 84.4 us -> 84.6 us (level)
    ppermute x1 -> x2, waiting for transfers between devices: 2.66 us -> 2.15 us  [shards(): lax.ppermute(rows, 'core', [(0, 1), (1, 0)])]
  transfers between devices with their start and end apart: 1 -> 2, of which waited for: 1 -> 2; matrix products, arithmetic and copies ran while one was open for 0% -> 0% of each run, Pallas kernels for 0% -> 0%
where the time goes in v12:
time: 84.6 us; the launch traced here: 84.3 us
  blocking collectives  77.2 us (91%)
  Pallas kernels  3.13 us (4%)
  waiting for transfers between devices  2.15 us (3%)
  local copies, waits for them, and re-layouts  1.24 us (1%)
    all_to_all x4, blocking collectives, exchange(): return lax.all_to_all(x, axes, 0, 0, tiled=True)  77.2 us
    pallas_call x5, Pallas kernels, call(): pl.pallas_call(kernel, out_shape=jax.ShapeDtypeStruct(shape, dtype), in_s...  3.13 us
    ppermute x2, waiting for transfers between devices, shards(): lax.ppermute(rows, 'core', [(0, 1), (1, 0)])  2.15 us
  transfers between devices with their start and end apart: 2, of which 2 were waited for; matrix products, arithmetic and copies ran while one was open for 0% of the time, Pallas kernels for 0%

profile of v12, /device:TPU:8, one launch (start us, length us, event | category | flops | bytes accessed | tf_op | source)
XLA Modules:
  0.0 84.3 jit_solution(14739387667883979979)
XLA Ops:
  0.0 0.0 copy-start
  0.0 1.0 %copy-done = bf16[4,2,2,32,512]{4,3,2,1,0:T(8,128)(2,1)S(1)} copy-done((bf16[4,2,2,32,512]{4,3,2,1,0:T(8,128)(2,1)S(1)}, bf16[4,2,2,32,512]{4,3,2,1,0:T(8,128)(2,1)}, u32[]{:S(2)}) %copy-start) | copy-done | bytes 524312
  1.0 0.2 shard_map.28
  1.2 0.0 copy-start.1
  1.2 29.1 %all_to_all.20 = bf16[32,2,2,16,128]{4,3,2,1,0:T(8,128)(2,1)S(1)} all-to-all(bf16[32,2,2,16,128]{4,3,2,1,0:T(8,128)(2,1)S(1)} %bitcast.11), channel_id=1, replica_groups=mesh['x'=4,'za'=2,'zb'=2,'zh'=2,'y'=4,'core'=2] {'zb','zh','x','za'}, dimensions={0} | all-to-all | bytes 1048576 | tf_op jit(solution)/shard_map/all_to_all | solution.py:178
  30.3 0.0 copy-done.1
  30.3 0.6 shard_map.29
  30.9 20.1 %all_to_all.21 = bf16[32,2,2,2,16,128]{5,4,3,2,1,0:T(8,128)(2,1)S(1)} all-to-all(bf16[32,2,2,2,16,128]{5,4,3,2,1,0:T(8,128)(2,1)S(1)} %shard_map.29), channel_id=1, replica_groups=mesh['x'=4,'za'=2,'zb'=2,'zh'=2,'y'=4,'core'=2] {'y','zb','x'}, dimensions={0} | all-to-all | bytes 2097152 | tf_op jit(solution)/shard_map/all_to_all | solution.py:178
  51.0 0.2 fusion
  51.2 0.1 collective-permute-start
  51.3 0.5 collective-permute-start.1
  51.8 1.4 %collective-permute-done.low_ref = bf16[2,2,4,2,2,2,16,128]{7,6,5,4,3,2,1,0:T(8,128)(2,1)S(1)} collective-permute-done((bf16[2,2,4,2,2,2,16,128]{7,6,5,4,3,2,1,0:T(8,128)(2,1)S(1)}, bf16[2,2,4,2,2,2,16,128]{7,6,5,4,3,2,1,0:T(8,128)(2,1)S(1)}, u32[]{:S(2)}, u32[]{:S(2)}) %collective-permute-start) | collective-permute-done | bytes 524320 | tf_op jit(solution)/shard_map/ppermute | solution.py:201
  53.2 0.7 collective-permute-done.1.high_ref
  53.9 1.6 %shard_map.30 = bf16[4,4,4,2,16,128]{5,4,3,2,1,0:T(8,128)(2,1)S(1)} custom-call(bf16[4,2,4,2,2,2,16,128]{7,6,5,4,3,2,1,0:T(8,128)(2,1)S(1)} %bitcast.9, bf16[2,2,4,2,2,2,16,128]{7,6,5,4,3,2,1,0:T(8,128)(2,1)S(1)} %collective-permute-done.low_ref, bf16[2,2,4,2,2,2,16,128]{7,6,5,4,3,2,1,0:T(8,128)(2,1)S(1)} %collective-permute-done.1.high_ref), custom_call_target="tpu_custom_call" | custom-call | flops 1073741824 | bytes 2621440 | tf_op jit(solution)/shard_map/pallas_call | solution.py:166
  55.5 15.8 %all_to_all.22.parts_ref = bf16[16,4,2,16,128]{4,3,2,1,0:T(8,128)(2,1)S(1)} all-to-all(bf16[16,4,2,16,128]{4,3,2,1,0:T(8,128)(2,1)S(1)} %bitcast.13), channel_id=1, replica_groups=mesh['x'=4,'za'=2,'zb'=2,'zh'=2,'y'=4,'core'=2] {'x','y'}, dimensions={0} | all-to-all | bytes 1048576 | tf_op jit(solution)/shard_map/all_to_all | solution.py:178
  71.3 0.1 shard_map.31
  71.4 12.2 %all_to_all.23 = f32[8,16,128]{2,1,0:T(8,128)S(1)} all-to-all(f32[8,16,128]{2,1,0:T(8,128)S(1)} %bitcast.14), channel_id=1, replica_groups=mesh['x'=4,'za'=2,'zb'=2,'zh'=2,'y'=4,'core'=2] {'zh','za','zb'}, dimensions={0} | all-to-all | bytes 131072 | tf_op jit(solution)/shard_map/all_to_all | solution.py:178
  83.6 0.7 shard_map.32
Async XLA Ops:
  0.0 1.0 %copy-start = (bf16[4,2,2,32,512]{4,3,2,1,0:T(8,128)(2,1)S(1)}, bf16[4,2,2,32,512]{4,3,2,1,0:T(8,128)(2,1)}, u32[]{:S(2)}) copy-start(bf16[4,2,2,32,512]{4,3,2,1,0:T(8,128)(2,1)} %param.2) | copy-start | bytes 1572868
  1.2 29.1 %copy-start.1 = (f32[4,512]{1,0:T(4,128)S(1)}, f32[4,512]{1,0:T(4,128)}, u32[]{:S(2)}) copy-start(f32[4,512]{1,0:T(4,128)} %vert_ref.1) | copy-start | bytes 24580
  51.2 2.0 %collective-permute-start = (bf16[2,2,4,2,2,2,16,128]{7,6,5,4,3,2,1,0:T(8,128)(2,1)S(1)}, bf16[2,2,4,2,2,2,16,128]{7,6,5,4,3,2,1,0:T(8,128)(2,1)S(1)}, u32[]{:S(2)}, u32[]{:S(2)}) collective-permute-start(bf16[2,2,4,2,2,2,16,128]{7,6,5,4,3,2,1,0:T(8,128)(2,1)S(1)} %bitcast.17), channel_id=1, source_target_pairs={{0,1},{1,0},{2,3},{3,2},{4,5},{5,4},{6,7},{7,6},{8,9},{9,8},{10,11... | collective-permute-start | bytes 1572872 | tf_op jit(solution)/shard_map/ppermute | solution.py:201
  51.3 2.6 %collective-permute-start.1 = (bf16[2,2,4,2,2,2,16,128]{7,6,5,4,3,2,1,0:T(8,128)(2,1)S(1)}, bf16[2,2,4,2,2,2,16,128]{7,6,5,4,3,2,1,0:T(8,128)(2,1)S(1)}, u32[]{:S(2)}, u32[]{:S(2)}) collective-permute-start(bf16[2,2,4,2,2,2,16,128]{7,6,5,4,3,2,1,0:T(8,128)(2,1)S(1)} %bitcast.16), channel_id=1, source_target_pairs={{0,1},{1,0},{2,3},{3,2},{4,5},{5,4},{6,7},{7,6},{8,9},{9,8},{10,11... | collective-permute-start | bytes 1572872 | tf_op jit(solution)/shard_map/ppermute | solution.py:201

commit v13 on v10

--- a/solution.py
+++ b/solution.py
@@ -46,9 +46,14 @@
     col_wave = of_frequency(vert_ref[:, pl.ds(pl.multiple_of(first_col, 128), 128)])
     angle = row_wave + col_wave
     step_re, step_im = jnp.cos(angle), jnp.sin(angle)
-    last = angle * float(NZ - 1)
-    scale = 1.0 / NZ
-    c, s = jnp.cos(last) * scale, jnp.sin(last) * scale
+    c, s = step_re * (1.0 / NZ), step_im * (1.0 / NZ)
+    power_re, power_im = step_re, step_im
+    for _ in range(4):
+        power_re, power_im = (
+            power_re * power_re - power_im * power_im,
+            2.0 * power_re * power_im,
+        )
+        c, s = c * power_re - s * power_im, s * power_re + c * power_im
     tail_re = jnp.zeros((32, 128), F32)
     tail_im = jnp.zeros((32, 128), F32)
     for z in range(NZ - 1, -1, -1):

time: 84.4 us -> 84.3 us (level)
  no operation moved by 1% of the time
where the time goes in v13:
time: 84.3 us; the launch traced here: 84 us
  blocking collectives  77.2 us (92%)
  Pallas kernels  3.09 us (4%)
  waiting for transfers between devices  2.66 us (3%)
  local copies, waits for them, and re-layouts  1.05 us (1%)
    all_to_all x4, blocking collectives, exchange(): return lax.all_to_all(x, axes, 0, 0, tiled=True)  77.2 us
    pallas_call x5, Pallas kernels, call(): pl.pallas_call(kernel, out_shape=jax.ShapeDtypeStruct(shape, dtype), in_s...  3.09 us
    ppermute x1, waiting for transfers between devices, shards(): other = lax.ppermute(mine, 'core', [(0, 1), (1, 0)])  2.66 us
  transfers between devices with their start and end apart: 1, of which 1 were waited for; matrix products, arithmetic and copies ran while one was open for 0% of the time, Pallas kernels for 0%

profile of v13, /device:TPU:8, one launch (start us, length us, event | category | flops | bytes accessed | tf_op | source)
XLA Modules:
  0.0 84.0 jit_solution(10857743442689692850)
XLA Ops:
  0.0 0.0 copy-start
  0.0 1.0 %copy-done = bf16[4,2,2,32,512]{4,3,2,1,0:T(8,128)(2,1)S(1)} copy-done((bf16[4,2,2,32,512]{4,3,2,1,0:T(8,128)(2,1)S(1)}, bf16[4,2,2,32,512]{4,3,2,1,0:T(8,128)(2,1)}, u32[]{:S(2)}) %copy-start) | copy-done | bytes 524312
  1.0 0.2 shard_map.28
  1.2 0.0 copy-start.1
  1.2 29.1 %all_to_all.20 = bf16[32,2,2,16,128]{4,3,2,1,0:T(8,128)(2,1)S(1)} all-to-all(bf16[32,2,2,16,128]{4,3,2,1,0:T(8,128)(2,1)S(1)} %bitcast.8), channel_id=1, replica_groups=mesh['x'=4,'za'=2,'zb'=2,'zh'=2,'y'=4,'core'=2] {'zb','zh','x','za'}, dimensions={0} | all-to-all | bytes 1048576 | tf_op jit(solution)/shard_map/all_to_all | solution.py:181
  30.3 0.0 copy-done.1
  30.3 0.5 shard_map.29
  30.8 20.1 %all_to_all.21 = bf16[32,2,2,2,16,128]{5,4,3,2,1,0:T(8,128)(2,1)S(1)} all-to-all(bf16[32,2,2,2,16,128]{5,4,3,2,1,0:T(8,128)(2,1)S(1)} %shard_map.29), channel_id=1, replica_groups=mesh['x'=4,'za'=2,'zb'=2,'zh'=2,'y'=4,'core'=2] {'y','zb','x'}, dimensions={0} | all-to-all | bytes 2097152 | tf_op jit(solution)/shard_map/all_to_all | solution.py:181
  50.9 0.0 collective-permute-start
  50.9 2.7 %collective-permute-done.other_ref = bf16[4,2,4,2,2,2,16,128]{7,6,5,4,3,2,1,0:T(8,128)(2,1)S(1)} collective-permute-done((bf16[4,2,4,2,2,2,16,128]{7,6,5,4,3,2,1,0:T(8,128)(2,1)S(1)}, bf16[4,2,4,2,2,2,16,128]{7,6,5,4,3,2,1,0:T(8,128)(2,1)S(1)}, u32[]{:S(2)}, u32[]{:S(2)}) %collective-permute-start) | collective-permute-done | bytes 1048608 | tf_op jit(solution)/shard_map/ppermute | solution.py:204
  53.6 1.6 %shard_map.30 = bf16[4,4,4,2,16,128]{5,4,3,2,1,0:T(8,128)(2,1)S(1)} custom-call(bf16[4,2,4,2,2,2,16,128]{7,6,5,4,3,2,1,0:T(8,128)(2,1)S(1)} %bitcast.10, bf16[4,2,4,2,2,2,16,128]{7,6,5,4,3,2,1,0:T(8,128)(2,1)S(1)} %collective-permute-done.other_ref), custom_call_target="tpu_custom_call" | custom-call | flops 1073741824 | bytes 2621440 | tf_op jit(solution)/shard_map/pallas_call | solution.py:169
  55.2 15.8 %all_to_all.22.parts_ref = bf16[16,4,2,16,128]{4,3,2,1,0:T(8,128)(2,1)S(1)} all-to-all(bf16[16,4,2,16,128]{4,3,2,1,0:T(8,128)(2,1)S(1)} %bitcast.12), channel_id=1, replica_groups=mesh['x'=4,'za'=2,'zb'=2,'zh'=2,'y'=4,'core'=2] {'x','y'}, dimensions={0} | all-to-all | bytes 1048576 | tf_op jit(solution)/shard_map/all_to_all | solution.py:181
  71.0 0.1 shard_map.31
  71.1 12.2 %all_to_all.23 = f32[8,16,128]{2,1,0:T(8,128)S(1)} all-to-all(f32[8,16,128]{2,1,0:T(8,128)S(1)} %bitcast.13), channel_id=1, replica_groups=mesh['x'=4,'za'=2,'zb'=2,'zh'=2,'y'=4,'core'=2] {'zh','za','zb'}, dimensions={0} | all-to-all | bytes 131072 | tf_op jit(solution)/shard_map/all_to_all | solution.py:181
  83.3 0.7 shard_map.32
Async XLA Ops:
  0.0 1.0 %copy-start = (bf16[4,2,2,32,512]{4,3,2,1,0:T(8,128)(2,1)S(1)}, bf16[4,2,2,32,512]{4,3,2,1,0:T(8,128)(2,1)}, u32[]{:S(2)}) copy-start(bf16[4,2,2,32,512]{4,3,2,1,0:T(8,128)(2,1)} %param.2) | copy-start | bytes 1572868
  1.2 29.1 %copy-start.1 = (f32[4,512]{1,0:T(4,128)S(1)}, f32[4,512]{1,0:T(4,128)}, u32[]{:S(2)}) copy-start(f32[4,512]{1,0:T(4,128)} %vert_ref.1) | copy-start | bytes 24580
  50.9 2.7 %collective-permute-start = (bf16[4,2,4,2,2,2,16,128]{7,6,5,4,3,2,1,0:T(8,128)(2,1)S(1)}, bf16[4,2,4,2,2,2,16,128]{7,6,5,4,3,2,1,0:T(8,128)(2,1)S(1)}, u32[]{:S(2)}, u32[]{:S(2)}) collective-permute-start(bf16[4,2,4,2,2,2,16,128]{7,6,5,4,3,2,1,0:T(8,128)(2,1)S(1)} %bitcast.9), channel_id=1, source_target_pairs={{0,1},{1,0},{2,3},{3,2},{4,5},{5,4},{6,7},{7,6},{8,9},{9,8},{10,11... | collective-permute-start | bytes 3145736 | tf_op jit(solution)/shard_map/ppermute | solution.py:204

commit v14 on v13

--- a/solution.py
+++ b/solution.py
@@ -151,26 +151,31 @@
             out_ref[zh, zl] = jnp.sum(parts_ref[:, zl, zh].astype(F32), axis=0)
 
 
-def last_kernel(parts_ref, out_ref):
+def last_kernel(parts_ref, out_ref, held_ref, sems):
+    copies = []
     for w in range(4):
         total = parts_ref[w, 0] + parts_ref[w, 1]
         for part in range(2):
             for g in range(4):
-                out_ref[w, part, g * 8 : (g + 1) * 8, :] = total[
+                held_ref[w, part, g * 8 : (g + 1) * 8, :] = total[
                     part * 8 : (part + 1) * 8, g * 32 : (g + 1) * 32
                 ]
+        copies.append(pltpu.make_async_copy(held_ref.at[w], out_ref.at[w], sems.at[w]))
+        copies[-1].start()
+    for copy in copies:
+        copy.wait()
 
 
 def vmem(n):
     return [pl.BlockSpec(memory_space=pltpu.VMEM)] * n
 
 
-def call(kernel, shape, dtype, in_specs, args, scratch=(), limit=16, flops=0, moved=0):
+def call(kernel, shape, dtype, in_specs, args, scratch=(), limit=16, flops=0, moved=0, out_space=pltpu.VMEM):
     return pl.pallas_call(
         kernel,
         out_shape=jax.ShapeDtypeStruct(shape, dtype),
         in_specs=in_specs,
-        out_specs=pl.BlockSpec(memory_space=pltpu.VMEM),
+        out_specs=pl.BlockSpec(memory_space=out_space),
         scratch_shapes=list(scratch),
         compiler_params=pltpu.CompilerParams(vmem_limit_bytes=limit << 20),
         cost_estimate=pl.CostEstimate(flops=flops, bytes_accessed=moved, transcendentals=0),
@@ -215,7 +220,15 @@
     parts = exchange(partial.reshape(16, 4, 2, 16, 128), ("x", "y"))
     summed = call(sum_kernel, (2, 4, 16, 128), F32, vmem(1), (parts,), moved=1 << 19)
     last = exchange(summed.reshape(8, 16, 128), ("zh", "za", "zb"))
-    return call(last_kernel, (4, 2, 32, 32), F32, vmem(1), (last.reshape(4, 2, 16, 128),))
+    return call(
+        last_kernel,
+        (4, 2, 32, 32),
+        F32,
+        vmem(1),
+        (last.reshape(4, 2, 16, 128),),
+        scratch=[pltpu.VMEM((4, 2, 32, 32), F32), pltpu.SemaphoreType.DMA((4,))],
+        out_space=pl.ANY,
+    )
 
 
 def solution(mesh):

time: 84.3 us -> 84.3 us (level)
  no operation moved by 1% of the time
where the time goes in v14:
time: 84.3 us; the launch traced here: 84 us
  blocking collectives  77.2 us (92%)
  Pallas kernels  3.09 us (4%)
  waiting for transfers between devices  2.66 us (3%)
  local copies, waits for them, and re-layouts  1.05 us (1%)
    all_to_all x4, blocking collectives, exchange(): return lax.all_to_all(x, axes, 0, 0, tiled=True)  77.2 us
    pallas_call x5, Pallas kernels, call(): pl.pallas_call(kernel, out_shape=jax.ShapeDtypeStruct(shape, dtype), in_s...  3.09 us
    ppermute x1, waiting for transfers between devices, shards(): other = lax.ppermute(mine, 'core', [(0, 1), (1, 0)])  2.66 us
  transfers between devices with their start and end apart: 1, of which 1 were waited for; matrix products, arithmetic and copies ran while one was open for 0% of the time, Pallas kernels for 0%

profile of v14, /device:TPU:8, one launch (start us, length us, event | category | flops | bytes accessed | tf_op | source)
XLA Modules:
  0.0 84.0 jit_solution(13447427663763233930)
XLA Ops:
  0.0 0.0 copy-start
  0.0 1.0 %copy-done = bf16[4,2,2,32,512]{4,3,2,1,0:T(8,128)(2,1)S(1)} copy-done((bf16[4,2,2,32,512]{4,3,2,1,0:T(8,128)(2,1)S(1)}, bf16[4,2,2,32,512]{4,3,2,1,0:T(8,128)(2,1)}, u32[]{:S(2)}) %copy-start) | copy-done | bytes 524312
  1.0 0.2 shard_map.28
  1.2 0.0 copy-start.1
  1.2 29.1 %all_to_all.20 = bf16[32,2,2,16,128]{4,3,2,1,0:T(8,128)(2,1)S(1)} all-to-all(bf16[32,2,2,16,128]{4,3,2,1,0:T(8,128)(2,1)S(1)} %bitcast.8), channel_id=1, replica_groups=mesh['x'=4,'za'=2,'zb'=2,'zh'=2,'y'=4,'core'=2] {'zb','zh','x','za'}, dimensions={0} | all-to-all | bytes 1048576 | tf_op jit(solution)/shard_map/all_to_all | solution.py:186
  30.3 0.0 copy-done.1
  30.3 0.5 shard_map.29
  30.8 20.1 %all_to_all.21 = bf16[32,2,2,2,16,128]{5,4,3,2,1,0:T(8,128)(2,1)S(1)} all-to-all(bf16[32,2,2,2,16,128]{5,4,3,2,1,0:T(8,128)(2,1)S(1)} %shard_map.29), channel_id=1, replica_groups=mesh['x'=4,'za'=2,'zb'=2,'zh'=2,'y'=4,'core'=2] {'y','zb','x'}, dimensions={0} | all-to-all | bytes 2097152 | tf_op jit(solution)/shard_map/all_to_all | solution.py:186
  50.9 0.0 collective-permute-start
  50.9 2.7 %collective-permute-done.other_ref = bf16[4,2,4,2,2,2,16,128]{7,6,5,4,3,2,1,0:T(8,128)(2,1)S(1)} collective-permute-done((bf16[4,2,4,2,2,2,16,128]{7,6,5,4,3,2,1,0:T(8,128)(2,1)S(1)}, bf16[4,2,4,2,2,2,16,128]{7,6,5,4,3,2,1,0:T(8,128)(2,1)S(1)}, u32[]{:S(2)}, u32[]{:S(2)}) %collective-permute-start) | collective-permute-done | bytes 1048608 | tf_op jit(solution)/shard_map/ppermute | solution.py:209
  53.6 1.6 %shard_map.30 = bf16[4,4,4,2,16,128]{5,4,3,2,1,0:T(8,128)(2,1)S(1)} custom-call(bf16[4,2,4,2,2,2,16,128]{7,6,5,4,3,2,1,0:T(8,128)(2,1)S(1)} %bitcast.10, bf16[4,2,4,2,2,2,16,128]{7,6,5,4,3,2,1,0:T(8,128)(2,1)S(1)} %collective-permute-done.other_ref), custom_call_target="tpu_custom_call" | custom-call | flops 1073741824 | bytes 2621440 | tf_op jit(solution)/shard_map/pallas_call | solution.py:174
  55.2 15.8 %all_to_all.22.parts_ref = bf16[16,4,2,16,128]{4,3,2,1,0:T(8,128)(2,1)S(1)} all-to-all(bf16[16,4,2,16,128]{4,3,2,1,0:T(8,128)(2,1)S(1)} %bitcast.12), channel_id=1, replica_groups=mesh['x'=4,'za'=2,'zb'=2,'zh'=2,'y'=4,'core'=2] {'x','y'}, dimensions={0} | all-to-all | bytes 1048576 | tf_op jit(solution)/shard_map/all_to_all | solution.py:186
  71.0 0.1 shard_map.31
  71.1 12.2 %all_to_all.23 = f32[8,16,128]{2,1,0:T(8,128)S(1)} all-to-all(f32[8,16,128]{2,1,0:T(8,128)S(1)} %bitcast.13), channel_id=1, replica_groups=mesh['x'=4,'za'=2,'zb'=2,'zh'=2,'y'=4,'core'=2] {'zh','za','zb'}, dimensions={0} | all-to-all | bytes 131072 | tf_op jit(solution)/shard_map/all_to_all | solution.py:186
  83.3 0.8 shard_map.32
Async XLA Ops:
  0.0 1.0 %copy-start = (bf16[4,2,2,32,512]{4,3,2,1,0:T(8,128)(2,1)S(1)}, bf16[4,2,2,32,512]{4,3,2,1,0:T(8,128)(2,1)}, u32[]{:S(2)}) copy-start(bf16[4,2,2,32,512]{4,3,2,1,0:T(8,128)(2,1)} %param.2) | copy-start | bytes 1572868
  1.2 29.1 %copy-start.1 = (f32[4,512]{1,0:T(4,128)S(1)}, f32[4,512]{1,0:T(4,128)}, u32[]{:S(2)}) copy-start(f32[4,512]{1,0:T(4,128)} %vert_ref.1) | copy-start | bytes 24580
  50.9 2.7 %collective-permute-start = (bf16[4,2,4,2,2,2,16,128]{7,6,5,4,3,2,1,0:T(8,128)(2,1)S(1)}, bf16[4,2,4,2,2,2,16,128]{7,6,5,4,3,2,1,0:T(8,128)(2,1)S(1)}, u32[]{:S(2)}, u32[]{:S(2)}) collective-permute-start(bf16[4,2,4,2,2,2,16,128]{7,6,5,4,3,2,1,0:T(8,128)(2,1)S(1)} %bitcast.9), channel_id=1, source_target_pairs={{0,1},{1,0},{2,3},{3,2},{4,5},{5,4},{6,7},{7,6},{8,9},{9,8},{10,11... | collective-permute-start | bytes 3145736 | tf_op jit(solution)/shard_map/ppermute | solution.py:209
